TPU v7x, 256 devices: a whole 4x4x8 slice. The times are simulated.
256 devices in a mesh: layer: 16 (over y_lo, z), latent: 16 (over y_hi, x, core).
Axes of the slice: x: 4, y: 4 (y_hi: 2, y_lo: 2; y = y_hi * 2 + y_lo), z: 8, core: 2. Of those that a mesh axis runs over, the one named last changes fastest.
Arguments:
- layer_inputs: bfloat16 [384, 16384], P('latent', 'layer'), may hold values from -6 to 6
- mlp_outputs: bfloat16 [384, 16384], P('latent', 'layer'), may hold values from -6 to 6
- enc_weight: bfloat16 [16384, 4096], P('layer', 'latent'), may hold values from -0.125 to 0.125
- enc_bias: float32 [8, 4096], P(None, 'latent'), may hold values from -1 to 0.5
- dec_weight: bfloat16 [8, 4096, 16384], P(None, 'latent', 'layer'), may hold values from -0.03125 to 0.03125
Outputs:
- enc_grad: float32 [16384, 4096], P('layer', 'latent')
- dec_grad: bfloat16 [8, 4096, 16384], P(None, 'latent', 'layer')
All inputs are finite; a program needn't handle non-finite values.
Results may differ from a plain program's by a relative error of at most 0.011.
Values may be sent and summed in bfloat16 or wider, within the bound.
No kernel may reach another device: no remote copies, remote signals or barrier semaphores. Data moves between devices by JAX's collectives and lax.ppermute only.
A program may use at most 64 MiB of HBM per device.

v0:
```python
import jax
import jax.numpy as jnp
from jax import lax
from jax.sharding import PartitionSpec as P


def copy_for_each(x, axis):
    copies = jnp.broadcast_to(x, (lax.axis_size(axis), *x.shape))
    return lax.all_to_all(copies, axis, split_axis=0, concat_axis=0, tiled=True)


def joined_along(parts, dim):
    parts = jnp.moveaxis(parts, 0, dim)
    dims = parts.shape
    return parts.reshape(*dims[:dim], dims[dim] * dims[dim + 1], *dims[dim + 2 :])


def gathered_copies(x, axis, dim):
    parts = copy_for_each(x, axis)
    return joined_along(parts, dim)


def from_partner(x, axis, distance):
    return lax.ppermute(x, axis, [(i, i ^ 1 << distance) for i in range(lax.axis_size(axis))])


def in_blocks(x, dim, devices):
    dims = x.shape
    parts = x.reshape(*dims[:dim], devices, dims[dim] // devices, *dims[dim + 1 :])
    return jnp.moveaxis(parts, dim, 0)


def sent_and_summed(x, axis, dim):
    parts = in_blocks(x, dim, lax.axis_size(axis))
    arrived = lax.all_to_all(parts, axis, split_axis=0, concat_axis=0, tiled=True)
    return arrived.sum(axis=0)


def take_layer(stack, index):
    return lax.dynamic_index_in_dim(stack, index, 0, keepdims=False)


def local(layer_inputs, mlp_outputs, enc_weight, enc_bias, dec_weight):
    position = lax.axis_index("layer")
    layer_now = position // 2
    which_half = position % 2
    inputs_half = gathered_copies(layer_inputs, "latent", 0)
    total_rows = inputs_half.shape[0]
    half_rows = total_rows // 2
    width_half = dec_weight.shape[2]
    latent_cols = enc_weight.shape[1]
    own_part = jnp.dot(inputs_half, enc_weight, preferred_element_type=jnp.float32)
    partner = from_partner(own_part, "layer", 0)
    pre_acts = own_part + partner + take_layer(enc_bias, layer_now)[None, :]
    latents = jnp.maximum(pre_acts, 0.0).astype(jnp.bfloat16)
    own_rows = lax.dynamic_slice_in_dim(latents, which_half * half_rows, half_rows, 0)
    gathered = gathered_copies(own_rows[None], "layer", 0)
    layer_count = gathered.shape[0] // 2
    gathered = gathered.reshape(layer_count, total_rows, latent_cols)
    upper = layer_now + 1
    rscale = total_rows ** (-0.5)
    local_rows = mlp_outputs.shape[0]

    def add_source(source, total):
        block = take_layer(gathered, source)
        return total + jnp.dot(
            block, take_layer(dec_weight, source), preferred_element_type=jnp.float32
        )

    recon_own = sent_and_summed(
        lax.fori_loop(
            0,
            upper,
            add_source,
            jnp.zeros((local_rows * lax.axis_size("latent"), width_half), jnp.float32),
        ),
        "latent",
        0,
    )
    grad_own = ((recon_own - mlp_outputs.astype(jnp.float32)) * rscale).astype(jnp.bfloat16)
    out_grad = gathered_copies(grad_own, "latent", 0)

    def back_source(source, carry):
        grads, lat_terms = carry
        block = take_layer(gathered, source)
        weight = take_layer(dec_weight, source)
        dec_piece = lax.dot_general(
            block, out_grad, (((0,), (0,)), ((), ())), preferred_element_type=jnp.float32
        ).astype(jnp.bfloat16)
        lat_piece = lax.dot_general(
            out_grad, weight, (((1,), (1,)), ((), ())), preferred_element_type=jnp.float32
        )
        grads = lax.dynamic_update_index_in_dim(grads, dec_piece, source, 0)
        lat_terms = lax.dynamic_update_index_in_dim(lat_terms, lat_piece, source, 0)
        return (grads, lat_terms)

    start_carry = (
        jnp.zeros(dec_weight.shape, jnp.bfloat16),
        jnp.zeros((layer_count, total_rows, latent_cols), jnp.float32),
    )
    dec_grad, lat_terms = lax.fori_loop(0, upper, back_source, start_carry)
    lat_all = lax.psum(lat_terms, "layer")
    lat_grad = take_layer(lat_all, layer_now)
    pre_grad = jnp.where(pre_acts > 0.0, lat_grad, 0.0).astype(jnp.bfloat16)
    enc_grad = lax.dot_general(
        inputs_half, pre_grad, (((0,), (0,)), ((), ())), preferred_element_type=jnp.float32
    )
    return (enc_grad, dec_grad)


def solution(mesh):
    in_specs = (
        P("latent", "layer"),
        P("latent", "layer"),
        P("layer", "latent"),
        P(None, "latent"),
        P(None, "latent", "layer"),
    )
    out_specs = (P("layer", "latent"), P(None, "latent", "layer"))
    return jax.shard_map(local, mesh=mesh, in_specs=in_specs, out_specs=out_specs, check_vma=False)
```

profile of v0, /device:TPU:2, one launch (start us, length us, event | category | flops | bytes accessed | tf_op | source)
XLA Modules:
  0.0 269.0 jit_solution(17720900140261801250)
XLA Ops:
  0.6 0.0 copy-start
  0.6 0.9 broadcast_in_dim.30
  1.6 19.8 %all_to_all.20 = bf16[16,24,1024]{2,1,0:T(8,128)(2,1)S(1)} all-to-all(bf16[16,24,1024]{2,1,0:T(8,128)(2,1)S(1)} %broadcast_in_dim.30), channel_id=1, replica_groups=mesh['layer'=16,'latent'=16] {'latent'}, dimensions={0} | all-to-all | bytes 1572864 | tf_op jit(solution)/shard_map/all_to_all | solution.py:9
  21.4 0.0 copy-done
  21.4 0.4 fusion.19
  21.8 2.0 collective-permute-start
  23.8 0.7 constant_dynamic-slice_fusion.1
  24.5 9.3 %collective-permute-done = f32[384,256]{1,0:T(8,128)S(1)} collective-permute-done((f32[384,256]{1,0:T(8,128)S(1)}, f32[384,256]{1,0:T(8,128)S(1)}, u32[]{:S(2)}, u32[]{:S(2)}) %collective-permute-start) | collective-permute-done | bytes 393248 | tf_op jit(solution)/shard_map/ppermute | solution.py:24
  33.9 0.1 add_add_fusion
  34.0 1.3 broadcast_in_dim.33
  35.2 8.5 %all-to-all-start.1 = ((bf16[16,1,192,256]{3,2,1,0:T(8,128)(2,1)}), bf16[16,1,192,256]{3,2,1,0:T(8,128)(2,1)S(1)}, u32[]{:S(2)}, u32[]{:S(2)}) async-start(bf16[16,1,192,256]{3,2,1,0:T(8,128)(2,1)} %broadcast_in_dim.33), calls=%async_computation.1 | async-start | bytes 3145728 | tf_op jit(solution)/shard_map/all_to_all | solution.py:9
  43.8 38.1 %all-to-all-done.1 = bf16[16,1,192,256]{3,2,1,0:T(8,128)(2,1)S(1)} async-done(((bf16[16,1,192,256]{3,2,1,0:T(8,128)(2,1)}), bf16[16,1,192,256]{3,2,1,0:T(8,128)(2,1)S(1)}, u32[]{:S(2)}, u32[]{:S(2)}) %all-to-all-start.1) | async-done | bytes 1572896 | tf_op jit(solution)/shard_map/all_to_all | solution.py:9
  81.9 1.1 copy-done.1
  83.0 0.2 broadcast_in_dim.34
  83.2 1.6 while.22
  83.2 1.6 convolution_add_fusion.2
  84.8 0.0 copy-start.2
  84.8 24.4 %all_to_all.21 = f32[16,24,1024]{2,1,0:T(8,128)} all-to-all(f32[16,24,1024]{2,1,0:T(8,128)S(1)} %bitcast.56), channel_id=1, replica_groups=mesh['layer'=16,'latent'=16] {'latent'}, dimensions={0} | all-to-all | bytes 3145728 | tf_op jit(solution)/shard_map/all_to_all | solution.py:35
  109.3 1.5 reduce_sum.9
  110.8 0.0 copy-done.2
  110.8 1.0 broadcast_in_dim.35
  111.8 7.1 %all-to-all-start.3 = ((bf16[16,24,1024]{2,1,0:T(8,128)(2,1)}), bf16[16,24,1024]{2,1,0:T(8,128)(2,1)S(1)}, u32[]{:S(2)}, u32[]{:S(2)}) async-start(bf16[16,24,1024]{2,1,0:T(8,128)(2,1)} %broadcast_in_dim.35), calls=%async_computation.3 | async-start | bytes 1572864 | tf_op jit(solution)/shard_map/all_to_all | solution.py:9
  118.9 12.2 %all-to-all-done.3 = bf16[16,24,1024]{2,1,0:T(8,128)(2,1)S(1)} async-done(((bf16[16,24,1024]{2,1,0:T(8,128)(2,1)}), bf16[16,24,1024]{2,1,0:T(8,128)(2,1)S(1)}, u32[]{:S(2)}, u32[]{:S(2)}) %all-to-all-start.3) | async-done | bytes 786464 | tf_op jit(solution)/shard_map/all_to_all | solution.py:9
  131.1 1.9 broadcast_in_dim.32
  133.0 2.5 broadcast_in_dim.31
  135.5 4.4 %while.23 = (s32[]{:T(128)}, bf16[8,256,1024]{2,1,0:T(8,128)(2,1)}, f32[8,384,256]{1,2,0:T(8,128)}, s32[]{:T(128)}, bf16[8,384,256]{2,1,0:T(8,128)(2,1)}, /*inde...) while((s32[]{:T(128)}, bf16[8,256,1024]{2,1,0:T(8,128)(2,1)}, ...), condition=%wide.region_4.5_spmd, body=%wide.region_3.4_spmd.sunk | while | flops 402915328 | bytes 3213455 | solution.py:101
  135.5 2.2 fusion.40
  137.8 2.2 fusion.39
  140.0 127.0 %all-reduce.1 = bf16[8,384,256]{1,2,0:T(8,128)(2,1)S(1)} all-reduce(f32[8,384,256]{1,2,0:T(8,128)} %get-tuple-element.70), channel_id=1, replica_groups=mesh['layer'=16,'latent'=16] {'layer'}, use_global_device_ids=true, to_apply=%region_5.6 | all-reduce | flops 786432 | bytes 4718592 | tf_op jit(solution)/shard_map/psum | solution.py:102
  267.0 0.1 copy.9
  267.2 0.5 convolution_bitcast_fusion.1
  267.6 1.3 copy.10
  (4 shorter events, 0.1 us)
Async XLA Ops:
  0.6 20.8 %copy-start = (bf16[1024,256]{1,0:T(8,128)(2,1)S(1)}, bf16[1024,256]{1,0:T(8,128)(2,1)}, u32[]{:S(2)}) copy-start(bf16[1024,256]{1,0:T(8,128)(2,1)} %param.11) | copy-start | bytes 1572868
  21.8 12.1 %collective-permute-start = (f32[384,256]{1,0:T(8,128)S(1)}, f32[384,256]{1,0:T(8,128)S(1)}, u32[]{:S(2)}, u32[]{:S(2)}) collective-permute-start(f32[384,256]{1,0:T(8,128)S(1)} %fusion.19), channel_id=1, source_target_pairs={{0,16},{16,0},{32,48},{48,32},{64,80},{80,64},{96,112},{112,96},{1... | collective-permute-start | bytes 1179656 | tf_op jit(solution)/shard_map/ppermute | solution.py:24
  35.2 46.6 %all-to-all-start.1 = ((bf16[16,1,192,256]{3,2,1,0:T(8,128)(2,1)}), bf16[16,1,192,256]{3,2,1,0:T(8,128)(2,1)S(1)}, u32[]{:S(2)}, u32[]{:S(2)}) async-start(bf16[16,1,192,256]{3,2,1,0:T(8,128)(2,1)} %broadcast_in_dim.33), calls=%async_computation.1 | async-start | bytes 3145728 | tf_op jit(solution)/shard_map/all_to_all | solution.py:9
  81.9 1.1 copy-start.1
  84.8 26.0 %copy-start.2 = (bf16[24,1024]{1,0:T(8,128)(2,1)S(1)}, bf16[24,1024]{1,0:T(8,128)(2,1)}, u32[]{:S(2)}) copy-start(bf16[24,1024]{1,0:T(8,128)(2,1)} %param.10) | copy-start | bytes 147460
  111.8 19.3 %all-to-all-start.3 = ((bf16[16,24,1024]{2,1,0:T(8,128)(2,1)}), bf16[16,24,1024]{2,1,0:T(8,128)(2,1)S(1)}, u32[]{:S(2)}, u32[]{:S(2)}) async-start(bf16[16,24,1024]{2,1,0:T(8,128)(2,1)} %broadcast_in_dim.35), calls=%async_computation.3 | async-start | bytes 1572864 | tf_op jit(solution)/shard_map/all_to_all | solution.py:9
where the time goes:
time: 271 us; the launch traced here: 269 us
  blocking collectives  171 us (63%)
  waiting for transfers between devices  59.6 us (22%)
  starting transfers between devices  17.6 us (6%)
  local copies, waits for them, and re-layouts  11.2 us (4%)
  matrix products  6.85 us (3%)
    psum x1, blocking collectives, local(): lat_all = lax.psum(lat_terms, 'layer')  127 us
    all_to_all x2, waiting for transfers between devices, copy_for_each(): return lax.all_to_all(copies, axis, split_axis=0, concat_axis=0, tiled=True)  50.3 us
    all_to_all x1, blocking collectives, sent_and_summed(): lax.all_to_all(parts, axis, split_axis=0, concat_axis=0, tiled=True)  24.4 us
    all_to_all x1, blocking collectives, copy_for_each(): return lax.all_to_all(copies, axis, split_axis=0, concat_axis=0, tiled=True)  19.8 us
    all_to_all x2, starting transfers between devices, copy_for_each(): return lax.all_to_all(copies, axis, split_axis=0, concat_axis=0, tiled=True)  15.6 us
    ppermute x1, waiting for transfers between devices, from_partner(): lax.ppermute(x, axis, [(i, i ^ 1 << distance) for i in range(lax.axis_siz...  9.34 us
  transfers between devices with their start and end apart: 3, of which 3 were waited for; matrix products, arithmetic and copies ran while one was open for 0% of the time, Pallas kernels for 0%

commit v1 on v0

v1 whole, which is shorter than its diff:
```python
import jax
import jax.numpy as jnp
from jax import lax
from jax.sharding import PartitionSpec as P


def from_partner(x, axis, bit):
    return lax.ppermute(x, axis, [(i, i ^ bit) for i in range(lax.axis_size(axis))])


def same_core_groups(size):
    return [[2 * k + core for k in range(size // 2)] for core in range(2)]


def exchanged(parts, axis, groups=None):
    return lax.all_to_all(
        parts, axis, split_axis=0, concat_axis=0, tiled=True, axis_index_groups=groups
    )


def rows_of_all(x):
    size = lax.axis_size("latent")
    chips = size // 2
    rows, width = x.shape
    copies = jnp.broadcast_to(x[None], (chips, rows, width))
    own = exchanged(copies, "latent", same_core_groups(size)).reshape(chips * rows, width)
    other = from_partner(own, "latent", 1)
    return jnp.concatenate([own, other], 0)


def rows_summed(x):
    size = lax.axis_size("latent")
    chips = size // 2
    half = x.shape[0] // 2
    theirs = from_partner(x[half:].astype(jnp.bfloat16), "latent", 1)
    both = (x[:half] + theirs.astype(jnp.float32)).astype(jnp.bfloat16)
    parts = both.reshape(chips, half // chips, x.shape[1])
    arrived = exchanged(parts, "latent", same_core_groups(size))
    return arrived.astype(jnp.float32).sum(axis=0)


def local(layer_inputs, mlp_outputs, enc_weight, enc_bias, dec_weight):
    position = lax.axis_index("layer")
    places = lax.axis_size("layer")
    layer_now = position // 2
    which_half = position % 2
    layer_count = places // 2
    latent_cols = enc_weight.shape[1]

    inputs_half = rows_of_all(layer_inputs)
    total_rows = inputs_half.shape[0]
    half_rows = total_rows // 2
    own_part = jnp.dot(inputs_half, enc_weight, preferred_element_type=jnp.float32)
    kept = lax.dynamic_slice_in_dim(own_part, which_half * half_rows, half_rows, 0)
    given = lax.dynamic_slice_in_dim(own_part, (1 - which_half) * half_rows, half_rows, 0)
    bias = lax.dynamic_slice_in_dim(enc_bias, layer_now, 1, 0)
    pre_half = kept + from_partner(given, "layer", 1) + bias
    latents_half = jnp.maximum(pre_half, 0.0).astype(jnp.bfloat16)

    copies = jnp.broadcast_to(latents_half[None], (places, half_rows, latent_cols))
    gathered = exchanged(copies, "layer").reshape(layer_count, total_rows, latent_cols)
    used = lax.broadcasted_iota(jnp.int32, (layer_count, 1, 1), 0) <= layer_now
    latents = jnp.where(used, gathered, jnp.zeros_like(gathered))

    recon = lax.dot_general(
        latents, dec_weight, (((0, 2), (0, 1)), ((), ())), preferred_element_type=jnp.float32
    )
    recon_own = rows_summed(recon)
    rscale = total_rows ** (-0.5)
    grad_own = ((recon_own - mlp_outputs.astype(jnp.float32)) * rscale).astype(jnp.bfloat16)
    out_grad = rows_of_all(grad_own)

    lat_terms = lax.dot_general(
        dec_weight, out_grad, (((2,), (1,)), ((), ())), preferred_element_type=jnp.float32
    )
    lat_terms = jnp.swapaxes(lat_terms, 1, 2).astype(jnp.bfloat16)
    dec_grad = lax.dot_general(
        latents, out_grad, (((1,), (0,)), ((), ())), preferred_element_type=jnp.float32
    ).astype(jnp.bfloat16)
    arrived = exchanged(lat_terms.reshape(places, half_rows, latent_cols), "layer")
    later = lax.broadcasted_iota(jnp.int32, (places, 1, 1), 0) // 2 >= layer_now
    lat_grad = jnp.where(later, arrived, jnp.zeros_like(arrived)).astype(jnp.float32).sum(axis=0)
    pre_grad = jnp.where(latents_half > 0, lat_grad, 0.0).astype(jnp.bfloat16)
    pre_other = from_partner(pre_grad, "layer", 1)
    first = which_half == 0
    pre_all = jnp.concatenate(
        [jnp.where(first, pre_grad, pre_other), jnp.where(first, pre_other, pre_grad)], 0
    )
    enc_grad = lax.dot_general(
        inputs_half, pre_all, (((0,), (0,)), ((), ())), preferred_element_type=jnp.float32
    )
    return (enc_grad, dec_grad)


def solution(mesh):
    in_specs = (
        P("latent", "layer"),
        P("latent", "layer"),
        P("layer", "latent"),
        P(None, "latent"),
        P(None, "latent", "layer"),
    )
    out_specs = (P("layer", "latent"), P(None, "latent", "layer"))
    return jax.shard_map(local, mesh=mesh, in_specs=in_specs, out_specs=out_specs, check_vma=False)
```

time: 271 us -> 163 us (0.60)
  blocking collectives: 171 us -> 42.5 us
  waiting for transfers between devices: 59.6 us -> 85.2 us
  local copies, waits for them, and re-layouts: 11.2 us -> 3.02 us
  matrix products: 6.85 us -> 13.8 us
    psum x1 -> x0, blocking collectives: 127 us -> none  [local(): lat_all = lax.psum(lat_terms, 'layer')]
    all_to_all x2, waiting for transfers between devices: 50.3 us -> 75.5 us  [exchanged(): lax.all_to_all(parts, axis, split_axis=0, concat_axis=0, tiled=True, axis...]
    dot_general x4, matrix products: 6.48 us -> 13.4 us  [the longest x1 4.59 us: local(): lax.dot_general(latents, dec_weight, (((0, 2), (0, 1)), ((), ())), prefer...]
    broadcast_in_dim x6 -> x3, local copies, waits for them, and re-layouts: 7.82 us -> 2.22 us  [the longest x1 1.3 us: local(): jnp.broadcast_to(latents_half[None], (places, half_rows, latent_cols))]
    all_to_all x2 -> x3, blocking collectives: 44.3 us -> 42.5 us  [exchanged(): lax.all_to_all(parts, axis, split_axis=0, concat_axis=0, tiled=True, axis...]
    ppermute x1 -> x5, waiting for transfers between devices: 9.34 us -> 9.65 us  [from_partner(): lax.ppermute(x, axis, [(i, i ^ bit) for i in range(lax.axis_size(axis))])]
  transfers between devices with their start and end apart: 3 -> 7, of which waited for: 3 -> 6; matrix products, arithmetic and copies ran while one was open for 0% -> 3% of each run, Pallas kernels for 0% -> 0%
where the time goes in v1:
time: 163 us
  waiting for transfers between devices  85.2 us (52%)
  blocking collectives  42.5 us (26%)
  starting transfers between devices  16.8 us (10%)
  matrix products  13.8 us (8%)
  local copies, waits for them, and re-layouts  3.02 us (2%)
    all_to_all x2, waiting for transfers between devices, exchanged(): lax.all_to_all(parts, axis, split_axis=0, concat_axis=0, tiled=True, axis...  75.5 us
    all_to_all x3, blocking collectives, exchanged(): lax.all_to_all(parts, axis, split_axis=0, concat_axis=0, tiled=True, axis...  42.5 us
    all_to_all x2, starting transfers between devices, exchanged(): lax.all_to_all(parts, axis, split_axis=0, concat_axis=0, tiled=True, axis...  13 us
    ppermute x5, waiting for transfers between devices, from_partner(): lax.ppermute(x, axis, [(i, i ^ bit) for i in range(lax.axis_size(axis))])  9.65 us
    dot_general x1, matrix products, local(): lax.dot_general(latents, dec_weight, (((0, 2), (0, 1)), ((), ())), prefer...  4.59 us
    dot_general x1, matrix products, local(): lax.dot_general(latents, out_grad, (((1,), (0,)), ((), ())), preferred_el...  4.39 us
    ppermute x5, starting transfers between devices, from_partner(): lax.ppermute(x, axis, [(i, i ^ bit) for i in range(lax.axis_size(axis))])  3.73 us
  transfers between devices with their start and end apart: 7, of which 6 were waited for; matrix products, arithmetic and copies ran while one was open for 3% of the time, Pallas kernels for 0%

profile of v1, /device:TPU:2, one launch (start us, length us, event | category | flops | bytes accessed | tf_op | source)
XLA Modules:
  0.0 162.9 jit_solution(12008189444375098934)
XLA Ops:
  0.6 0.0 copy-start
  0.6 0.9 broadcast_in_dim.42
  1.5 16.3 %all_to_all.25 = bf16[8,24,1024]{2,1,0:T(8,128)(2,1)S(1)} all-to-all(bf16[8,24,1024]{2,1,0:T(8,128)(2,1)S(1)} %broadcast_in_dim.42), channel_id=1, replica_groups={{0,2,4,6,8,10,12,14},{1,3,5,7,9,11,13,15},{16,18,20,22,24,26,28,30},{17..., dimensions={0} | all-to-all | bytes 786432 | tf_op jit(solution)/shard_map/all_to_all | solution.py:16
  17.8 0.0 collective-permute-start
  17.8 1.7 %collective-permute-done = bf16[192,1024]{1,0:T(8,128)(2,1)S(1)} collective-permute-done((bf16[192,1024]{1,0:T(8,128)(2,1)S(1)}, bf16[192,1024]{1,0:T(8,128)(2,1)S(1)}, u32[]{:S(2)}, u32[]{:S(2)}) %collective-permute-start) | collective-permute-done | bytes 393248 | tf_op jit(solution)/shard_map/ppermute | solution.py:8
  19.5 0.0 copy-done
  19.5 0.4 fusion.2
  20.0 2.0 %collective-permute-start.1 = (f32[192,256]{1,0:T(8,128)S(1)}, f32[192,256]{1,0:T(8,128)S(1)}, u32[]{:S(2)}, u32[]{:S(2)}) collective-permute-start(f32[192,256]{1,0:T(8,128)S(1)} %constant_dynamic-slice_fusion.1), channel_id=1, source_target_pairs={{0,16},{16,0},{32,48},{48,32},{64,80},{80,64},{96,112},{112,96},{1... | collective-permute-start | bytes 589832 | tf_op jit(solution)/shard_map/ppermute | solution.py:8
  22.0 0.7 constant_dynamic-slice_fusion
  22.7 4.5 %collective-permute-done.1 = f32[192,256]{1,0:T(8,128)S(1)} collective-permute-done((f32[192,256]{1,0:T(8,128)S(1)}, f32[192,256]{1,0:T(8,128)S(1)}, u32[]{:S(2)}, u32[]{:S(2)}) %collective-permute-start.1) | collective-permute-done | bytes 196640 | tf_op jit(solution)/shard_map/ppermute | solution.py:8
  27.2 1.3 broadcast_in_dim.45
  28.5 8.5 %all-to-all-start.1 = ((bf16[16,192,256]{2,1,0:T(8,128)(2,1)}), bf16[16,192,256]{2,1,0:T(8,128)(2,1)S(1)}, u32[]{:S(2)}, u32[]{:S(2)}) async-start(bf16[16,192,256]{2,1,0:T(8,128)(2,1)} %broadcast_in_dim.45), calls=%async_computation.1 | async-start | bytes 3145728 | tf_op jit(solution)/shard_map/all_to_all | solution.py:16
  37.0 37.2 %all-to-all-done.1 = bf16[16,192,256]{2,1,0:T(8,128)(2,1)S(1)} async-done(((bf16[16,192,256]{2,1,0:T(8,128)(2,1)}), bf16[16,192,256]{2,1,0:T(8,128)(2,1)S(1)}, u32[]{:S(2)}, u32[]{:S(2)}) %all-to-all-start.1) | async-done | bytes 1572896 | tf_op jit(solution)/shard_map/all_to_all | solution.py:16
  74.3 0.2 bitcast_select_fusion
  74.4 4.6 %convolution_bitcast_fusion = f32[384,1024]{1,0:T(8,128)S(1)} fusion(bf16[8,384,256]{2,1,0:T(8,128)(2,1)S(1)} %bitcast_select_fusion, bf16[8,256,1024]{2,1,0:T(8,128)(2,1)} %param.9), kind=kOutput, calls=%fused_computation.4 | convolution fusion | flops 1610612736 | bytes 7340032 | tf_op jit(solution)/shard_map/dot_general | solution.py:65
  79.1 0.0 copy-start.3
  79.1 0.1 collective-permute-start.2
  79.2 1.7 %collective-permute-done.2 = bf16[192,1024]{1,0:T(8,128)(2,1)S(1)} collective-permute-done((bf16[192,1024]{1,0:T(8,128)(2,1)S(1)}, bf16[192,1024]{1,0:T(8,128)(2,1)S(1)}, u32[]{:S(2)}, u32[]{:S(2)}) %collective-permute-start.2) | collective-permute-done | bytes 393248 | tf_op jit(solution)/shard_map/ppermute | solution.py:8
  80.9 0.1 fusion
  81.0 13.9 %all_to_all.26 = bf16[8,24,1024]{2,1,0:T(8,128)(2,1)S(1)} all-to-all(bf16[8,24,1024]{2,1,0:T(8,128)(2,1)S(1)} %bitcast.23), channel_id=1, replica_groups={{0,2,4,6,8,10,12,14},{1,3,5,7,9,11,13,15},{16,18,20,22,24,26,28,30},{17..., dimensions={0} | all-to-all | bytes 786432 | tf_op jit(solution)/shard_map/all_to_all | solution.py:16
  94.9 0.1 convert_reduce_fusion.1
  95.1 12.4 %all_to_all.27 = bf16[8,24,1024]{2,1,0:T(8,128)(2,1)S(1)} all-to-all(bf16[8,24,1024]{2,1,0:T(8,128)(2,1)S(1)} %broadcast_in_dim.47), channel_id=1, replica_groups={{0,2,4,6,8,10,12,14},{1,3,5,7,9,11,13,15},{16,18,20,22,24,26,28,30},{17..., dimensions={0} | all-to-all | bytes 786432 | tf_op jit(solution)/shard_map/all_to_all | solution.py:16
  107.4 0.0 collective-permute-start.3
  107.4 1.7 %collective-permute-done.3 = bf16[192,1024]{1,0:T(8,128)(2,1)S(1)} collective-permute-done((bf16[192,1024]{1,0:T(8,128)(2,1)S(1)}, bf16[192,1024]{1,0:T(8,128)(2,1)S(1)}, u32[]{:S(2)}, u32[]{:S(2)}) %collective-permute-start.3) | collective-permute-done | bytes 393248 | tf_op jit(solution)/shard_map/ppermute | solution.py:8
  109.1 3.0 %convolution_convert_fusion.1 = bf16[384,8,256]{2,0,1:T(8,128)(2,1)} fusion(bf16[8,256,1024]{2,1,0:T(8,128)(2,1)S(1)} %copy-done.4, bf16[192,1024]{1,0:T(8,128)(2,1)S(1)} %collective-permute-done.3, bf16[192,1024]{1,0:T(8,128)(2,1)S(1)} %bitcast.28), kind=kOutput, calls=%fused_computation.2 | convolution fusion | flops 1612972032 | bytes 6553600 | tf_op jit(solution)/shard_map/dot_general | solution.py:73
  112.1 4.5 %all-to-all-start.4 = ((bf16[16,192,256]{2,1,0:T(8,128)(2,1)}), bf16[16,192,256]{2,1,0:T(8,128)(2,1)S(1)}, u32[]{:S(2)}, u32[]{:S(2)}) async-start(bf16[16,192,256]{2,1,0:T(8,128)(2,1)} %bitcast.22), calls=%async_computation.4 | async-start | bytes 3145728 | tf_op jit(solution)/shard_map/all_to_all | solution.py:16
  116.7 38.3 %all-to-all-done.4 = bf16[16,192,256]{2,1,0:T(8,128)(2,1)S(1)} async-done(((bf16[16,192,256]{2,1,0:T(8,128)(2,1)}), bf16[16,192,256]{2,1,0:T(8,128)(2,1)S(1)}, u32[]{:S(2)}, u32[]{:S(2)}) %all-to-all-start.4) | async-done | bytes 1572896 | tf_op jit(solution)/shard_map/all_to_all | solution.py:16
  155.0 0.4 convert_reduce_fusion
  155.4 1.6 %collective-permute-start.4 = (bf16[192,256]{1,0:T(8,128)(2,1)S(1)}, bf16[192,256]{1,0:T(8,128)(2,1)S(1)}, u32[]{:S(2)}, u32[]{:S(2)}) collective-permute-start(bf16[192,256]{1,0:T(8,128)(2,1)S(1)} %select_convert_fusion), channel_id=1, source_target_pairs={{0,16},{16,0},{32,48},{48,32},{64,80},{80,64},{96,112},{112,96},{1... | collective-permute-start | bytes 294920 | tf_op jit(solution)/shard_map/ppermute | solution.py:8
  157.0 4.4 %convolution_convert_fusion = bf16[8,256,1024]{2,1,0:T(8,128)(2,1)} fusion(bf16[8,384,256]{2,1,0:T(8,128)(2,1)S(1)} %copy-done.2, bf16[192,1024]{1,0:T(8,128)(2,1)S(1)} %copy-done.6, bf16[192,1024]{1,0:T(8,128)(2,1)S(1)} %bitcast.29), kind=kOutput, calls=%fused_computation.1 | convolution fusion | flops 1614282752 | bytes 6553600 | tf_op jit(solution)/shard_map/dot_general | solution.py:77
  161.4 0.0 collective-permute-done.4
  161.4 1.5 fusion.1
  (20 shorter events, 0.2 us)
Async XLA Ops:
  0.6 18.9 %copy-start = (bf16[1024,256]{1,0:T(8,128)(2,1)S(1)}, bf16[1024,256]{1,0:T(8,128)(2,1)}, u32[]{:S(2)}) copy-start(bf16[1024,256]{1,0:T(8,128)(2,1)} %param.7) | copy-start | bytes 1572868
  17.8 1.7 %collective-permute-start = (bf16[192,1024]{1,0:T(8,128)(2,1)S(1)}, bf16[192,1024]{1,0:T(8,128)(2,1)S(1)}, u32[]{:S(2)}, u32[]{:S(2)}) collective-permute-start(bf16[192,1024]{1,0:T(8,128)(2,1)S(1)} %bitcast.24), channel_id=1, source_target_pairs={{0,1},{1,0},{2,3},{3,2},{4,5},{5,4},{6,7},{7,6},{8,9},{9,8},{10,11... | collective-permute-start | bytes 1179656 | tf_op jit(solution)/shard_map/ppermute | solution.py:8
  20.0 7.2 %collective-permute-start.1 = (f32[192,256]{1,0:T(8,128)S(1)}, f32[192,256]{1,0:T(8,128)S(1)}, u32[]{:S(2)}, u32[]{:S(2)}) collective-permute-start(f32[192,256]{1,0:T(8,128)S(1)} %constant_dynamic-slice_fusion.1), channel_id=1, source_target_pairs={{0,16},{16,0},{32,48},{48,32},{64,80},{80,64},{96,112},{112,96},{1... | collective-permute-start | bytes 589832 | tf_op jit(solution)/shard_map/ppermute | solution.py:8
  28.5 45.8 %all-to-all-start.1 = ((bf16[16,192,256]{2,1,0:T(8,128)(2,1)}), bf16[16,192,256]{2,1,0:T(8,128)(2,1)S(1)}, u32[]{:S(2)}, u32[]{:S(2)}) async-start(bf16[16,192,256]{2,1,0:T(8,128)(2,1)} %broadcast_in_dim.45), calls=%async_computation.1 | async-start | bytes 3145728 | tf_op jit(solution)/shard_map/all_to_all | solution.py:16
  74.4 4.6 %copy-start.1 = (bf16[8,384,256]{2,1,0:T(8,128)(2,1)}, bf16[8,384,256]{2,1,0:T(8,128)(2,1)S(1)}, u32[]{:S(2)}) copy-start(bf16[8,384,256]{2,1,0:T(8,128)(2,1)S(1)} %bitcast_select_fusion) | copy-start | bytes 4718596
  79.1 15.9 %copy-start.3 = (bf16[24,1024]{1,0:T(8,128)(2,1)S(1)}, bf16[24,1024]{1,0:T(8,128)(2,1)}, u32[]{:S(2)}) copy-start(bf16[24,1024]{1,0:T(8,128)(2,1)} %param.6) | copy-start | bytes 147460
  79.1 1.8 %collective-permute-start.2 = (bf16[192,1024]{1,0:T(8,128)(2,1)S(1)}, bf16[192,1024]{1,0:T(8,128)(2,1)S(1)}, u32[]{:S(2)}, u32[]{:S(2)}) collective-permute-start(bf16[192,1024]{1,0:T(8,128)(2,1)S(1)} %slice.15), channel_id=1, source_target_pairs={{0,1},{1,0},{2,3},{3,2},{4,5},{5,4},{6,7},{7,6},{8,9},{9,8},{10,11... | collective-permute-start | bytes 1179656 | tf_op jit(solution)/shard_map/ppermute | solution.py:8
  80.9 28.2 %copy-start.4 = (bf16[8,256,1024]{2,1,0:T(8,128)(2,1)S(1)}, bf16[8,256,1024]{2,1,0:T(8,128)(2,1)}, u32[]{:S(2)}) copy-start(bf16[8,256,1024]{2,1,0:T(8,128)(2,1)} %param.9) | copy-start | bytes 12582916
  107.4 1.7 %collective-permute-start.3 = (bf16[192,1024]{1,0:T(8,128)(2,1)S(1)}, bf16[192,1024]{1,0:T(8,128)(2,1)S(1)}, u32[]{:S(2)}, u32[]{:S(2)}) collective-permute-start(bf16[192,1024]{1,0:T(8,128)(2,1)S(1)} %bitcast.27), channel_id=1, source_target_pairs={{0,1},{1,0},{2,3},{3,2},{4,5},{5,4},{6,7},{7,6},{8,9},{9,8},{10,11... | collective-permute-start | bytes 1179656 | tf_op jit(solution)/shard_map/ppermute | solution.py:8
  109.1 3.0 %copy-start.5 = (bf16[192,1024]{1,0:T(8,128)(2,1)}, bf16[192,1024]{1,0:T(8,128)(2,1)S(1)}, u32[]{:S(2)}) copy-start(bf16[192,1024]{1,0:T(8,128)(2,1)S(1)} %collective-permute-done.3) | copy-start | bytes 1179652
  112.1 42.8 %all-to-all-start.4 = ((bf16[16,192,256]{2,1,0:T(8,128)(2,1)}), bf16[16,192,256]{2,1,0:T(8,128)(2,1)S(1)}, u32[]{:S(2)}, u32[]{:S(2)}) async-start(bf16[16,192,256]{2,1,0:T(8,128)(2,1)} %bitcast.22), calls=%async_computation.4 | async-start | bytes 3145728 | tf_op jit(solution)/shard_map/all_to_all | solution.py:16
  155.0 2.1 %copy-start.2 = (bf16[8,384,256]{2,1,0:T(8,128)(2,1)S(1)}, bf16[8,384,256]{2,1,0:T(8,128)(2,1)}, u32[]{:S(2)}) copy-start(bf16[8,384,256]{2,1,0:T(8,128)(2,1)} %copy-done.1) | copy-start | bytes 4718596
  155.0 2.1 %copy-start.6 = (bf16[192,1024]{1,0:T(8,128)(2,1)S(1)}, bf16[192,1024]{1,0:T(8,128)(2,1)}, u32[]{:S(2)}) copy-start(bf16[192,1024]{1,0:T(8,128)(2,1)} %copy-done.5) | copy-start | bytes 1179652
  155.4 6.0 %collective-permute-start.4 = (bf16[192,256]{1,0:T(8,128)(2,1)S(1)}, bf16[192,256]{1,0:T(8,128)(2,1)S(1)}, u32[]{:S(2)}, u32[]{:S(2)}) collective-permute-start(bf16[192,256]{1,0:T(8,128)(2,1)S(1)} %select_convert_fusion), channel_id=1, source_target_pairs={{0,16},{16,0},{32,48},{48,32},{64,80},{80,64},{96,112},{112,96},{1... | collective-permute-start | bytes 294920 | tf_op jit(solution)/shard_map/ppermute | solution.py:8

commit v2 on v1

--- a/solution.py
+++ b/solution.py
@@ -16,6 +16,71 @@
     return lax.all_to_all(
         parts, axis, split_axis=0, concat_axis=0, tiled=True, axis_index_groups=groups
     )
+
+
+def along_ring(x):
+    places, lanes = lax.axis_size("layer"), lax.axis_size("latent")
+    ring = places // 2
+    pairs = []
+    for place in range(places):
+        for lane in range(lanes):
+            hop = 1 if lane % 2 == 0 else ring - 1
+            target = (place // ring) * ring + (place % ring + hop) % ring
+            pairs.append((place * lanes + lane, target * lanes + lane))
+    return lax.ppermute(x, ("layer", "latent"), pairs)
+
+
+def block_at(blocks, spot):
+    return lax.dynamic_index_in_dim(blocks, spot % blocks.shape[1], 1, keepdims=False)
+
+
+def added(a, b):
+    return (a.astype(jnp.float32) + b.astype(jnp.float32)).astype(jnp.bfloat16)
+
+
+def latents_of_all(own, plane, spot, way):
+    places = lax.axis_size("layer")
+    ring = places // 2
+    lower = lax.ppermute(own, "layer", [(i, i + ring) for i in range(ring)])
+    upper = plane == 1
+    both = jnp.stack(
+        [jnp.where(upper, lower, own), jnp.where(upper, own, jnp.zeros_like(own))], 0
+    )
+    stack = jnp.zeros((2, ring, *own.shape), own.dtype)
+
+    def put(stack, block, where):
+        return lax.dynamic_update_index_in_dim(stack, block, where % ring, 1)
+
+    stack = put(stack, both, spot)
+    moving = jnp.stack([both, from_partner(both, "latent", 1)], 0)
+    for step in range(1, ring // 2):
+        moving = along_ring(moving)
+        stack = put(stack, moving[0], spot + ring - step * way)
+        stack = put(stack, from_partner(moving[1], "latent", 1), spot + ring + step * way)
+    return put(stack, along_ring(moving[0]), spot + ring // 2)
+
+
+def terms_to_layers(terms, plane, spot, way):
+    ring = terms.shape[1]
+    far = ring // 2
+    mine = [block_at(terms, spot + ring + step * way) for step in range(far + 1)]
+    given = jnp.stack([block_at(terms, spot + ring - step * way) for step in range(1, far)], 0)
+    taken = from_partner(given, "latent", 1)
+    moving = along_ring(mine[far])
+    moving = jnp.stack([added(mine[far - 1], moving), taken[far - 2]], 0)
+    for step in range(far - 2, 0, -1):
+        moving = added(along_ring(moving), jnp.stack([mine[step], taken[step - 1]], 0))
+    moving = along_ring(moving)
+    from_other = from_partner(moving[1], "latent", 1)
+    total = (
+        moving[0].astype(jnp.float32)
+        + from_other.astype(jnp.float32)
+        + mine[0].astype(jnp.float32)
+    )
+    crossed = lax.ppermute(
+        total[0].astype(jnp.bfloat16), "layer", [(i + ring, i) for i in range(ring)]
+    )
+    return jnp.where(plane == 1, total[1], total[0] + crossed.astype(jnp.float32))
 
 
 def rows_of_all(x):
@@ -57,8 +122,11 @@
     pre_half = kept + from_partner(given, "layer", 1) + bias
     latents_half = jnp.maximum(pre_half, 0.0).astype(jnp.bfloat16)
 
-    copies = jnp.broadcast_to(latents_half[None], (places, half_rows, latent_cols))
-    gathered = exchanged(copies, "layer").reshape(layer_count, total_rows, latent_cols)
+    ring = places // 2
+    plane, spot = position // ring, position % ring
+    way = 1 - 2 * (lax.axis_index("latent") % 2)
+    gathered = latents_of_all(latents_half, plane, spot, way)
+    gathered = gathered.reshape(layer_count, total_rows, latent_cols)
     used = lax.broadcasted_iota(jnp.int32, (layer_count, 1, 1), 0) <= layer_now
     latents = jnp.where(used, gathered, jnp.zeros_like(gathered))
 
@@ -73,13 +141,13 @@
     lat_terms = lax.dot_general(
         dec_weight, out_grad, (((2,), (1,)), ((), ())), preferred_element_type=jnp.float32
     )
-    lat_terms = jnp.swapaxes(lat_terms, 1, 2).astype(jnp.bfloat16)
+    lat_terms = jnp.where(used, jnp.swapaxes(lat_terms, 1, 2), 0.0).astype(jnp.bfloat16)
     dec_grad = lax.dot_general(
         latents, out_grad, (((1,), (0,)), ((), ())), preferred_element_type=jnp.float32
     ).astype(jnp.bfloat16)
-    arrived = exchanged(lat_terms.reshape(places, half_rows, latent_cols), "layer")
-    later = lax.broadcasted_iota(jnp.int32, (places, 1, 1), 0) // 2 >= layer_now
-    lat_grad = jnp.where(later, arrived, jnp.zeros_like(arrived)).astype(jnp.float32).sum(axis=0)
+    lat_grad = terms_to_layers(
+        lat_terms.reshape(2, ring, half_rows, latent_cols), plane, spot, way
+    )
     pre_grad = jnp.where(latents_half > 0, lat_grad, 0.0).astype(jnp.bfloat16)
     pre_other = from_partner(pre_grad, "layer", 1)
     first = which_half == 0

time: 163 us -> 161 us (0.988)
  starting transfers between devices: 16.8 us -> 9.08 us
  waiting for transfers between devices: 85.2 us -> 88.1 us
    all_to_all x2 -> x0, waiting for transfers between devices: 75.5 us -> none  [exchanged(): lax.all_to_all(parts, axis, split_axis=0, concat_axis=0, tiled=True, axis...]
    ppermute x0 -> x10, waiting for transfers between devices: none -> 71.5 us  [the longest x8 63.9 us: along_ring(): return lax.ppermute(x, ('layer', 'latent'), pairs)]
    all_to_all x2 -> x0, starting transfers between devices: 13 us -> none  [exchanged(): lax.all_to_all(parts, axis, split_axis=0, concat_axis=0, tiled=True, axis...]
    ppermute x5 -> x11, waiting for transfers between devices: 9.65 us -> 16.6 us  [from_partner(): lax.ppermute(x, axis, [(i, i ^ bit) for i in range(lax.axis_size(axis))])]
    ppermute x0 -> x10, starting transfers between devices: none -> 6.2 us  [the longest x1 2.59 us: latents_of_all(): lower = lax.ppermute(own, 'layer', [(i, i + ring) for i in range(ring)])]
    dot_general x1, matrix products: 4.59 us -> 1.84 us  [local(): lax.dot_general(latents, dec_weight, (((0, 2), (0, 1)), ((), ())), prefer...]
    dot_general x1, matrix products: 4.39 us -> 6.13 us  [local(): lax.dot_general(latents, out_grad, (((1,), (0,)), ((), ())), preferred_el...]
    ppermute x5 -> x11, starting transfers between devices: 3.73 us -> 2.88 us  [from_partner(): lax.ppermute(x, axis, [(i, i ^ bit) for i in range(lax.axis_size(axis))])]
  transfers between devices with their start and end apart: 7 -> 21, of which waited for: 6 -> 19; matrix products, arithmetic and copies ran while one was open for 3% -> 4% of each run, Pallas kernels for 0% -> 0%
where the time goes in v2:
time: 161 us; the launch traced here: 160 us
  waiting for transfers between devices  88.1 us (55%)
  blocking collectives  42.3 us (26%)
  matrix products  13.9 us (9%)
  starting transfers between devices  9.08 us (6%)
  local copies, waits for them, and re-layouts  3.71 us (2%)
  other arithmetic  1.86 us (1%)
    ppermute x8, waiting for transfers between devices, along_ring(): return lax.ppermute(x, ('layer', 'latent'), pairs)  63.9 us
    all_to_all x3, blocking collectives, exchanged(): lax.all_to_all(parts, axis, split_axis=0, concat_axis=0, tiled=True, axis...  42.3 us
    ppermute x11, waiting for transfers between devices, from_partner(): lax.ppermute(x, axis, [(i, i ^ bit) for i in range(lax.axis_size(axis))])  16.6 us
    dot_general x1, matrix products, local(): lax.dot_general(latents, out_grad, (((1,), (0,)), ((), ())), preferred_el...  6.13 us
    ppermute x1, waiting for transfers between devices, terms_to_layers(): lax.ppermute(total[0].astype(jnp.bfloat16), 'layer', [(i + ring, i) for i...  5.43 us
    dot_general x1, matrix products, local(): lax.dot_general(dec_weight, out_grad, (((2,), (1,)), ((), ())), preferred...  4.15 us
  transfers between devices with their start and end apart: 21, of which 19 were waited for; matrix products, arithmetic and copies ran while one was open for 4% of the time, Pallas kernels for 0%

profile of v2, /device:TPU:2, one launch (start us, length us, event | category | flops | bytes accessed | tf_op | source)
XLA Modules:
  0.0 160.0 jit_solution(4311209386605984238)
XLA Ops:
  0.6 0.9 broadcast_in_dim.65
  1.5 16.3 %all_to_all.15 = bf16[8,24,1024]{2,1,0:T(8,128)(2,1)S(1)} all-to-all(bf16[8,24,1024]{2,1,0:T(8,128)(2,1)S(1)} %broadcast_in_dim.65), channel_id=1, replica_groups={{0,2,4,6,8,10,12,14},{1,3,5,7,9,11,13,15},{16,18,20,22,24,26,28,30},{17..., dimensions={0} | all-to-all | bytes 786432 | tf_op jit(solution)/shard_map/all_to_all | solution.py:16
  17.8 1.7 %collective-permute-done = bf16[192,1024]{1,0:T(8,128)(2,1)S(1)} collective-permute-done((bf16[192,1024]{1,0:T(8,128)(2,1)S(1)}, bf16[192,1024]{1,0:T(8,128)(2,1)S(1)}, u32[]{:S(2)}, u32[]{:S(2)}) %collective-permute-start) | collective-permute-done | bytes 393248 | tf_op jit(solution)/shard_map/ppermute | solution.py:8
  20.7 2.0 %collective-permute-start.1 = (f32[192,256]{1,0:T(8,128)S(1)}, f32[192,256]{1,0:T(8,128)S(1)}, u32[]{:S(2)}, u32[]{:S(2)}) collective-permute-start(f32[192,256]{1,0:T(8,128)S(1)} %constant_dynamic-slice_fusion.1), channel_id=1, source_target_pairs={{0,16},{16,0},{32,48},{48,32},{64,80},{80,64},{96,112},{112,96},{1... | collective-permute-start | bytes 589832 | tf_op jit(solution)/shard_map/ppermute | solution.py:8
  23.4 4.5 %collective-permute-done.1 = f32[192,256]{1,0:T(8,128)S(1)} collective-permute-done((f32[192,256]{1,0:T(8,128)S(1)}, f32[192,256]{1,0:T(8,128)S(1)}, u32[]{:S(2)}, u32[]{:S(2)}) %collective-permute-start.1) | collective-permute-done | bytes 196640 | tf_op jit(solution)/shard_map/ppermute | solution.py:8
  27.9 2.6 %collective-permute-start.2 = (bf16[192,256]{1,0:T(8,128)(2,1)S(1)}, bf16[192,256]{1,0:T(8,128)(2,1)S(1)}, u32[]{:S(2)}, u32[]{:S(2)}) collective-permute-start(bf16[192,256]{1,0:T(8,128)(2,1)S(1)} %get-tuple-element.3), channel_id=1, source_target_pairs={{0,128},{16,144},{32,160},{48,176},{64,192},{80,208},{96,224},{112... | collective-permute-start | bytes 294920 | tf_op jit(solution)/shard_map/ppermute | solution.py:44
  30.5 2.2 %collective-permute-done.2 = bf16[192,256]{1,0:T(8,128)(2,1)S(1)} collective-permute-done((bf16[192,256]{1,0:T(8,128)(2,1)S(1)}, bf16[192,256]{1,0:T(8,128)(2,1)S(1)}, u32[]{:S(2)}, u32[]{:S(2)}) %collective-permute-start.2) | collective-permute-done | bytes 98336 | tf_op jit(solution)/shard_map/ppermute | solution.py:44
  32.9 1.4 collective-permute-done.3
  34.4 1.8 %collective-permute-start.4 = (bf16[2,2,192,256]{3,2,1,0:T(8,128)(2,1)S(1)}, bf16[2,2,192,256]{3,2,1,0:T(8,128)(2,1)S(1)}, u32[]{:S(2)}, u32[]{:S(2)}) collective-permute-start(bf16[2,2,192,256]{3,2,1,0:T(8,128)(2,1)S(1)} %pad_maximum_fusion.4), channel_id=1, source_target_pairs={{0,16},{1,113},{2,18},{3,115},{4,20},{5,117},{6,22},{7,119},{8,24}... | collective-permute-start | bytes 1179656 | tf_op jit(solution)/shard_map/ppermute | solution.py:30
  36.4 9.5 %collective-permute-done.4 = bf16[2,2,192,256]{3,2,1,0:T(8,128)(2,1)S(1)} collective-permute-done((bf16[2,2,192,256]{3,2,1,0:T(8,128)(2,1)S(1)}, bf16[2,2,192,256]{3,2,1,0:T(8,128)(2,1)S(1)}, u32[]{:S(2)}, u32[]{:S(2)}) %collective-permute-start.4) | collective-permute-done | bytes 393248 | tf_op jit(solution)/shard_map/ppermute | solution.py:30
  46.1 1.3 collective-permute-done.5
  47.4 7.6 %collective-permute-done.6 = bf16[2,2,192,256]{3,2,1,0:T(8,128)(2,1)S(1)} collective-permute-done((bf16[2,2,192,256]{3,2,1,0:T(8,128)(2,1)S(1)}, bf16[2,2,192,256]{3,2,1,0:T(8,128)(2,1)S(1)}, u32[]{:S(2)}, u32[]{:S(2)}) %collective-permute-start.6) | collective-permute-done | bytes 393248 | tf_op jit(solution)/shard_map/ppermute | solution.py:30
  55.3 1.3 collective-permute-done.7
  56.6 7.6 %collective-permute-done.8 = bf16[2,2,192,256]{3,2,1,0:T(8,128)(2,1)S(1)} collective-permute-done((bf16[2,2,192,256]{3,2,1,0:T(8,128)(2,1)S(1)}, bf16[2,2,192,256]{3,2,1,0:T(8,128)(2,1)S(1)}, u32[]{:S(2)}, u32[]{:S(2)}) %collective-permute-start.8) | collective-permute-done | bytes 393248 | tf_op jit(solution)/shard_map/ppermute | solution.py:30
  64.5 1.4 collective-permute-done.9
  65.9 5.3 %collective-permute-done.10 = bf16[2,192,256]{2,1,0:T(8,128)(2,1)S(1)} collective-permute-done((bf16[2,192,256]{2,1,0:T(8,128)(2,1)S(1)}, bf16[2,192,256]{2,1,0:T(8,128)(2,1)S(1)}, u32[]{:S(2)}, u32[]{:S(2)}) %collective-permute-start.10) | collective-permute-done | bytes 196640 | tf_op jit(solution)/shard_map/ppermute | solution.py:30
  71.3 1.8 %convolution_bitcast_fusion = f32[384,1024]{1,0:T(8,128)S(1)} fusion(bf16[8,256,1024]{2,1,0:T(8,128)(2,1)S(1)} %copy-done.4, bf16[8,384,256]{2,1,0:T(8,128)(2,1)S(1)} %bitcast.116, pred[8]{0:T(512)(128)(4,1)S(1)} %iota_compare_fusion), kind=kOutput, calls=%fused_computation.3 | convolution fusion | flops 1611399168 | bytes 7340040 | tf_op jit(solution)/shard_map/dot_general | solution.py:133
  73.3 1.7 %collective-permute-done.11 = bf16[192,1024]{1,0:T(8,128)(2,1)S(1)} collective-permute-done((bf16[192,1024]{1,0:T(8,128)(2,1)S(1)}, bf16[192,1024]{1,0:T(8,128)(2,1)S(1)}, u32[]{:S(2)}, u32[]{:S(2)}) %collective-permute-start.11) | collective-permute-done | bytes 393248 | tf_op jit(solution)/shard_map/ppermute | solution.py:8
  75.1 13.6 %all_to_all.16 = bf16[8,24,1024]{2,1,0:T(8,128)(2,1)S(1)} all-to-all(bf16[8,24,1024]{2,1,0:T(8,128)(2,1)S(1)} %bitcast.118), channel_id=1, replica_groups={{0,2,4,6,8,10,12,14},{1,3,5,7,9,11,13,15},{16,18,20,22,24,26,28,30},{17..., dimensions={0} | all-to-all | bytes 786432 | tf_op jit(solution)/shard_map/all_to_all | solution.py:16
  88.9 12.4 %all_to_all.17 = bf16[8,24,1024]{2,1,0:T(8,128)(2,1)S(1)} all-to-all(bf16[8,24,1024]{2,1,0:T(8,128)(2,1)S(1)} %broadcast_in_dim.78), channel_id=1, replica_groups={{0,2,4,6,8,10,12,14},{1,3,5,7,9,11,13,15},{16,18,20,22,24,26,28,30},{17..., dimensions={0} | all-to-all | bytes 786432 | tf_op jit(solution)/shard_map/all_to_all | solution.py:16
  101.2 1.7 %collective-permute-done.12 = bf16[192,1024]{1,0:T(8,128)(2,1)S(1)} collective-permute-done((bf16[192,1024]{1,0:T(8,128)(2,1)S(1)}, bf16[192,1024]{1,0:T(8,128)(2,1)S(1)}, u32[]{:S(2)}, u32[]{:S(2)}) %collective-permute-start.12) | collective-permute-done | bytes 393248 | tf_op jit(solution)/shard_map/ppermute | solution.py:8
  103.0 4.2 %select_convert_fusion = bf16[384,8,256]{2,0,1:T(8,128)(2,1)S(1)} fusion(bf16[8,256,1024]{2,1,0:T(8,128)(2,1)} %param.9, pred[8]{0:T(512)(128)(4,1)S(1)} %iota_compare_fusion, bf16[192,1024]{1,0:T(8,128)(2,1)S(1)} %collective-permute-done.12, bf16[192,1024]{1,0:T(8,128)(2,1)S(1)} %bitcast.123), kind=kOutput, calls=%fused_computation | convolution fusion | flops 1613758464 | bytes 6553608 | tf_op jit(solution)/shard_map/dot_general | solution.py:141
  107.5 6.9 %collective-permute-done.13 = bf16[2,192,256]{2,1,0:T(8,128)(2,1)S(1)} collective-permute-done((bf16[2,192,256]{2,1,0:T(8,128)(2,1)S(1)}, bf16[2,192,256]{2,1,0:T(8,128)(2,1)S(1)}, u32[]{:S(2)}, u32[]{:S(2)}) %collective-permute-start.13) | collective-permute-done | bytes 196640 | tf_op jit(solution)/shard_map/ppermute | solution.py:30
  114.7 9.0 %collective-permute-done.15 = bf16[2,2,192,256]{3,2,1,0:T(8,128)(2,1)S(1)} collective-permute-done((bf16[2,2,192,256]{3,2,1,0:T(8,128)(2,1)S(1)}, bf16[2,2,192,256]{3,2,1,0:T(8,128)(2,1)S(1)}, u32[]{:S(2)}, u32[]{:S(2)}) %collective-permute-start.15) | collective-permute-done | bytes 393248 | tf_op jit(solution)/shard_map/ppermute | solution.py:30
  123.8 9.0 %collective-permute-done.16 = bf16[2,2,192,256]{3,2,1,0:T(8,128)(2,1)S(1)} collective-permute-done((bf16[2,2,192,256]{3,2,1,0:T(8,128)(2,1)S(1)}, bf16[2,2,192,256]{3,2,1,0:T(8,128)(2,1)S(1)}, u32[]{:S(2)}, u32[]{:S(2)}) %collective-permute-start.16) | collective-permute-done | bytes 393248 | tf_op jit(solution)/shard_map/ppermute | solution.py:30
  133.0 9.0 %collective-permute-done.17 = bf16[2,2,192,256]{3,2,1,0:T(8,128)(2,1)S(1)} collective-permute-done((bf16[2,2,192,256]{3,2,1,0:T(8,128)(2,1)S(1)}, bf16[2,2,192,256]{3,2,1,0:T(8,128)(2,1)S(1)}, u32[]{:S(2)}, u32[]{:S(2)}) %collective-permute-start.17) | collective-permute-done | bytes 393248 | tf_op jit(solution)/shard_map/ppermute | solution.py:30
  142.9 1.5 collective-permute-done.18
  144.4 1.1 convert_add_fusion
  145.5 1.3 collective-permute-start.19
  146.8 5.4 %collective-permute-done.19 = bf16[192,256]{1,0:T(8,128)(2,1)S(1)} collective-permute-done((bf16[192,256]{1,0:T(8,128)(2,1)S(1)}, bf16[192,256]{1,0:T(8,128)(2,1)S(1)}, u32[]{:S(2)}, u32[]{:S(2)}) %collective-permute-start.19) | collective-permute-done | bytes 98336 | tf_op jit(solution)/shard_map/ppermute | solution.py:80
  152.4 6.1 %convolution_convert_fusion = bf16[8,256,1024]{2,1,0:T(8,128)(2,1)} fusion(bf16[8,384,256]{2,1,0:T(8,128)(2,1)} %bitcast.117, pred[8]{0:T(512)(128)(4,1)S(1)} %iota_compare_fusion, bf16[192,1024]{1,0:T(8,128)(2,1)} %copy-done.7, bf16[192,1024]{1,0:T(8,128)(2,1)S(1)} %bitcast.124), kind=kOutput, calls=%fused_computation.1 | convolution fusion | flops 1615069184 | bytes 6553608 | tf_op jit(solution)/shard_map/dot_general | solution.py:145
  158.6 1.4 fusion.1
  (71 shorter events, 5.4 us)
Async XLA Ops:
  0.6 19.7 %copy-start = (bf16[1024,256]{1,0:T(8,128)(2,1)S(1)}, bf16[1024,256]{1,0:T(8,128)(2,1)}, u32[]{:S(2)}) copy-start(bf16[1024,256]{1,0:T(8,128)(2,1)} %param.7) | copy-start | bytes 1572868
  17.8 1.7 %collective-permute-start = (bf16[192,1024]{1,0:T(8,128)(2,1)S(1)}, bf16[192,1024]{1,0:T(8,128)(2,1)S(1)}, u32[]{:S(2)}, u32[]{:S(2)}) collective-permute-start(bf16[192,1024]{1,0:T(8,128)(2,1)S(1)} %bitcast.119), channel_id=1, source_target_pairs={{0,1},{1,0},{2,3},{3,2},{4,5},{5,4},{6,7},{7,6},{8,9},{9,8},{10,11... | collective-permute-start | bytes 1179656 | tf_op jit(solution)/shard_map/ppermute | solution.py:8
  19.5 0.7 copy-start.5
  20.7 7.2 %collective-permute-start.1 = (f32[192,256]{1,0:T(8,128)S(1)}, f32[192,256]{1,0:T(8,128)S(1)}, u32[]{:S(2)}, u32[]{:S(2)}) collective-permute-start(f32[192,256]{1,0:T(8,128)S(1)} %constant_dynamic-slice_fusion.1), channel_id=1, source_target_pairs={{0,16},{16,0},{32,48},{48,32},{64,80},{80,64},{96,112},{112,96},{1... | collective-permute-start | bytes 589832 | tf_op jit(solution)/shard_map/ppermute | solution.py:8
  27.9 4.8 %collective-permute-start.2 = (bf16[192,256]{1,0:T(8,128)(2,1)S(1)}, bf16[192,256]{1,0:T(8,128)(2,1)S(1)}, u32[]{:S(2)}, u32[]{:S(2)}) collective-permute-start(bf16[192,256]{1,0:T(8,128)(2,1)S(1)} %get-tuple-element.3), channel_id=1, source_target_pairs={{0,128},{16,144},{32,160},{48,176},{64,192},{80,208},{96,224},{112... | collective-permute-start | bytes 294920 | tf_op jit(solution)/shard_map/ppermute | solution.py:44
  32.8 1.5 collective-permute-start.3
  34.4 11.5 %collective-permute-start.4 = (bf16[2,2,192,256]{3,2,1,0:T(8,128)(2,1)S(1)}, bf16[2,2,192,256]{3,2,1,0:T(8,128)(2,1)S(1)}, u32[]{:S(2)}, u32[]{:S(2)}) collective-permute-start(bf16[2,2,192,256]{3,2,1,0:T(8,128)(2,1)S(1)} %pad_maximum_fusion.4), channel_id=1, source_target_pairs={{0,16},{1,113},{2,18},{3,115},{4,20},{5,117},{6,22},{7,119},{8,24}... | collective-permute-start | bytes 1179656 | tf_op jit(solution)/shard_map/ppermute | solution.py:30
  45.9 25.4 %copy-start.4 = (bf16[8,256,1024]{2,1,0:T(8,128)(2,1)S(1)}, bf16[8,256,1024]{2,1,0:T(8,128)(2,1)}, u32[]{:S(2)}) copy-start(bf16[8,256,1024]{2,1,0:T(8,128)(2,1)} %param.9) | copy-start | bytes 12582916
  45.9 1.5 collective-permute-start.5
  46.0 9.1 %collective-permute-start.6 = (bf16[2,2,192,256]{3,2,1,0:T(8,128)(2,1)S(1)}, bf16[2,2,192,256]{3,2,1,0:T(8,128)(2,1)S(1)}, u32[]{:S(2)}, u32[]{:S(2)}) collective-permute-start(bf16[2,2,192,256]{3,2,1,0:T(8,128)(2,1)S(1)} %collective-permute-done.4), channel_id=1, source_target_pairs={{0,16},{1,113},{2,18},{3,115},{4,20},{5,117},{6,22},{7,119},{8,24}... | collective-permute-start | bytes 1179656 | tf_op jit(solution)/shard_map/ppermute | solution.py:30
  55.1 1.5 collective-permute-start.7
  55.2 9.1 %collective-permute-start.8 = (bf16[2,2,192,256]{3,2,1,0:T(8,128)(2,1)S(1)}, bf16[2,2,192,256]{3,2,1,0:T(8,128)(2,1)S(1)}, u32[]{:S(2)}, u32[]{:S(2)}) collective-permute-start(bf16[2,2,192,256]{3,2,1,0:T(8,128)(2,1)S(1)} %collective-permute-done.6), channel_id=1, source_target_pairs={{0,16},{1,113},{2,18},{3,115},{4,20},{5,117},{6,22},{7,119},{8,24}... | collective-permute-start | bytes 1179656 | tf_op jit(solution)/shard_map/ppermute | solution.py:30
  64.3 7.0 %collective-permute-start.10 = (bf16[2,192,256]{2,1,0:T(8,128)(2,1)S(1)}, bf16[2,192,256]{2,1,0:T(8,128)(2,1)S(1)}, u32[]{:S(2)}, u32[]{:S(2)}) collective-permute-start(bf16[2,192,256]{2,1,0:T(8,128)(2,1)S(1)} %get-tuple-element.13), channel_id=1, source_target_pairs={{0,16},{1,113},{2,18},{3,115},{4,20},{5,117},{6,22},{7,119},{8,24}... | collective-permute-start | bytes 589832 | tf_op jit(solution)/shard_map/ppermute | solution.py:30
  64.4 1.5 collective-permute-start.9
  71.2 1.9 %copy-start.1 = (bf16[2,8,192,256]{3,2,1,0:T(8,128)(2,1)}, bf16[2,8,192,256]{3,2,1,0:T(8,128)(2,1)S(1)}, u32[]{:S(2)}) copy-start(bf16[2,8,192,256]{3,2,1,0:T(8,128)(2,1)S(1)} %bitcast_dynamic-update-slice_fusion) | copy-start | bytes 4718596
  73.2 15.6 %copy-start.3 = (bf16[24,1024]{1,0:T(8,128)(2,1)S(1)}, bf16[24,1024]{1,0:T(8,128)(2,1)}, u32[]{:S(2)}) copy-start(bf16[24,1024]{1,0:T(8,128)(2,1)} %param.6) | copy-start | bytes 147460
  73.2 1.8 %collective-permute-start.11 = (bf16[192,1024]{1,0:T(8,128)(2,1)S(1)}, bf16[192,1024]{1,0:T(8,128)(2,1)S(1)}, u32[]{:S(2)}, u32[]{:S(2)}) collective-permute-start(bf16[192,1024]{1,0:T(8,128)(2,1)S(1)} %slice.109), channel_id=1, source_target_pairs={{0,1},{1,0},{2,3},{3,2},{4,5},{5,4},{6,7},{7,6},{8,9},{9,8},{10,11... | collective-permute-start | bytes 1179656 | tf_op jit(solution)/shard_map/ppermute | solution.py:8
  101.2 1.7 %collective-permute-start.12 = (bf16[192,1024]{1,0:T(8,128)(2,1)S(1)}, bf16[192,1024]{1,0:T(8,128)(2,1)S(1)}, u32[]{:S(2)}, u32[]{:S(2)}) collective-permute-start(bf16[192,1024]{1,0:T(8,128)(2,1)S(1)} %bitcast.122), channel_id=1, source_target_pairs={{0,1},{1,0},{2,3},{3,2},{4,5},{5,4},{6,7},{7,6},{8,9},{9,8},{10,11... | collective-permute-start | bytes 1179656 | tf_op jit(solution)/shard_map/ppermute | solution.py:8
  102.9 4.2 %copy-start.7 = (bf16[192,1024]{1,0:T(8,128)(2,1)}, bf16[192,1024]{1,0:T(8,128)(2,1)S(1)}, u32[]{:S(2)}) copy-start(bf16[192,1024]{1,0:T(8,128)(2,1)S(1)} %collective-permute-done.12) | copy-start | bytes 1179652
  107.3 7.2 %collective-permute-start.14 = (bf16[3,2,192,256]{3,2,1,0:T(8,128)(2,1)S(1)}, bf16[3,2,192,256]{3,2,1,0:T(8,128)(2,1)S(1)}, u32[]{:S(2)}, u32[]{:S(2)}) collective-permute-start(bf16[3,2,192,256]{3,2,1,0:T(8,128)(2,1)S(1)} %pad_maximum_fusion.1), channel_id=1, source_target_pairs={{0,1},{1,0},{2,3},{3,2},{4,5},{5,4},{6,7},{7,6},{8,9},{9,8},{10,11... | collective-permute-start | bytes 1769480 | tf_op jit(solution)/shard_map/ppermute | solution.py:8
  107.5 6.9 %collective-permute-start.13 = (bf16[2,192,256]{2,1,0:T(8,128)(2,1)S(1)}, bf16[2,192,256]{2,1,0:T(8,128)(2,1)S(1)}, u32[]{:S(2)}, u32[]{:S(2)}) collective-permute-start(bf16[2,192,256]{2,1,0:T(8,128)(2,1)S(1)} %get-tuple-element.9), channel_id=1, source_target_pairs={{0,16},{1,113},{2,18},{3,115},{4,20},{5,117},{6,22},{7,119},{8,24}... | collective-permute-start | bytes 589832 | tf_op jit(solution)/shard_map/ppermute | solution.py:30
  114.6 9.1 %collective-permute-start.15 = (bf16[2,2,192,256]{3,2,1,0:T(8,128)(2,1)S(1)}, bf16[2,2,192,256]{3,2,1,0:T(8,128)(2,1)S(1)}, u32[]{:S(2)}, u32[]{:S(2)}) collective-permute-start(bf16[2,2,192,256]{3,2,1,0:T(8,128)(2,1)S(1)} %pad_maximum_fusion.5), channel_id=1, source_target_pairs={{0,16},{1,113},{2,18},{3,115},{4,20},{5,117},{6,22},{7,119},{8,24}... | collective-permute-start | bytes 1179656 | tf_op jit(solution)/shard_map/ppermute | solution.py:30
  123.8 9.1 %collective-permute-start.16 = (bf16[2,2,192,256]{3,2,1,0:T(8,128)(2,1)S(1)}, bf16[2,2,192,256]{3,2,1,0:T(8,128)(2,1)S(1)}, u32[]{:S(2)}, u32[]{:S(2)}) collective-permute-start(bf16[2,2,192,256]{3,2,1,0:T(8,128)(2,1)S(1)} %add_convert_fusion.1), channel_id=1, source_target_pairs={{0,16},{1,113},{2,18},{3,115},{4,20},{5,117},{6,22},{7,119},{8,24}... | collective-permute-start | bytes 1179656 | tf_op jit(solution)/shard_map/ppermute | solution.py:30
  132.9 9.1 %collective-permute-start.17 = (bf16[2,2,192,256]{3,2,1,0:T(8,128)(2,1)S(1)}, bf16[2,2,192,256]{3,2,1,0:T(8,128)(2,1)S(1)}, u32[]{:S(2)}, u32[]{:S(2)}) collective-permute-start(bf16[2,2,192,256]{3,2,1,0:T(8,128)(2,1)S(1)} %add_convert_fusion), channel_id=1, source_target_pairs={{0,16},{1,113},{2,18},{3,115},{4,20},{5,117},{6,22},{7,119},{8,24}... | collective-permute-start | bytes 1179656 | tf_op jit(solution)/shard_map/ppermute | solution.py:30
  142.0 0.7 copy-start.2
  142.8 1.7 %collective-permute-start.18 = (bf16[2,192,256]{2,1,0:T(8,128)(2,1)S(1)}, bf16[2,192,256]{2,1,0:T(8,128)(2,1)}, u32[]{:S(2)}, u32[]{:S(2)}) collective-permute-start(bf16[2,192,256]{2,1,0:T(8,128)(2,1)S(1)} %slice_bitcast_fusion.2), channel_id=1, source_target_pairs={{0,1},{1,0},{2,3},{3,2},{4,5},{5,4},{6,7},{7,6},{8,9},{9,8},{10,11... | collective-permute-start | bytes 589832 | tf_op jit(solution)/shard_map/ppermute | solution.py:8
  145.5 6.7 %collective-permute-start.19 = (bf16[192,256]{1,0:T(8,128)(2,1)S(1)}, bf16[192,256]{1,0:T(8,128)(2,1)S(1)}, u32[]{:S(2)}, u32[]{:S(2)}) collective-permute-start(bf16[192,256]{1,0:T(8,128)(2,1)S(1)} %fusion.13), channel_id=1, source_target_pairs={{128,0},{144,16},{160,32},{176,48},{192,64},{208,80},{224,96},{240... | collective-permute-start | bytes 294920 | tf_op jit(solution)/shard_map/ppermute | solution.py:80
  152.3 6.3 %copy-start.6 = (bf16[192,1024]{1,0:T(8,128)(2,1)S(1)}, bf16[192,1024]{1,0:T(8,128)(2,1)}, u32[]{:S(2)}) copy-start(bf16[192,1024]{1,0:T(8,128)(2,1)} %copy-done.5) | copy-start | bytes 1179652
  152.3 6.2 %collective-permute-start.20 = (bf16[192,256]{1,0:T(8,128)(2,1)S(1)}, bf16[192,256]{1,0:T(8,128)(2,1)S(1)}, u32[]{:S(2)}, u32[]{:S(2)}) collective-permute-start(bf16[192,256]{1,0:T(8,128)(2,1)S(1)} %fusion.7), channel_id=1, source_target_pairs={{0,16},{16,0},{32,48},{48,32},{64,80},{80,64},{96,112},{112,96},{1... | collective-permute-start | bytes 294920 | tf_op jit(solution)/shard_map/ppermute | solution.py:8

commit v3 on v1

--- a/solution.py
+++ b/solution.py
@@ -16,6 +16,97 @@
     return lax.all_to_all(
         parts, axis, split_axis=0, concat_axis=0, tiled=True, axis_index_groups=groups
     )
+
+
+def along_ring(x, hop):
+    places = lax.axis_size("layer")
+    ring = places // 2
+    pairs = [(i, (i // ring) * ring + (i % ring + hop) % ring) for i in range(places)]
+    return lax.ppermute(x, "layer", pairs)
+
+
+def to_later_plane(x):
+    ring = lax.axis_size("layer") // 2
+    return lax.ppermute(x, "layer", [(i, i + ring) for i in range(ring)])
+
+
+def to_earlier_plane(x):
+    ring = lax.axis_size("layer") // 2
+    return lax.ppermute(x, "layer", [(i + ring, i) for i in range(ring)])
+
+
+def added(*terms):
+    return sum(term.astype(jnp.float32) for term in terms).astype(jnp.bfloat16)
+
+
+def latents_of_all(own, plane, spot, ring):
+    far = ring // 2
+    half = own.shape[0] // 2
+    stack = jnp.zeros((2 * ring, *own.shape), own.dtype)
+
+    def put(stack, block, which, distance):
+        place = which * ring + (spot + distance) % ring
+        return lax.dynamic_update_index_in_dim(stack, block, place, 0)
+
+    found = [(own, 0)]
+    up = down = own
+    bundles = []
+    for step in range(1, far):
+        up, down = along_ring(up, 1), along_ring(down, ring - 1)
+        found += [(up, ring - step), (down, step)]
+        if step == far // 2:
+            crossed = to_later_plane(jnp.stack([block for block, _ in found], 0))
+            bundles.append((crossed, [distance for _, distance in found]))
+    ends = jnp.concatenate(
+        [along_ring(up[:half], 1), along_ring(down[half:], ring - 1)], 0
+    )
+    found.append((ends, far))
+    sent = len(bundles[0][1])
+    crossed = to_later_plane(jnp.stack([block for block, _ in found[sent:]], 0))
+    bundles.append((crossed, [distance for _, distance in found[sent:]]))
+    for block, distance in found:
+        stack = put(stack, block, plane, distance)
+    for crossed, distances in bundles:
+        for at, distance in enumerate(distances):
+            stack = put(stack, crossed[at], 1 - plane, distance)
+    return stack
+
+
+def layer_terms(out_grad, weight, used):
+    terms = lax.dot_general(
+        weight, out_grad, (((2,), (1,)), ((), ())), preferred_element_type=jnp.float32
+    )
+    return jnp.where(used, jnp.swapaxes(terms, 1, 2), 0.0).astype(jnp.bfloat16)
+
+
+def terms_to_layers(lower, own, spot, ring, tie):
+    far = ring // 2
+    half = own.shape[1] // 2
+
+    def at(blocks, distance):
+        return lax.dynamic_index_in_dim(blocks, (spot + distance) % ring, 0, keepdims=False)
+
+    first = [far, far - 1, ring - far + 1]
+    second = [d for d in range(ring) if d not in first]
+    crossed = {}
+    early = to_earlier_plane(jnp.stack([at(lower, d) for d in first], 0))
+    late = to_earlier_plane(jnp.stack([at(lower, d) for d in second], 0))
+    early, tie, own = lax.optimization_barrier((early, tie, own))
+    for bundle, distances in ((early, first), (late, second)):
+        for k, d in enumerate(distances):
+            crossed[d] = bundle[k]
+    ends = added(at(own, far), crossed[far])
+    up, down = along_ring(ends[:half], 1), along_ring(ends[half:], ring - 1)
+    for step in range(far - 1, 0, -1):
+        back = ring - step
+        if step == far - 1:
+            up = jnp.concatenate([up, jnp.zeros_like(up)], 0)
+            down = jnp.concatenate([jnp.zeros_like(down), down], 0)
+        up = added(at(own, step), crossed[step], up)
+        down = added(at(own, back), crossed[back], down)
+        up, down = along_ring(up, 1), along_ring(down, ring - 1)
+    total = sum(x.astype(jnp.float32) for x in (at(own, 0), crossed[0], up, down))
+    return total, tie
 
 
 def rows_of_all(x):
@@ -57,8 +148,10 @@
     pre_half = kept + from_partner(given, "layer", 1) + bias
     latents_half = jnp.maximum(pre_half, 0.0).astype(jnp.bfloat16)
 
-    copies = jnp.broadcast_to(latents_half[None], (places, half_rows, latent_cols))
-    gathered = exchanged(copies, "layer").reshape(layer_count, total_rows, latent_cols)
+    ring = places // 2
+    plane, spot = position // ring, position % ring
+    gathered = latents_of_all(latents_half, plane, spot, ring)
+    gathered = gathered.reshape(layer_count, total_rows, latent_cols)
     used = lax.broadcasted_iota(jnp.int32, (layer_count, 1, 1), 0) <= layer_now
     latents = jnp.where(used, gathered, jnp.zeros_like(gathered))
 
@@ -70,16 +163,18 @@
     grad_own = ((recon_own - mlp_outputs.astype(jnp.float32)) * rscale).astype(jnp.bfloat16)
     out_grad = rows_of_all(grad_own)
 
-    lat_terms = lax.dot_general(
-        dec_weight, out_grad, (((2,), (1,)), ((), ())), preferred_element_type=jnp.float32
+    near = layer_count // 2
+    lower = layer_terms(out_grad, dec_weight[:near], used[:near])
+    lower, grad_after = lax.optimization_barrier((lower, out_grad))
+    upper = layer_terms(grad_after, dec_weight[near:], used[near:])
+    own_terms = jnp.where(plane == 1, upper, lower)
+    dec_grad = lax.dot_general(
+        latents, grad_after, (((1,), (0,)), ((), ())), preferred_element_type=jnp.float32
+    ).astype(jnp.bfloat16)
+    places_shape = (ring, half_rows, latent_cols)
+    lat_grad, dec_grad = terms_to_layers(
+        lower.reshape(places_shape), own_terms.reshape(places_shape), spot, ring, dec_grad
     )
-    lat_terms = jnp.swapaxes(lat_terms, 1, 2).astype(jnp.bfloat16)
-    dec_grad = lax.dot_general(
-        latents, out_grad, (((1,), (0,)), ((), ())), preferred_element_type=jnp.float32
-    ).astype(jnp.bfloat16)
-    arrived = exchanged(lat_terms.reshape(places, half_rows, latent_cols), "layer")
-    later = lax.broadcasted_iota(jnp.int32, (places, 1, 1), 0) // 2 >= layer_now
-    lat_grad = jnp.where(later, arrived, jnp.zeros_like(arrived)).astype(jnp.float32).sum(axis=0)
     pre_grad = jnp.where(latents_half > 0, lat_grad, 0.0).astype(jnp.bfloat16)
     pre_other = from_partner(pre_grad, "layer", 1)
     first = which_half == 0

time: 163 us -> 144 us (0.88)
  waiting for transfers between devices: 85.2 us -> 46.3 us
  starting transfers between devices: 16.8 us -> 39.2 us
  matrix products: 13.8 us -> 11.6 us
    all_to_all x2 -> x0, waiting for transfers between devices: 75.5 us -> none  [exchanged(): lax.all_to_all(parts, axis, split_axis=0, concat_axis=0, tiled=True, axis...]
    ppermute x0 -> x20, starting transfers between devices: none -> 37 us  [the longest x16 28.7 us: along_ring(): return lax.ppermute(x, 'layer', pairs)]
    ppermute x0 -> x20, waiting for transfers between devices: none -> 32.1 us  [the longest x16 24.7 us: along_ring(): return lax.ppermute(x, 'layer', pairs)]
    all_to_all x2 -> x0, starting transfers between devices: 13 us -> none  [exchanged(): lax.all_to_all(parts, axis, split_axis=0, concat_axis=0, tiled=True, axis...]
    ppermute x5, waiting for transfers between devices: 9.65 us -> 14.2 us  [from_partner(): lax.ppermute(x, axis, [(i, i ^ bit) for i in range(lax.axis_size(axis))])]
    dot_general x1, matrix products: 4.59 us -> 1.78 us  [local(): lax.dot_general(latents, dec_weight, (((0, 2), (0, 1)), ((), ())), prefer...]
    dot_general x2 -> x3, matrix products: 7.39 us -> 8.02 us  [the longest x1 4.4 us: local(): lax.dot_general(latents, grad_after, (((1,), (0,)), ((), ())), preferred_...]
  transfers between devices with their start and end apart: 7 -> 25, of which waited for: 6 -> 16; matrix products, arithmetic and copies ran while one was open for 3% -> 5% of each run, Pallas kernels for 0% -> 0%
where the time goes in v3:
time: 144 us
  waiting for transfers between devices  46.3 us (32%)
  blocking collectives  42.3 us (29%)
  starting transfers between devices  39.2 us (27%)
  matrix products  11.6 us (8%)
  local copies, waits for them, and re-layouts  2.29 us (2%)
    all_to_all x3, blocking collectives, exchanged(): lax.all_to_all(parts, axis, split_axis=0, concat_axis=0, tiled=True, axis...  42.3 us
    ppermute x16, starting transfers between devices, along_ring(): return lax.ppermute(x, 'layer', pairs)  28.7 us
    ppermute x16, waiting for transfers between devices, along_ring(): return lax.ppermute(x, 'layer', pairs)  24.7 us
    ppermute x5, waiting for transfers between devices, from_partner(): lax.ppermute(x, axis, [(i, i ^ bit) for i in range(lax.axis_size(axis))])  14.2 us
    ppermute x2, starting transfers between devices, to_later_plane(): return lax.ppermute(x, 'layer', [(i, i + ring) for i in range(ring)])  5.49 us
    dot_general x1, matrix products, local(): lax.dot_general(latents, grad_after, (((1,), (0,)), ((), ())), preferred_...  4.4 us
    ppermute x2, waiting for transfers between devices, to_later_plane(): return lax.ppermute(x, 'layer', [(i, i + ring) for i in range(ring)])  4.05 us
    dot_general x2, matrix products, layer_terms(): lax.dot_general(weight, out_grad, (((2,), (1,)), ((), ())), preferred_ele...  3.62 us
  transfers between devices with their start and end apart: 25, of which 16 were waited for; matrix products, arithmetic and copies ran while one was open for 5% of the time, Pallas kernels for 0%

profile of v3, /device:TPU:2, one launch (start us, length us, event | category | flops | bytes accessed | tf_op | source)
XLA Modules:
  0.0 143.8 jit_solution(10857452319948482708)
XLA Ops:
  1.5 16.3 %all_to_all.15 = bf16[8,24,1024]{2,1,0:T(8,128)(2,1)S(1)} all-to-all(bf16[8,24,1024]{2,1,0:T(8,128)(2,1)S(1)} %broadcast_in_dim.83), channel_id=1, replica_groups={{0,2,4,6,8,10,12,14},{1,3,5,7,9,11,13,15},{16,18,20,22,24,26,28,30},{17..., dimensions={0} | all-to-all | bytes 786432 | tf_op jit(solution)/shard_map/all_to_all | solution.py:16
  17.8 1.7 %collective-permute-done = bf16[192,1024]{1,0:T(8,128)(2,1)S(1)} collective-permute-done((bf16[192,1024]{1,0:T(8,128)(2,1)S(1)}, bf16[192,1024]{1,0:T(8,128)(2,1)S(1)}, u32[]{:S(2)}, u32[]{:S(2)}) %collective-permute-start) | collective-permute-done | bytes 393248 | tf_op jit(solution)/shard_map/ppermute | solution.py:8
  20.0 2.0 %collective-permute-start.1 = (f32[192,256]{1,0:T(8,128)S(1)}, f32[192,256]{1,0:T(8,128)S(1)}, u32[]{:S(2)}, u32[]{:S(2)}) collective-permute-start(f32[192,256]{1,0:T(8,128)S(1)} %constant_dynamic-slice_fusion.4), channel_id=1, source_target_pairs={{0,16},{16,0},{32,48},{48,32},{64,80},{80,64},{96,112},{112,96},{1... | collective-permute-start | bytes 589832 | tf_op jit(solution)/shard_map/ppermute | solution.py:8
  22.7 4.5 %collective-permute-done.1 = f32[192,256]{1,0:T(8,128)S(1)} collective-permute-done((f32[192,256]{1,0:T(8,128)S(1)}, f32[192,256]{1,0:T(8,128)S(1)}, u32[]{:S(2)}, u32[]{:S(2)}) %collective-permute-start.1) | collective-permute-done | bytes 196640 | tf_op jit(solution)/shard_map/ppermute | solution.py:8
  27.2 5.8 %collective-permute-start.3 = (bf16[192,256]{1,0:T(8,128)(2,1)S(1)}, bf16[192,256]{1,0:T(8,128)(2,1)S(1)}, u32[]{:S(2)}, u32[]{:S(2)}) collective-permute-start(bf16[192,256]{1,0:T(8,128)(2,1)S(1)} %get-tuple-element.13), channel_id=1, source_target_pairs={{0,112},{16,0},{32,16},{48,32},{64,48},{80,64},{96,80},{112,96},{1... | collective-permute-start | bytes 294920 | tf_op jit(solution)/shard_map/ppermute | solution.py:25
  33.1 2.0 %collective-permute-done.3 = bf16[192,256]{1,0:T(8,128)(2,1)S(1)} collective-permute-done((bf16[192,256]{1,0:T(8,128)(2,1)S(1)}, bf16[192,256]{1,0:T(8,128)(2,1)S(1)}, u32[]{:S(2)}, u32[]{:S(2)}) %collective-permute-start.3) | collective-permute-done | bytes 98336 | tf_op jit(solution)/shard_map/ppermute | solution.py:25
  35.2 3.6 %collective-permute-start.5 = (bf16[192,256]{1,0:T(8,128)(2,1)S(1)}, bf16[192,256]{1,0:T(8,128)(2,1)S(1)}, u32[]{:S(2)}, u32[]{:S(2)}) collective-permute-start(bf16[192,256]{1,0:T(8,128)(2,1)S(1)} %collective-permute-done.3), channel_id=1, source_target_pairs={{0,112},{16,0},{32,16},{48,32},{64,48},{80,64},{96,80},{112,96},{1... | collective-permute-start | bytes 294920 | tf_op jit(solution)/shard_map/ppermute | solution.py:25
  38.8 2.2 %collective-permute-done.5 = bf16[192,256]{1,0:T(8,128)(2,1)S(1)} collective-permute-done((bf16[192,256]{1,0:T(8,128)(2,1)S(1)}, bf16[192,256]{1,0:T(8,128)(2,1)S(1)}, u32[]{:S(2)}, u32[]{:S(2)}) %collective-permute-start.5) | collective-permute-done | bytes 98336 | tf_op jit(solution)/shard_map/ppermute | solution.py:25
  41.0 3.6 %collective-permute-start.7 = (bf16[192,256]{1,0:T(8,128)(2,1)S(1)}, bf16[192,256]{1,0:T(8,128)(2,1)S(1)}, u32[]{:S(2)}, u32[]{:S(2)}) collective-permute-start(bf16[192,256]{1,0:T(8,128)(2,1)S(1)} %collective-permute-done.5), channel_id=1, source_target_pairs={{0,112},{16,0},{32,16},{48,32},{64,48},{80,64},{96,80},{112,96},{1... | collective-permute-start | bytes 294920 | tf_op jit(solution)/shard_map/ppermute | solution.py:25
  44.7 2.6 %collective-permute-start.10 = (bf16[5,192,256]{2,1,0:T(8,128)(2,1)S(1)}, bf16[5,192,256]{2,1,0:T(8,128)(2,1)S(1)}, u32[]{:S(2)}, u32[]{:S(2)}) collective-permute-start(bf16[5,192,256]{2,1,0:T(8,128)(2,1)S(1)} %get-tuple-element.26), channel_id=1, source_target_pairs={{0,128},{16,144},{32,160},{48,176},{64,192},{80,208},{96,224},{112... | collective-permute-start | bytes 1474568 | tf_op jit(solution)/shard_map/ppermute | solution.py:30
  47.3 3.3 %collective-permute-start.9 = (bf16[96,256]{1,0:T(8,128)(2,1)S(1)}, bf16[96,256]{1,0:T(8,128)(2,1)S(1)}, u32[]{:S(2)}, u32[]{:S(2)}) collective-permute-start(bf16[96,256]{1,0:T(8,128)(2,1)S(1)} %slice.114), channel_id=1, source_target_pairs={{0,112},{16,0},{32,16},{48,32},{64,48},{80,64},{96,80},{112,96},{1... | collective-permute-start | bytes 147464 | tf_op jit(solution)/shard_map/ppermute | solution.py:25
  52.4 3.6 %collective-permute-done.8 = bf16[96,256]{1,0:T(8,128)(2,1)S(1)} collective-permute-done((bf16[96,256]{1,0:T(8,128)(2,1)S(1)}, bf16[96,256]{1,0:T(8,128)(2,1)S(1)}, u32[]{:S(2)}, u32[]{:S(2)}) %collective-permute-start.8) | collective-permute-done | bytes 49184 | tf_op jit(solution)/shard_map/ppermute | solution.py:25
  56.0 2.9 %collective-permute-start.11 = (bf16[3,192,256]{2,1,0:T(8,128)(2,1)S(1)}, bf16[3,192,256]{2,1,0:T(8,128)(2,1)S(1)}, u32[]{:S(2)}, u32[]{:S(2)}) collective-permute-start(bf16[3,192,256]{2,1,0:T(8,128)(2,1)S(1)} %pad_maximum_fusion.4), channel_id=1, source_target_pairs={{0,128},{16,144},{32,160},{48,176},{64,192},{80,208},{96,224},{112... | collective-permute-start | bytes 884744 | tf_op jit(solution)/shard_map/ppermute | solution.py:30
  59.1 4.1 %collective-permute-done.11 = bf16[3,192,256]{2,1,0:T(8,128)(2,1)S(1)} collective-permute-done((bf16[3,192,256]{2,1,0:T(8,128)(2,1)S(1)}, bf16[3,192,256]{2,1,0:T(8,128)(2,1)S(1)}, u32[]{:S(2)}, u32[]{:S(2)}) %collective-permute-start.11) | collective-permute-done | bytes 294944 | tf_op jit(solution)/shard_map/ppermute | solution.py:30
  63.4 1.8 %convolution_bitcast_fusion = f32[384,1024]{1,0:T(8,128)S(1)} fusion(bf16[8,384,256]{2,1,0:T(8,128)(2,1)S(1)} %bitcast_select_fusion, bf16[8,256,1024]{2,1,0:T(8,128)(2,1)S(1)} %copy-done.2), kind=kOutput, calls=%fused_computation.8 | convolution fusion | flops 1610612736 | bytes 7340032 | tf_op jit(solution)/shard_map/dot_general | solution.py:158
  65.3 1.7 %collective-permute-done.12 = bf16[192,1024]{1,0:T(8,128)(2,1)S(1)} collective-permute-done((bf16[192,1024]{1,0:T(8,128)(2,1)S(1)}, bf16[192,1024]{1,0:T(8,128)(2,1)S(1)}, u32[]{:S(2)}, u32[]{:S(2)}) %collective-permute-start.12) | collective-permute-done | bytes 393248 | tf_op jit(solution)/shard_map/ppermute | solution.py:8
  67.2 13.6 %all_to_all.16 = bf16[8,24,1024]{2,1,0:T(8,128)(2,1)S(1)} all-to-all(bf16[8,24,1024]{2,1,0:T(8,128)(2,1)S(1)} %bitcast.96), channel_id=1, replica_groups={{0,2,4,6,8,10,12,14},{1,3,5,7,9,11,13,15},{16,18,20,22,24,26,28,30},{17..., dimensions={0} | all-to-all | bytes 786432 | tf_op jit(solution)/shard_map/all_to_all | solution.py:16
  80.9 12.4 %all_to_all.17 = bf16[8,24,1024]{2,1,0:T(8,128)(2,1)S(1)} all-to-all(bf16[8,24,1024]{2,1,0:T(8,128)(2,1)S(1)} %broadcast_in_dim.97), channel_id=1, replica_groups={{0,2,4,6,8,10,12,14},{1,3,5,7,9,11,13,15},{16,18,20,22,24,26,28,30},{17..., dimensions={0} | all-to-all | bytes 786432 | tf_op jit(solution)/shard_map/all_to_all | solution.py:16
  93.4 1.6 %collective-permute-done.13 = bf16[192,1024]{1,0:T(8,128)(2,1)S(1)} collective-permute-done((bf16[192,1024]{1,0:T(8,128)(2,1)S(1)}, bf16[192,1024]{1,0:T(8,128)(2,1)S(1)}, u32[]{:S(2)}, u32[]{:S(2)}) %collective-permute-start.13) | collective-permute-done | bytes 393248 | tf_op jit(solution)/shard_map/ppermute | solution.py:8
  95.1 2.6 %fusion.8 = bf16[4,384,256]{2,1,0:T(8,128)(2,1)S(1)} fusion(bf16[8,256,1024]{2,1,0:T(8,128)(2,1)} %param.9, pred[4]{0:T(512)(128)(4,1)S(1)} %get-tuple-element.35, bf16[192,1024]{1,0:T(8,128)(2,1)S(1)} %collective-permute-done.13, bf16[192,1024]{1,0:T(8,128)(2,1)S(1)} %bitcast.95), kind=kOutput, calls=%fused_computation.9 | convolution fusion | flops 807665664 | bytes 3670020 | tf_op jit(solution)/shard_map/dot_general | solution.py:76
  100.7 4.4 %convolution_convert_fusion = bf16[8,256,1024]{2,1,0:T(8,128)(2,1)} fusion(bf16[8,384,256]{2,1,0:T(8,128)(2,1)S(1)} %bitcast_select_fusion, bf16[384,1024]{1,0:T(8,128)(2,1)S(1)} %pad_maximum_fusion.1), kind=kOutput, calls=%fused_computation | convolution fusion | flops 1612709888 | bytes 6553600 | tf_op jit(solution)/shard_map/dot_general | solution.py:171
  106.2 3.4 %collective-permute-done.14 = bf16[3,192,256]{2,1,0:T(8,128)(2,1)S(1)} collective-permute-done((bf16[3,192,256]{2,1,0:T(8,128)(2,1)S(1)}, bf16[3,192,256]{2,1,0:T(8,128)(2,1)S(1)}, u32[]{:S(2)}, u32[]{:S(2)}) %collective-permute-start.14) | collective-permute-done | bytes 294944 | tf_op jit(solution)/shard_map/ppermute | solution.py:35
  109.8 3.2 %collective-permute-start.20 = (bf16[96,256]{1,0:T(8,128)(2,1)S(1)}, bf16[96,256]{1,0:T(8,128)(2,1)S(1)}, u32[]{:S(2)}, u32[]{:S(2)}) collective-permute-start(bf16[96,256]{1,0:T(8,128)(2,1)S(1)} %get-tuple-element.25), channel_id=1, source_target_pairs={{0,112},{16,0},{32,16},{48,32},{64,48},{80,64},{96,80},{112,96},{1... | collective-permute-start | bytes 147464 | tf_op jit(solution)/shard_map/ppermute | solution.py:25
  113.0 2.1 %collective-permute-done.16 = bf16[96,256]{1,0:T(8,128)(2,1)S(1)} collective-permute-done((bf16[96,256]{1,0:T(8,128)(2,1)S(1)}, bf16[96,256]{1,0:T(8,128)(2,1)S(1)}, u32[]{:S(2)}, u32[]{:S(2)}) %collective-permute-start.16) | collective-permute-done | bytes 49184 | tf_op jit(solution)/shard_map/ppermute | solution.py:25
  115.2 3.3 %collective-permute-start.21 = (bf16[192,256]{1,0:T(8,128)(2,1)S(1)}, bf16[192,256]{1,0:T(8,128)(2,1)S(1)}, u32[]{:S(2)}, u32[]{:S(2)}) collective-permute-start(bf16[192,256]{1,0:T(8,128)(2,1)S(1)} %get-tuple-element.17), channel_id=1, source_target_pairs={{0,112},{16,0},{32,16},{48,32},{64,48},{80,64},{96,80},{112,96},{1... | collective-permute-start | bytes 294920 | tf_op jit(solution)/shard_map/ppermute | solution.py:25
  118.5 2.5 %collective-permute-done.17 = bf16[192,256]{1,0:T(8,128)(2,1)S(1)} collective-permute-done((bf16[192,256]{1,0:T(8,128)(2,1)S(1)}, bf16[192,256]{1,0:T(8,128)(2,1)S(1)}, u32[]{:S(2)}, u32[]{:S(2)}) %collective-permute-start.17) | collective-permute-done | bytes 98336 | tf_op jit(solution)/shard_map/ppermute | solution.py:25
  121.2 5.8 %collective-permute-done.18 = bf16[192,256]{1,0:T(8,128)(2,1)S(1)} collective-permute-done((bf16[192,256]{1,0:T(8,128)(2,1)S(1)}, bf16[192,256]{1,0:T(8,128)(2,1)S(1)}, u32[]{:S(2)}, u32[]{:S(2)}) %collective-permute-start.18) | collective-permute-done | bytes 98336 | tf_op jit(solution)/shard_map/ppermute | solution.py:25
  127.1 2.2 %collective-permute-start.22 = (bf16[192,256]{1,0:T(8,128)(2,1)S(1)}, bf16[192,256]{1,0:T(8,128)(2,1)S(1)}, u32[]{:S(2)}, u32[]{:S(2)}) collective-permute-start(bf16[192,256]{1,0:T(8,128)(2,1)S(1)} %get-tuple-element.15), channel_id=1, source_target_pairs={{0,112},{16,0},{32,16},{48,32},{64,48},{80,64},{96,80},{112,96},{1... | collective-permute-start | bytes 294920 | tf_op jit(solution)/shard_map/ppermute | solution.py:25
  129.3 2.6 %collective-permute-done.22 = bf16[192,256]{1,0:T(8,128)(2,1)S(1)} collective-permute-done((bf16[192,256]{1,0:T(8,128)(2,1)S(1)}, bf16[192,256]{1,0:T(8,128)(2,1)S(1)}, u32[]{:S(2)}, u32[]{:S(2)}) %collective-permute-start.22) | collective-permute-done | bytes 98336 | tf_op jit(solution)/shard_map/ppermute | solution.py:25
  132.0 3.3 %collective-permute-start.23 = (bf16[192,256]{1,0:T(8,128)(2,1)S(1)}, bf16[192,256]{1,0:T(8,128)(2,1)S(1)}, u32[]{:S(2)}, u32[]{:S(2)}) collective-permute-start(bf16[192,256]{1,0:T(8,128)(2,1)S(1)} %fusion.28), channel_id=1, source_target_pairs={{0,112},{16,0},{32,16},{48,32},{64,48},{80,64},{96,80},{112,96},{1... | collective-permute-start | bytes 294920 | tf_op jit(solution)/shard_map/ppermute | solution.py:25
  135.3 2.2 %collective-permute-done.23 = bf16[192,256]{1,0:T(8,128)(2,1)S(1)} collective-permute-done((bf16[192,256]{1,0:T(8,128)(2,1)S(1)}, bf16[192,256]{1,0:T(8,128)(2,1)S(1)}, u32[]{:S(2)}, u32[]{:S(2)}) %collective-permute-start.23) | collective-permute-done | bytes 98336 | tf_op jit(solution)/shard_map/ppermute | solution.py:25
  137.7 4.6 %collective-permute-done.24 = bf16[192,256]{1,0:T(8,128)(2,1)S(1)} collective-permute-done((bf16[192,256]{1,0:T(8,128)(2,1)S(1)}, bf16[192,256]{1,0:T(8,128)(2,1)S(1)}, u32[]{:S(2)}, u32[]{:S(2)}) %collective-permute-start.24) | collective-permute-done | bytes 98336 | tf_op jit(solution)/shard_map/ppermute | solution.py:8
  (88 shorter events, 11.1 us)
Async XLA Ops:
  0.6 18.9 %copy-start = (bf16[1024,256]{1,0:T(8,128)(2,1)S(1)}, bf16[1024,256]{1,0:T(8,128)(2,1)}, u32[]{:S(2)}) copy-start(bf16[1024,256]{1,0:T(8,128)(2,1)} %param.7) | copy-start | bytes 1572868
  17.8 1.7 %collective-permute-start = (bf16[192,1024]{1,0:T(8,128)(2,1)S(1)}, bf16[192,1024]{1,0:T(8,128)(2,1)S(1)}, u32[]{:S(2)}, u32[]{:S(2)}) collective-permute-start(bf16[192,1024]{1,0:T(8,128)(2,1)S(1)} %bitcast.110), channel_id=1, source_target_pairs={{0,1},{1,0},{2,3},{3,2},{4,5},{5,4},{6,7},{7,6},{8,9},{9,8},{10,11... | collective-permute-start | bytes 1179656 | tf_op jit(solution)/shard_map/ppermute | solution.py:8
  19.5 7.6 %copy-start.4 = (bf16[192,1024]{1,0:T(8,128)(2,1)}, bf16[192,1024]{1,0:T(8,128)(2,1)S(1)}, u32[]{:S(2)}) copy-start(bf16[192,1024]{1,0:T(8,128)(2,1)S(1)} %collective-permute-done) | copy-start | bytes 1179652
  20.0 7.2 %collective-permute-start.1 = (f32[192,256]{1,0:T(8,128)S(1)}, f32[192,256]{1,0:T(8,128)S(1)}, u32[]{:S(2)}, u32[]{:S(2)}) collective-permute-start(f32[192,256]{1,0:T(8,128)S(1)} %constant_dynamic-slice_fusion.4), channel_id=1, source_target_pairs={{0,16},{16,0},{32,48},{48,32},{64,80},{80,64},{96,112},{112,96},{1... | collective-permute-start | bytes 589832 | tf_op jit(solution)/shard_map/ppermute | solution.py:8
  27.2 8.0 %collective-permute-start.3 = (bf16[192,256]{1,0:T(8,128)(2,1)S(1)}, bf16[192,256]{1,0:T(8,128)(2,1)S(1)}, u32[]{:S(2)}, u32[]{:S(2)}) collective-permute-start(bf16[192,256]{1,0:T(8,128)(2,1)S(1)} %get-tuple-element.13), channel_id=1, source_target_pairs={{0,112},{16,0},{32,16},{48,32},{64,48},{80,64},{96,80},{112,96},{1... | collective-permute-start | bytes 294920 | tf_op jit(solution)/shard_map/ppermute | solution.py:25
  33.0 5.8 %collective-permute-start.2 = (bf16[192,256]{1,0:T(8,128)(2,1)S(1)}, bf16[192,256]{1,0:T(8,128)(2,1)S(1)}, u32[]{:S(2)}, u32[]{:S(2)}) collective-permute-start(bf16[192,256]{1,0:T(8,128)(2,1)S(1)} %get-tuple-element.13), channel_id=1, source_target_pairs={{0,16},{16,32},{32,48},{48,64},{64,80},{80,96},{96,112},{112,0},{1... | collective-permute-start | bytes 294920 | tf_op jit(solution)/shard_map/ppermute | solution.py:25
  35.2 5.8 %collective-permute-start.5 = (bf16[192,256]{1,0:T(8,128)(2,1)S(1)}, bf16[192,256]{1,0:T(8,128)(2,1)S(1)}, u32[]{:S(2)}, u32[]{:S(2)}) collective-permute-start(bf16[192,256]{1,0:T(8,128)(2,1)S(1)} %collective-permute-done.3), channel_id=1, source_target_pairs={{0,112},{16,0},{32,16},{48,32},{64,48},{80,64},{96,80},{112,96},{1... | collective-permute-start | bytes 294920 | tf_op jit(solution)/shard_map/ppermute | solution.py:25
  38.8 5.8 %collective-permute-start.4 = (bf16[192,256]{1,0:T(8,128)(2,1)S(1)}, bf16[192,256]{1,0:T(8,128)(2,1)S(1)}, u32[]{:S(2)}, u32[]{:S(2)}) collective-permute-start(bf16[192,256]{1,0:T(8,128)(2,1)S(1)} %collective-permute-done.2), channel_id=1, source_target_pairs={{0,16},{16,32},{32,48},{48,64},{64,80},{80,96},{96,112},{112,0},{1... | collective-permute-start | bytes 294920 | tf_op jit(solution)/shard_map/ppermute | solution.py:25
  41.0 6.3 %collective-permute-start.7 = (bf16[192,256]{1,0:T(8,128)(2,1)S(1)}, bf16[192,256]{1,0:T(8,128)(2,1)S(1)}, u32[]{:S(2)}, u32[]{:S(2)}) collective-permute-start(bf16[192,256]{1,0:T(8,128)(2,1)S(1)} %collective-permute-done.5), channel_id=1, source_target_pairs={{0,112},{16,0},{32,16},{48,32},{64,48},{80,64},{96,80},{112,96},{1... | collective-permute-start | bytes 294920 | tf_op jit(solution)/shard_map/ppermute | solution.py:25
  44.6 6.0 %collective-permute-start.6 = (bf16[192,256]{1,0:T(8,128)(2,1)S(1)}, bf16[192,256]{1,0:T(8,128)(2,1)S(1)}, u32[]{:S(2)}, u32[]{:S(2)}) collective-permute-start(bf16[192,256]{1,0:T(8,128)(2,1)S(1)} %collective-permute-done.4), channel_id=1, source_target_pairs={{0,16},{16,32},{32,48},{48,64},{64,80},{80,96},{96,112},{112,0},{1... | collective-permute-start | bytes 294920 | tf_op jit(solution)/shard_map/ppermute | solution.py:25
  44.7 14.3 %collective-permute-start.10 = (bf16[5,192,256]{2,1,0:T(8,128)(2,1)S(1)}, bf16[5,192,256]{2,1,0:T(8,128)(2,1)S(1)}, u32[]{:S(2)}, u32[]{:S(2)}) collective-permute-start(bf16[5,192,256]{2,1,0:T(8,128)(2,1)S(1)} %get-tuple-element.26), channel_id=1, source_target_pairs={{0,128},{16,144},{32,160},{48,176},{64,192},{80,208},{96,224},{112... | collective-permute-start | bytes 1474568 | tf_op jit(solution)/shard_map/ppermute | solution.py:30
  47.3 5.1 %collective-permute-start.9 = (bf16[96,256]{1,0:T(8,128)(2,1)S(1)}, bf16[96,256]{1,0:T(8,128)(2,1)S(1)}, u32[]{:S(2)}, u32[]{:S(2)}) collective-permute-start(bf16[96,256]{1,0:T(8,128)(2,1)S(1)} %slice.114), channel_id=1, source_target_pairs={{0,112},{16,0},{32,16},{48,32},{64,48},{80,64},{96,80},{112,96},{1... | collective-permute-start | bytes 147464 | tf_op jit(solution)/shard_map/ppermute | solution.py:25
  50.6 5.4 %collective-permute-start.8 = (bf16[96,256]{1,0:T(8,128)(2,1)S(1)}, bf16[96,256]{1,0:T(8,128)(2,1)S(1)}, u32[]{:S(2)}, u32[]{:S(2)}) collective-permute-start(bf16[96,256]{1,0:T(8,128)(2,1)S(1)} %slice.113), channel_id=1, source_target_pairs={{0,16},{16,32},{32,48},{48,64},{64,80},{80,96},{96,112},{112,0},{1... | collective-permute-start | bytes 147464 | tf_op jit(solution)/shard_map/ppermute | solution.py:25
  56.0 7.1 %collective-permute-start.11 = (bf16[3,192,256]{2,1,0:T(8,128)(2,1)S(1)}, bf16[3,192,256]{2,1,0:T(8,128)(2,1)S(1)}, u32[]{:S(2)}, u32[]{:S(2)}) collective-permute-start(bf16[3,192,256]{2,1,0:T(8,128)(2,1)S(1)} %pad_maximum_fusion.4), channel_id=1, source_target_pairs={{0,128},{16,144},{32,160},{48,176},{64,192},{80,208},{96,224},{112... | collective-permute-start | bytes 884744 | tf_op jit(solution)/shard_map/ppermute | solution.py:30
  59.0 4.4 %copy-start.2 = (bf16[8,256,1024]{2,1,0:T(8,128)(2,1)S(1)}, bf16[8,256,1024]{2,1,0:T(8,128)(2,1)}, u32[]{:S(2)}) copy-start(bf16[8,256,1024]{2,1,0:T(8,128)(2,1)} %param.9) | copy-start | bytes 12582916
  65.2 15.6 %copy-start.1 = (bf16[24,1024]{1,0:T(8,128)(2,1)S(1)}, bf16[24,1024]{1,0:T(8,128)(2,1)}, u32[]{:S(2)}) copy-start(bf16[24,1024]{1,0:T(8,128)(2,1)} %param.6) | copy-start | bytes 147460
  65.2 1.8 %collective-permute-start.12 = (bf16[192,1024]{1,0:T(8,128)(2,1)S(1)}, bf16[192,1024]{1,0:T(8,128)(2,1)S(1)}, u32[]{:S(2)}, u32[]{:S(2)}) collective-permute-start(bf16[192,1024]{1,0:T(8,128)(2,1)S(1)} %slice.170), channel_id=1, source_target_pairs={{0,1},{1,0},{2,3},{3,2},{4,5},{5,4},{6,7},{7,6},{8,9},{9,8},{10,11... | collective-permute-start | bytes 1179656 | tf_op jit(solution)/shard_map/ppermute | solution.py:8
  93.3 1.7 %collective-permute-start.13 = (bf16[192,1024]{1,0:T(8,128)(2,1)S(1)}, bf16[192,1024]{1,0:T(8,128)(2,1)S(1)}, u32[]{:S(2)}, u32[]{:S(2)}) collective-permute-start(bf16[192,1024]{1,0:T(8,128)(2,1)S(1)} %bitcast.93), channel_id=1, source_target_pairs={{0,1},{1,0},{2,3},{3,2},{4,5},{5,4},{6,7},{7,6},{8,9},{9,8},{10,11... | collective-permute-start | bytes 1179656 | tf_op jit(solution)/shard_map/ppermute | solution.py:8
  97.9 11.7 %collective-permute-start.14 = (bf16[3,192,256]{2,1,0:T(8,128)(2,1)S(1)}, bf16[3,192,256]{2,1,0:T(8,128)(2,1)S(1)}, u32[]{:S(2)}, u32[]{:S(2)}) collective-permute-start(bf16[3,192,256]{2,1,0:T(8,128)(2,1)S(1)} %pad_maximum_fusion.5), channel_id=1, source_target_pairs={{128,0},{144,16},{160,32},{176,48},{192,64},{208,80},{224,96},{240... | collective-permute-start | bytes 884744 | tf_op jit(solution)/shard_map/ppermute | solution.py:35
  99.2 6.0 %copy-start.3 = (bf16[8,256,1024]{2,1,0:T(8,128)(2,1)S(1)}, bf16[8,256,1024]{2,1,0:T(8,128)(2,1)}, u32[]{:S(2)}) copy-start(bf16[8,256,1024]{2,1,0:T(8,128)(2,1)} %param.9) | copy-start | bytes 12582916
  99.2 21.8 %collective-permute-start.15 = (bf16[5,192,256]{2,1,0:T(8,128)(2,1)S(1)}, bf16[5,192,256]{2,1,0:T(8,128)(2,1)S(1)}, u32[]{:S(2)}, u32[]{:S(2)}) collective-permute-start(bf16[5,192,256]{2,1,0:T(8,128)(2,1)S(1)} %get-tuple-element.18), channel_id=1, source_target_pairs={{128,0},{144,16},{160,32},{176,48},{192,64},{208,80},{224,96},{240... | collective-permute-start | bytes 1474568 | tf_op jit(solution)/shard_map/ppermute | solution.py:35
  109.7 5.4 %collective-permute-start.16 = (bf16[96,256]{1,0:T(8,128)(2,1)S(1)}, bf16[96,256]{1,0:T(8,128)(2,1)S(1)}, u32[]{:S(2)}, u32[]{:S(2)}) collective-permute-start(bf16[96,256]{1,0:T(8,128)(2,1)S(1)} %get-tuple-element.24), channel_id=1, source_target_pairs={{0,16},{16,32},{32,48},{48,64},{64,80},{80,96},{96,112},{112,0},{1... | collective-permute-start | bytes 147464 | tf_op jit(solution)/shard_map/ppermute | solution.py:25
  109.7 32.6 %copy-start.5 = (bf16[192,1024]{1,0:T(8,128)(2,1)S(1)}, bf16[192,1024]{1,0:T(8,128)(2,1)}, u32[]{:S(2)}) copy-start(bf16[192,1024]{1,0:T(8,128)(2,1)} %copy-done.4) | copy-start | bytes 1179652
  109.8 5.3 %collective-permute-start.20 = (bf16[96,256]{1,0:T(8,128)(2,1)S(1)}, bf16[96,256]{1,0:T(8,128)(2,1)S(1)}, u32[]{:S(2)}, u32[]{:S(2)}) collective-permute-start(bf16[96,256]{1,0:T(8,128)(2,1)S(1)} %get-tuple-element.25), channel_id=1, source_target_pairs={{0,112},{16,0},{32,16},{48,32},{64,48},{80,64},{96,80},{112,96},{1... | collective-permute-start | bytes 147464 | tf_op jit(solution)/shard_map/ppermute | solution.py:25
  115.1 5.9 %collective-permute-start.17 = (bf16[192,256]{1,0:T(8,128)(2,1)S(1)}, bf16[192,256]{1,0:T(8,128)(2,1)S(1)}, u32[]{:S(2)}, u32[]{:S(2)}) collective-permute-start(bf16[192,256]{1,0:T(8,128)(2,1)S(1)} %get-tuple-element.16), channel_id=1, source_target_pairs={{0,16},{16,32},{32,48},{48,64},{64,80},{80,96},{96,112},{112,0},{1... | collective-permute-start | bytes 294920 | tf_op jit(solution)/shard_map/ppermute | solution.py:25
  115.2 6.0 %collective-permute-start.21 = (bf16[192,256]{1,0:T(8,128)(2,1)S(1)}, bf16[192,256]{1,0:T(8,128)(2,1)S(1)}, u32[]{:S(2)}, u32[]{:S(2)}) collective-permute-start(bf16[192,256]{1,0:T(8,128)(2,1)S(1)} %get-tuple-element.17), channel_id=1, source_target_pairs={{0,112},{16,0},{32,16},{48,32},{64,48},{80,64},{96,80},{112,96},{1... | collective-permute-start | bytes 294920 | tf_op jit(solution)/shard_map/ppermute | solution.py:25
  121.1 5.9 %collective-permute-start.18 = (bf16[192,256]{1,0:T(8,128)(2,1)S(1)}, bf16[192,256]{1,0:T(8,128)(2,1)S(1)}, u32[]{:S(2)}, u32[]{:S(2)}) collective-permute-start(bf16[192,256]{1,0:T(8,128)(2,1)S(1)} %fusion.30), channel_id=1, source_target_pairs={{0,16},{16,32},{32,48},{48,64},{64,80},{80,96},{96,112},{112,0},{1... | collective-permute-start | bytes 294920 | tf_op jit(solution)/shard_map/ppermute | solution.py:25
  127.1 4.9 %collective-permute-start.22 = (bf16[192,256]{1,0:T(8,128)(2,1)S(1)}, bf16[192,256]{1,0:T(8,128)(2,1)S(1)}, u32[]{:S(2)}, u32[]{:S(2)}) collective-permute-start(bf16[192,256]{1,0:T(8,128)(2,1)S(1)} %get-tuple-element.15), channel_id=1, source_target_pairs={{0,112},{16,0},{32,16},{48,32},{64,48},{80,64},{96,80},{112,96},{1... | collective-permute-start | bytes 294920 | tf_op jit(solution)/shard_map/ppermute | solution.py:25
  129.3 6.0 %collective-permute-start.19 = (bf16[192,256]{1,0:T(8,128)(2,1)S(1)}, bf16[192,256]{1,0:T(8,128)(2,1)S(1)}, u32[]{:S(2)}, u32[]{:S(2)}) collective-permute-start(bf16[192,256]{1,0:T(8,128)(2,1)S(1)} %get-tuple-element.14), channel_id=1, source_target_pairs={{0,16},{16,32},{32,48},{48,64},{64,80},{80,96},{96,112},{112,0},{1... | collective-permute-start | bytes 294920 | tf_op jit(solution)/shard_map/ppermute | solution.py:25
  132.0 5.5 %collective-permute-start.23 = (bf16[192,256]{1,0:T(8,128)(2,1)S(1)}, bf16[192,256]{1,0:T(8,128)(2,1)S(1)}, u32[]{:S(2)}, u32[]{:S(2)}) collective-permute-start(bf16[192,256]{1,0:T(8,128)(2,1)S(1)} %fusion.28), channel_id=1, source_target_pairs={{0,112},{16,0},{32,16},{48,32},{64,48},{80,64},{96,80},{112,96},{1... | collective-permute-start | bytes 294920 | tf_op jit(solution)/shard_map/ppermute | solution.py:25
  137.6 4.7 %collective-permute-start.24 = (bf16[192,256]{1,0:T(8,128)(2,1)S(1)}, bf16[192,256]{1,0:T(8,128)(2,1)S(1)}, u32[]{:S(2)}, u32[]{:S(2)}) collective-permute-start(bf16[192,256]{1,0:T(8,128)(2,1)S(1)} %fusion.34), channel_id=1, source_target_pairs={{0,16},{16,0},{32,48},{48,32},{64,80},{80,64},{96,112},{112,96},{1... | collective-permute-start | bytes 294920 | tf_op jit(solution)/shard_map/ppermute | solution.py:8

commit v4 on v3

--- a/solution.py
+++ b/solution.py
@@ -40,7 +40,6 @@
 
 
 def latents_of_all(own, plane, spot, ring):
-    far = ring // 2
     half = own.shape[0] // 2
     stack = jnp.zeros((2 * ring, *own.shape), own.dtype)
 
@@ -48,26 +47,26 @@
         place = which * ring + (spot + distance) % ring
         return lax.dynamic_update_index_in_dim(stack, block, place, 0)
 
-    found = [(own, 0)]
-    up = down = own
-    bundles = []
-    for step in range(1, far):
-        up, down = along_ring(up, 1), along_ring(down, ring - 1)
-        found += [(up, ring - step), (down, step)]
-        if step == far // 2:
-            crossed = to_later_plane(jnp.stack([block for block, _ in found], 0))
-            bundles.append((crossed, [distance for _, distance in found]))
-    ends = jnp.concatenate(
-        [along_ring(up[:half], 1), along_ring(down[half:], ring - 1)], 0
-    )
-    found.append((ends, far))
-    sent = len(bundles[0][1])
-    crossed = to_later_plane(jnp.stack([block for block, _ in found[sent:]], 0))
-    bundles.append((crossed, [distance for _, distance in found[sent:]]))
-    for block, distance in found:
-        stack = put(stack, block, plane, distance)
-    for crossed, distances in bundles:
-        for at, distance in enumerate(distances):
+    near = {0: own}
+    for distance in (1, -1, 2, -2):
+        near[distance] = along_ring(own, -distance)
+    behind = along_ring(jnp.concatenate([near[-1], near[-2][:half]], 0), 2)
+    ahead = along_ring(jnp.concatenate([near[1], near[2][half:]], 0), -2)
+    near_order = list(near)
+    near_crossed = to_later_plane(jnp.stack([near[d] for d in near_order], 0))
+    far = {
+        -3: behind[: 2 * half],
+        3: ahead[: 2 * half],
+        4: jnp.concatenate([behind[2 * half :], ahead[2 * half :]], 0),
+    }
+    far_order = list(far)
+    far_crossed = to_later_plane(jnp.stack([far[d] for d in far_order], 0))
+    for blocks, crossed, order in (
+        (near, near_crossed, near_order),
+        (far, far_crossed, far_order),
+    ):
+        for at, distance in enumerate(order):
+            stack = put(stack, blocks[distance], plane, distance)
             stack = put(stack, crossed[at], 1 - plane, distance)
     return stack
 
@@ -80,32 +79,36 @@
 
 
 def terms_to_layers(lower, own, spot, ring, tie):
-    far = ring // 2
     half = own.shape[1] // 2
 
     def at(blocks, distance):
         return lax.dynamic_index_in_dim(blocks, (spot + distance) % ring, 0, keepdims=False)
 
-    first = [far, far - 1, ring - far + 1]
-    second = [d for d in range(ring) if d not in first]
-    crossed = {}
+    first, second = (4, 3, -3), (1, -1, 2, -2, 0)
     early = to_earlier_plane(jnp.stack([at(lower, d) for d in first], 0))
     late = to_earlier_plane(jnp.stack([at(lower, d) for d in second], 0))
     early, tie, own = lax.optimization_barrier((early, tie, own))
-    for bundle, distances in ((early, first), (late, second)):
-        for k, d in enumerate(distances):
-            crossed[d] = bundle[k]
-    ends = added(at(own, far), crossed[far])
-    up, down = along_ring(ends[:half], 1), along_ring(ends[half:], ring - 1)
-    for step in range(far - 1, 0, -1):
-        back = ring - step
-        if step == far - 1:
-            up = jnp.concatenate([up, jnp.zeros_like(up)], 0)
-            down = jnp.concatenate([jnp.zeros_like(down), down], 0)
-        up = added(at(own, step), crossed[step], up)
-        down = added(at(own, back), crossed[back], down)
-        up, down = along_ring(up, 1), along_ring(down, ring - 1)
-    total = sum(x.astype(jnp.float32) for x in (at(own, 0), crossed[0], up, down))
+    crossed = {d: early[k] for k, d in enumerate(first)}
+    ends = added(at(own, 4), crossed[4])
+    behind = along_ring(
+        jnp.concatenate([added(at(own, 3), crossed[3]), ends[:half]], 0), 2
+    )
+    ahead = along_ring(
+        jnp.concatenate([added(at(own, -3), crossed[-3]), ends[half:]], 0), -2
+    )
+    crossed = {d: late[k] for k, d in enumerate(second)}
+    blank = jnp.zeros_like(ends[:half])
+    arrived = [
+        along_ring(added(at(own, 1), crossed[1], behind[: 2 * half]), 1),
+        along_ring(added(at(own, -1), crossed[-1], ahead[: 2 * half]), -1),
+        along_ring(
+            added(at(own, 2), crossed[2], jnp.concatenate([behind[2 * half :], blank], 0)), 2
+        ),
+        along_ring(
+            added(at(own, -2), crossed[-2], jnp.concatenate([blank, ahead[2 * half :]], 0)), -2
+        ),
+    ]
+    total = sum(x.astype(jnp.float32) for x in (at(own, 0), crossed[0], *arrived))
     return total, tie
 
 

time: 144 us -> 139 us (0.965)
  waiting for transfers between devices: 46.3 us -> 42.9 us
  starting transfers between devices: 39.2 us -> 36.8 us
    ppermute x16 -> x12, starting transfers between devices: 28.7 us -> 24 us  [along_ring(): return lax.ppermute(x, 'layer', pairs)]
    ppermute x16 -> x12, waiting for transfers between devices: 24.7 us -> 20.9 us  [along_ring(): return lax.ppermute(x, 'layer', pairs)]
    ppermute x2, waiting for transfers between devices: 4.05 us -> 6.61 us  [to_later_plane(): return lax.ppermute(x, 'layer', [(i, i + ring) for i in range(ring)])]
    ppermute x5, starting transfers between devices: 2.2 us -> 4.49 us  [from_partner(): lax.ppermute(x, axis, [(i, i ^ bit) for i in range(lax.axis_size(axis))])]
    ppermute x5, waiting for transfers between devices: 14.2 us -> 12.2 us  [from_partner(): lax.ppermute(x, axis, [(i, i ^ bit) for i in range(lax.axis_size(axis))])]
  transfers between devices with their start and end apart: 25 -> 21, of which waited for: 16 -> 16; matrix products, arithmetic and copies ran while one was open for 5% -> 5% of each run, Pallas kernels for 0% -> 0%
where the time goes in v4:
time: 139 us; the launch traced here: 138 us
  waiting for transfers between devices  42.9 us (31%)
  blocking collectives  42.3 us (30%)
  starting transfers between devices  36.8 us (26%)
  matrix products  11.6 us (8%)
  local copies, waits for them, and re-layouts  2.34 us (2%)
    all_to_all x3, blocking collectives, exchanged(): lax.all_to_all(parts, axis, split_axis=0, concat_axis=0, tiled=True, axis...  42.3 us
    ppermute x12, starting transfers between devices, along_ring(): return lax.ppermute(x, 'layer', pairs)  24 us
    ppermute x12, waiting for transfers between devices, along_ring(): return lax.ppermute(x, 'layer', pairs)  20.9 us
    ppermute x5, waiting for transfers between devices, from_partner(): lax.ppermute(x, axis, [(i, i ^ bit) for i in range(lax.axis_size(axis))])  12.2 us
    ppermute x2, waiting for transfers between devices, to_later_plane(): return lax.ppermute(x, 'layer', [(i, i + ring) for i in range(ring)])  6.61 us
    ppermute x2, starting transfers between devices, to_later_plane(): return lax.ppermute(x, 'layer', [(i, i + ring) for i in range(ring)])  5.21 us
    ppermute x5, starting transfers between devices, from_partner(): lax.ppermute(x, axis, [(i, i ^ bit) for i in range(lax.axis_size(axis))])  4.49 us
    dot_general x1, matrix products, local(): lax.dot_general(latents, grad_after, (((1,), (0,)), ((), ())), preferred_...  4.4 us
  transfers between devices with their start and end apart: 21, of which 16 were waited for; matrix products, arithmetic and copies ran while one was open for 5% of the time, Pallas kernels for 0%

profile of v4, /device:TPU:2, one launch (start us, length us, event | category | flops | bytes accessed | tf_op | source)
XLA Modules:
  0.0 138.0 jit_solution(16183288636973946539)
XLA Ops:
  1.5 16.3 %all_to_all.15 = bf16[8,24,1024]{2,1,0:T(8,128)(2,1)S(1)} all-to-all(bf16[8,24,1024]{2,1,0:T(8,128)(2,1)S(1)} %broadcast_in_dim.72), channel_id=1, replica_groups={{0,2,4,6,8,10,12,14},{1,3,5,7,9,11,13,15},{16,18,20,22,24,26,28,30},{17..., dimensions={0} | all-to-all | bytes 786432 | tf_op jit(solution)/shard_map/all_to_all | solution.py:16
  17.8 1.7 %collective-permute-done = bf16[192,1024]{1,0:T(8,128)(2,1)S(1)} collective-permute-done((bf16[192,1024]{1,0:T(8,128)(2,1)S(1)}, bf16[192,1024]{1,0:T(8,128)(2,1)S(1)}, u32[]{:S(2)}, u32[]{:S(2)}) %collective-permute-start) | collective-permute-done | bytes 393248 | tf_op jit(solution)/shard_map/ppermute | solution.py:8
  20.0 2.0 %collective-permute-start.1 = (f32[192,256]{1,0:T(8,128)S(1)}, f32[192,256]{1,0:T(8,128)S(1)}, u32[]{:S(2)}, u32[]{:S(2)}) collective-permute-start(f32[192,256]{1,0:T(8,128)S(1)} %constant_dynamic-slice_fusion.4), channel_id=1, source_target_pairs={{0,16},{16,0},{32,48},{48,32},{64,80},{80,64},{96,112},{112,96},{1... | collective-permute-start | bytes 589832 | tf_op jit(solution)/shard_map/ppermute | solution.py:8
  22.7 4.5 %collective-permute-done.1 = f32[192,256]{1,0:T(8,128)S(1)} collective-permute-done((f32[192,256]{1,0:T(8,128)S(1)}, f32[192,256]{1,0:T(8,128)S(1)}, u32[]{:S(2)}, u32[]{:S(2)}) %collective-permute-start.1) | collective-permute-done | bytes 196640 | tf_op jit(solution)/shard_map/ppermute | solution.py:8
  27.2 3.3 %collective-permute-start.5 = (bf16[192,256]{1,0:T(8,128)(2,1)S(1)}, bf16[192,256]{1,0:T(8,128)(2,1)S(1)}, u32[]{:S(2)}, u32[]{:S(2)}) collective-permute-start(bf16[192,256]{1,0:T(8,128)(2,1)S(1)} %get-tuple-element.13), channel_id=1, source_target_pairs={{0,32},{16,48},{32,64},{48,80},{64,96},{80,112},{96,0},{112,16},{1... | collective-permute-start | bytes 294920 | tf_op jit(solution)/shard_map/ppermute | solution.py:25
  30.5 2.9 %collective-permute-start.4 = (bf16[192,256]{1,0:T(8,128)(2,1)S(1)}, bf16[192,256]{1,0:T(8,128)(2,1)S(1)}, u32[]{:S(2)}, u32[]{:S(2)}) collective-permute-start(bf16[192,256]{1,0:T(8,128)(2,1)S(1)} %get-tuple-element.13), channel_id=1, source_target_pairs={{0,96},{16,112},{32,0},{48,16},{64,32},{80,48},{96,64},{112,80},{1... | collective-permute-start | bytes 294920 | tf_op jit(solution)/shard_map/ppermute | solution.py:25
  34.5 2.2 %collective-permute-start.2 = (bf16[192,256]{1,0:T(8,128)(2,1)S(1)}, bf16[192,256]{1,0:T(8,128)(2,1)S(1)}, u32[]{:S(2)}, u32[]{:S(2)}) collective-permute-start(bf16[192,256]{1,0:T(8,128)(2,1)S(1)} %get-tuple-element.13), channel_id=1, source_target_pairs={{0,112},{16,0},{32,16},{48,32},{64,48},{80,64},{96,80},{112,96},{1... | collective-permute-start | bytes 294920 | tf_op jit(solution)/shard_map/ppermute | solution.py:25
  36.9 2.7 %collective-permute-done.4 = bf16[192,256]{1,0:T(8,128)(2,1)S(1)} collective-permute-done((bf16[192,256]{1,0:T(8,128)(2,1)S(1)}, bf16[192,256]{1,0:T(8,128)(2,1)S(1)}, u32[]{:S(2)}, u32[]{:S(2)}) %collective-permute-start.4) | collective-permute-done | bytes 98336 | tf_op jit(solution)/shard_map/ppermute | solution.py:25
  40.7 2.6 %collective-permute-start.8 = (bf16[288,256]{1,0:T(8,128)(2,1)S(1)}, bf16[288,256]{1,0:T(8,128)(2,1)S(1)}, u32[]{:S(2)}, u32[]{:S(2)}) collective-permute-start(bf16[288,256]{1,0:T(8,128)(2,1)S(1)} %pad_maximum_fusion.7), channel_id=1, source_target_pairs={{0,96},{16,112},{32,0},{48,16},{64,32},{80,48},{96,64},{112,80},{1... | collective-permute-start | bytes 442376 | tf_op jit(solution)/shard_map/ppermute | solution.py:25
  43.9 2.6 %collective-permute-start.6 = (bf16[5,192,256]{2,1,0:T(8,128)(2,1)S(1)}, bf16[5,192,256]{2,1,0:T(8,128)(2,1)S(1)}, u32[]{:S(2)}, u32[]{:S(2)}) collective-permute-start(bf16[5,192,256]{2,1,0:T(8,128)(2,1)S(1)} %bitcast_dynamic-update-slice_fusion.1), channel_id=1, source_target_pairs={{0,128},{16,144},{32,160},{48,176},{64,192},{80,208},{96,224},{112... | collective-permute-start | bytes 1474568 | tf_op jit(solution)/shard_map/ppermute | solution.py:30
  46.9 5.3 %collective-permute-done.7 = bf16[288,256]{1,0:T(8,128)(2,1)S(1)} collective-permute-done((bf16[288,256]{1,0:T(8,128)(2,1)S(1)}, bf16[288,256]{1,0:T(8,128)(2,1)S(1)}, u32[]{:S(2)}, u32[]{:S(2)}) %collective-permute-start.7) | collective-permute-done | bytes 147488 | tf_op jit(solution)/shard_map/ppermute | solution.py:25
  52.3 2.6 %collective-permute-start.9 = (bf16[3,192,256]{2,1,0:T(8,128)(2,1)S(1)}, bf16[3,192,256]{2,1,0:T(8,128)(2,1)S(1)}, u32[]{:S(2)}, u32[]{:S(2)}) collective-permute-start(bf16[3,192,256]{2,1,0:T(8,128)(2,1)S(1)} %pad_maximum_fusion.4), channel_id=1, source_target_pairs={{0,128},{16,144},{32,160},{48,176},{64,192},{80,208},{96,224},{112... | collective-permute-start | bytes 884744 | tf_op jit(solution)/shard_map/ppermute | solution.py:30
  54.9 3.2 %collective-permute-done.6 = bf16[5,192,256]{2,1,0:T(8,128)(2,1)S(1)} collective-permute-done((bf16[5,192,256]{2,1,0:T(8,128)(2,1)S(1)}, bf16[5,192,256]{2,1,0:T(8,128)(2,1)S(1)}, u32[]{:S(2)}, u32[]{:S(2)}) %collective-permute-start.6) | collective-permute-done | bytes 491552 | tf_op jit(solution)/shard_map/ppermute | solution.py:30
  58.4 3.4 %collective-permute-done.9 = bf16[3,192,256]{2,1,0:T(8,128)(2,1)S(1)} collective-permute-done((bf16[3,192,256]{2,1,0:T(8,128)(2,1)S(1)}, bf16[3,192,256]{2,1,0:T(8,128)(2,1)S(1)}, u32[]{:S(2)}, u32[]{:S(2)}) %collective-permute-start.9) | collective-permute-done | bytes 294944 | tf_op jit(solution)/shard_map/ppermute | solution.py:30
  62.0 1.8 %convolution_bitcast_fusion = f32[384,1024]{1,0:T(8,128)S(1)} fusion(bf16[8,384,256]{2,1,0:T(8,128)(2,1)S(1)} %bitcast_select_fusion, bf16[8,256,1024]{2,1,0:T(8,128)(2,1)S(1)} %copy-done.2), kind=kOutput, calls=%fused_computation.8 | convolution fusion | flops 1610612736 | bytes 7340032 | tf_op jit(solution)/shard_map/dot_general | solution.py:161
  64.0 1.7 %collective-permute-done.10 = bf16[192,1024]{1,0:T(8,128)(2,1)S(1)} collective-permute-done((bf16[192,1024]{1,0:T(8,128)(2,1)S(1)}, bf16[192,1024]{1,0:T(8,128)(2,1)S(1)}, u32[]{:S(2)}, u32[]{:S(2)}) %collective-permute-start.10) | collective-permute-done | bytes 393248 | tf_op jit(solution)/shard_map/ppermute | solution.py:8
  65.8 13.6 %all_to_all.16 = bf16[8,24,1024]{2,1,0:T(8,128)(2,1)S(1)} all-to-all(bf16[8,24,1024]{2,1,0:T(8,128)(2,1)S(1)} %bitcast.100), channel_id=1, replica_groups={{0,2,4,6,8,10,12,14},{1,3,5,7,9,11,13,15},{16,18,20,22,24,26,28,30},{17..., dimensions={0} | all-to-all | bytes 786432 | tf_op jit(solution)/shard_map/all_to_all | solution.py:16
  79.6 12.4 %all_to_all.17 = bf16[8,24,1024]{2,1,0:T(8,128)(2,1)S(1)} all-to-all(bf16[8,24,1024]{2,1,0:T(8,128)(2,1)S(1)} %broadcast_in_dim.80), channel_id=1, replica_groups={{0,2,4,6,8,10,12,14},{1,3,5,7,9,11,13,15},{16,18,20,22,24,26,28,30},{17..., dimensions={0} | all-to-all | bytes 786432 | tf_op jit(solution)/shard_map/all_to_all | solution.py:16
  92.0 1.6 %collective-permute-done.11 = bf16[192,1024]{1,0:T(8,128)(2,1)S(1)} collective-permute-done((bf16[192,1024]{1,0:T(8,128)(2,1)S(1)}, bf16[192,1024]{1,0:T(8,128)(2,1)S(1)}, u32[]{:S(2)}, u32[]{:S(2)}) %collective-permute-start.11) | collective-permute-done | bytes 393248 | tf_op jit(solution)/shard_map/ppermute | solution.py:8
  93.7 2.6 %fusion.8 = bf16[4,384,256]{2,1,0:T(8,128)(2,1)S(1)} fusion(bf16[8,256,1024]{2,1,0:T(8,128)(2,1)} %param.9, pred[4]{0:T(512)(128)(4,1)S(1)} %get-tuple-element.30, bf16[192,1024]{1,0:T(8,128)(2,1)S(1)} %collective-permute-done.11, bf16[192,1024]{1,0:T(8,128)(2,1)S(1)} %bitcast.99), kind=kOutput, calls=%fused_computation.9 | convolution fusion | flops 807665664 | bytes 3670020 | tf_op jit(solution)/shard_map/dot_general | solution.py:75
  97.8 1.7 %collective-permute-start.13 = (bf16[5,192,256]{2,1,0:T(8,128)(2,1)S(1)}, bf16[5,192,256]{2,1,0:T(8,128)(2,1)S(1)}, u32[]{:S(2)}, u32[]{:S(2)}) collective-permute-start(bf16[5,192,256]{2,1,0:T(8,128)(2,1)S(1)} %get-tuple-element.22), channel_id=1, source_target_pairs={{128,0},{144,16},{160,32},{176,48},{192,64},{208,80},{224,96},{240... | collective-permute-start | bytes 1474568 | tf_op jit(solution)/shard_map/ppermute | solution.py:35
  99.5 4.4 %convolution_convert_fusion = bf16[8,256,1024]{2,1,0:T(8,128)(2,1)} fusion(bf16[8,384,256]{2,1,0:T(8,128)(2,1)S(1)} %bitcast_select_fusion, bf16[384,1024]{1,0:T(8,128)(2,1)S(1)} %pad_maximum_fusion.1), kind=kOutput, calls=%fused_computation | convolution fusion | flops 1612709888 | bytes 6553600 | tf_op jit(solution)/shard_map/dot_general | solution.py:174
  105.0 3.3 %collective-permute-done.12 = bf16[3,192,256]{2,1,0:T(8,128)(2,1)S(1)} collective-permute-done((bf16[3,192,256]{2,1,0:T(8,128)(2,1)S(1)}, bf16[3,192,256]{2,1,0:T(8,128)(2,1)S(1)}, u32[]{:S(2)}, u32[]{:S(2)}) %collective-permute-start.12) | collective-permute-done | bytes 294944 | tf_op jit(solution)/shard_map/ppermute | solution.py:35
  108.4 3.9 %collective-permute-start.16 = (bf16[288,256]{1,0:T(8,128)(2,1)S(1)}, bf16[288,256]{1,0:T(8,128)(2,1)S(1)}, u32[]{:S(2)}, u32[]{:S(2)}) collective-permute-start(bf16[288,256]{1,0:T(8,128)(2,1)S(1)} %pad_maximum_fusion.9), channel_id=1, source_target_pairs={{0,96},{16,112},{32,0},{48,16},{64,32},{80,48},{96,64},{112,80},{1... | collective-permute-start | bytes 442376 | tf_op jit(solution)/shard_map/ppermute | solution.py:25
  112.4 4.9 %collective-permute-done.16 = bf16[288,256]{1,0:T(8,128)(2,1)S(1)} collective-permute-done((bf16[288,256]{1,0:T(8,128)(2,1)S(1)}, bf16[288,256]{1,0:T(8,128)(2,1)S(1)}, u32[]{:S(2)}, u32[]{:S(2)}) %collective-permute-start.16) | collective-permute-done | bytes 147488 | tf_op jit(solution)/shard_map/ppermute | solution.py:25
  117.3 4.3 %collective-permute-done.14 = bf16[288,256]{1,0:T(8,128)(2,1)S(1)} collective-permute-done((bf16[288,256]{1,0:T(8,128)(2,1)S(1)}, bf16[288,256]{1,0:T(8,128)(2,1)S(1)}, u32[]{:S(2)}, u32[]{:S(2)}) %collective-permute-start.14) | collective-permute-done | bytes 147488 | tf_op jit(solution)/shard_map/ppermute | solution.py:25
  123.1 2.0 %collective-permute-start.18 = (bf16[192,256]{1,0:T(8,128)(2,1)S(1)}, bf16[192,256]{1,0:T(8,128)(2,1)S(1)}, u32[]{:S(2)}, u32[]{:S(2)}) collective-permute-start(bf16[192,256]{1,0:T(8,128)(2,1)S(1)} %get-tuple-element.16), channel_id=1, source_target_pairs={{0,32},{16,48},{32,64},{48,80},{64,96},{80,112},{96,0},{112,16},{1... | collective-permute-start | bytes 294920 | tf_op jit(solution)/shard_map/ppermute | solution.py:25
  125.1 4.1 %collective-permute-start.17 = (bf16[192,256]{1,0:T(8,128)(2,1)S(1)}, bf16[192,256]{1,0:T(8,128)(2,1)S(1)}, u32[]{:S(2)}, u32[]{:S(2)}) collective-permute-start(bf16[192,256]{1,0:T(8,128)(2,1)S(1)} %get-tuple-element.17), channel_id=1, source_target_pairs={{0,112},{16,0},{32,16},{48,32},{64,48},{80,64},{96,80},{112,96},{1... | collective-permute-start | bytes 294920 | tf_op jit(solution)/shard_map/ppermute | solution.py:25
  129.3 1.9 %collective-permute-done.18 = bf16[192,256]{1,0:T(8,128)(2,1)S(1)} collective-permute-done((bf16[192,256]{1,0:T(8,128)(2,1)S(1)}, bf16[192,256]{1,0:T(8,128)(2,1)S(1)}, u32[]{:S(2)}, u32[]{:S(2)}) %collective-permute-start.18) | collective-permute-done | bytes 98336 | tf_op jit(solution)/shard_map/ppermute | solution.py:25
  131.5 2.4 %collective-permute-start.20 = (bf16[192,256]{1,0:T(8,128)(2,1)S(1)}, bf16[192,256]{1,0:T(8,128)(2,1)S(1)}, u32[]{:S(2)}, u32[]{:S(2)}) collective-permute-start(bf16[192,256]{1,0:T(8,128)(2,1)S(1)} %fusion.34), channel_id=1, source_target_pairs={{0,16},{16,0},{32,48},{48,32},{64,80},{80,64},{96,112},{112,96},{1... | collective-permute-start | bytes 294920 | tf_op jit(solution)/shard_map/ppermute | solution.py:8
  133.9 2.6 %collective-permute-done.20 = bf16[192,256]{1,0:T(8,128)(2,1)S(1)} collective-permute-done((bf16[192,256]{1,0:T(8,128)(2,1)S(1)}, bf16[192,256]{1,0:T(8,128)(2,1)S(1)}, u32[]{:S(2)}, u32[]{:S(2)}) %collective-permute-start.20) | collective-permute-done | bytes 98336 | tf_op jit(solution)/shard_map/ppermute | solution.py:8
  136.6 1.4 %fusion.21 = f32[1024,256]{1,0:T(8,128)} fusion(bf16[192,1024]{1,0:T(8,128)(2,1)S(1)} %copy-done.5, bf16[192,1024]{1,0:T(8,128)(2,1)S(1)} %bitcast.111, bf16[192,256]{1,0:T(8,128)(2,1)S(1)} %get-tuple-element.26, bf16[192,256]{1,0:T(8,128)(2,1)S(1)} %get-tuple-element.25), kind=kOutput, calls=%fused_computation.21 | convolution fusion | flops 203292672 | bytes 2031616 | tf_op jit(solution)/shard_map/dot_general | solution.py:187
  (91 shorter events, 10.7 us)
Async XLA Ops:
  0.6 18.9 %copy-start = (bf16[1024,256]{1,0:T(8,128)(2,1)S(1)}, bf16[1024,256]{1,0:T(8,128)(2,1)}, u32[]{:S(2)}) copy-start(bf16[1024,256]{1,0:T(8,128)(2,1)} %param.7) | copy-start | bytes 1572868
  17.8 1.7 %collective-permute-start = (bf16[192,1024]{1,0:T(8,128)(2,1)S(1)}, bf16[192,1024]{1,0:T(8,128)(2,1)S(1)}, u32[]{:S(2)}, u32[]{:S(2)}) collective-permute-start(bf16[192,1024]{1,0:T(8,128)(2,1)S(1)} %bitcast.109), channel_id=1, source_target_pairs={{0,1},{1,0},{2,3},{3,2},{4,5},{5,4},{6,7},{7,6},{8,9},{9,8},{10,11... | collective-permute-start | bytes 1179656 | tf_op jit(solution)/shard_map/ppermute | solution.py:8
  19.5 7.6 %copy-start.4 = (bf16[192,1024]{1,0:T(8,128)(2,1)}, bf16[192,1024]{1,0:T(8,128)(2,1)S(1)}, u32[]{:S(2)}) copy-start(bf16[192,1024]{1,0:T(8,128)(2,1)S(1)} %collective-permute-done) | copy-start | bytes 1179652
  20.0 7.2 %collective-permute-start.1 = (f32[192,256]{1,0:T(8,128)S(1)}, f32[192,256]{1,0:T(8,128)S(1)}, u32[]{:S(2)}, u32[]{:S(2)}) collective-permute-start(f32[192,256]{1,0:T(8,128)S(1)} %constant_dynamic-slice_fusion.4), channel_id=1, source_target_pairs={{0,16},{16,0},{32,48},{48,32},{64,80},{80,64},{96,112},{112,96},{1... | collective-permute-start | bytes 589832 | tf_op jit(solution)/shard_map/ppermute | solution.py:8
  27.2 16.2 %collective-permute-start.5 = (bf16[192,256]{1,0:T(8,128)(2,1)S(1)}, bf16[192,256]{1,0:T(8,128)(2,1)S(1)}, u32[]{:S(2)}, u32[]{:S(2)}) collective-permute-start(bf16[192,256]{1,0:T(8,128)(2,1)S(1)} %get-tuple-element.13), channel_id=1, source_target_pairs={{0,32},{16,48},{32,64},{48,80},{64,96},{80,112},{96,0},{112,16},{1... | collective-permute-start | bytes 294920 | tf_op jit(solution)/shard_map/ppermute | solution.py:25
  30.5 9.1 %collective-permute-start.4 = (bf16[192,256]{1,0:T(8,128)(2,1)S(1)}, bf16[192,256]{1,0:T(8,128)(2,1)S(1)}, u32[]{:S(2)}, u32[]{:S(2)}) collective-permute-start(bf16[192,256]{1,0:T(8,128)(2,1)S(1)} %get-tuple-element.13), channel_id=1, source_target_pairs={{0,96},{16,112},{32,0},{48,16},{64,32},{80,48},{96,64},{112,80},{1... | collective-permute-start | bytes 294920 | tf_op jit(solution)/shard_map/ppermute | solution.py:25
  33.5 9.9 %collective-permute-start.3 = (bf16[192,256]{1,0:T(8,128)(2,1)S(1)}, bf16[192,256]{1,0:T(8,128)(2,1)S(1)}, u32[]{:S(2)}, u32[]{:S(2)}) collective-permute-start(bf16[192,256]{1,0:T(8,128)(2,1)S(1)} %get-tuple-element.13), channel_id=1, source_target_pairs={{0,16},{16,32},{32,48},{48,64},{64,80},{80,96},{96,112},{112,0},{1... | collective-permute-start | bytes 294920 | tf_op jit(solution)/shard_map/ppermute | solution.py:25
  34.5 6.2 %collective-permute-start.2 = (bf16[192,256]{1,0:T(8,128)(2,1)S(1)}, bf16[192,256]{1,0:T(8,128)(2,1)S(1)}, u32[]{:S(2)}, u32[]{:S(2)}) collective-permute-start(bf16[192,256]{1,0:T(8,128)(2,1)S(1)} %get-tuple-element.13), channel_id=1, source_target_pairs={{0,112},{16,0},{32,16},{48,32},{64,48},{80,64},{96,80},{112,96},{1... | collective-permute-start | bytes 294920 | tf_op jit(solution)/shard_map/ppermute | solution.py:25
  40.7 6.1 %collective-permute-start.8 = (bf16[288,256]{1,0:T(8,128)(2,1)S(1)}, bf16[288,256]{1,0:T(8,128)(2,1)S(1)}, u32[]{:S(2)}, u32[]{:S(2)}) collective-permute-start(bf16[288,256]{1,0:T(8,128)(2,1)S(1)} %pad_maximum_fusion.7), channel_id=1, source_target_pairs={{0,96},{16,112},{32,0},{48,16},{64,32},{80,48},{96,64},{112,80},{1... | collective-permute-start | bytes 442376 | tf_op jit(solution)/shard_map/ppermute | solution.py:25
  43.4 8.8 %collective-permute-start.7 = (bf16[288,256]{1,0:T(8,128)(2,1)S(1)}, bf16[288,256]{1,0:T(8,128)(2,1)S(1)}, u32[]{:S(2)}, u32[]{:S(2)}) collective-permute-start(bf16[288,256]{1,0:T(8,128)(2,1)S(1)} %pad_maximum_fusion.6), channel_id=1, source_target_pairs={{0,32},{16,48},{32,64},{48,80},{64,96},{80,112},{96,0},{112,16},{1... | collective-permute-start | bytes 442376 | tf_op jit(solution)/shard_map/ppermute | solution.py:25
  43.9 14.2 %collective-permute-start.6 = (bf16[5,192,256]{2,1,0:T(8,128)(2,1)S(1)}, bf16[5,192,256]{2,1,0:T(8,128)(2,1)S(1)}, u32[]{:S(2)}, u32[]{:S(2)}) collective-permute-start(bf16[5,192,256]{2,1,0:T(8,128)(2,1)S(1)} %bitcast_dynamic-update-slice_fusion.1), channel_id=1, source_target_pairs={{0,128},{16,144},{32,160},{48,176},{64,192},{80,208},{96,224},{112... | collective-permute-start | bytes 1474568 | tf_op jit(solution)/shard_map/ppermute | solution.py:30
  52.3 9.4 %collective-permute-start.9 = (bf16[3,192,256]{2,1,0:T(8,128)(2,1)S(1)}, bf16[3,192,256]{2,1,0:T(8,128)(2,1)S(1)}, u32[]{:S(2)}, u32[]{:S(2)}) collective-permute-start(bf16[3,192,256]{2,1,0:T(8,128)(2,1)S(1)} %pad_maximum_fusion.4), channel_id=1, source_target_pairs={{0,128},{16,144},{32,160},{48,176},{64,192},{80,208},{96,224},{112... | collective-permute-start | bytes 884744 | tf_op jit(solution)/shard_map/ppermute | solution.py:30
  58.3 3.7 %copy-start.2 = (bf16[8,256,1024]{2,1,0:T(8,128)(2,1)S(1)}, bf16[8,256,1024]{2,1,0:T(8,128)(2,1)}, u32[]{:S(2)}) copy-start(bf16[8,256,1024]{2,1,0:T(8,128)(2,1)} %param.9) | copy-start | bytes 12582916
  63.9 15.6 %copy-start.1 = (bf16[24,1024]{1,0:T(8,128)(2,1)S(1)}, bf16[24,1024]{1,0:T(8,128)(2,1)}, u32[]{:S(2)}) copy-start(bf16[24,1024]{1,0:T(8,128)(2,1)} %param.6) | copy-start | bytes 147460
  63.9 1.8 %collective-permute-start.10 = (bf16[192,1024]{1,0:T(8,128)(2,1)S(1)}, bf16[192,1024]{1,0:T(8,128)(2,1)S(1)}, u32[]{:S(2)}, u32[]{:S(2)}) collective-permute-start(bf16[192,1024]{1,0:T(8,128)(2,1)S(1)} %slice.218), channel_id=1, source_target_pairs={{0,1},{1,0},{2,3},{3,2},{4,5},{5,4},{6,7},{7,6},{8,9},{9,8},{10,11... | collective-permute-start | bytes 1179656 | tf_op jit(solution)/shard_map/ppermute | solution.py:8
  91.9 1.7 %collective-permute-start.11 = (bf16[192,1024]{1,0:T(8,128)(2,1)S(1)}, bf16[192,1024]{1,0:T(8,128)(2,1)S(1)}, u32[]{:S(2)}, u32[]{:S(2)}) collective-permute-start(bf16[192,1024]{1,0:T(8,128)(2,1)S(1)} %bitcast.97), channel_id=1, source_target_pairs={{0,1},{1,0},{2,3},{3,2},{4,5},{5,4},{6,7},{7,6},{8,9},{9,8},{10,11... | collective-permute-start | bytes 1179656 | tf_op jit(solution)/shard_map/ppermute | solution.py:8
  96.5 11.7 %collective-permute-start.12 = (bf16[3,192,256]{2,1,0:T(8,128)(2,1)S(1)}, bf16[3,192,256]{2,1,0:T(8,128)(2,1)S(1)}, u32[]{:S(2)}, u32[]{:S(2)}) collective-permute-start(bf16[3,192,256]{2,1,0:T(8,128)(2,1)S(1)} %pad_maximum_fusion.5), channel_id=1, source_target_pairs={{128,0},{144,16},{160,32},{176,48},{192,64},{208,80},{224,96},{240... | collective-permute-start | bytes 884744 | tf_op jit(solution)/shard_map/ppermute | solution.py:35
  97.8 6.2 %copy-start.3 = (bf16[8,256,1024]{2,1,0:T(8,128)(2,1)S(1)}, bf16[8,256,1024]{2,1,0:T(8,128)(2,1)}, u32[]{:S(2)}) copy-start(bf16[8,256,1024]{2,1,0:T(8,128)(2,1)} %param.9) | copy-start | bytes 12582916
  97.8 23.8 %collective-permute-start.13 = (bf16[5,192,256]{2,1,0:T(8,128)(2,1)S(1)}, bf16[5,192,256]{2,1,0:T(8,128)(2,1)S(1)}, u32[]{:S(2)}, u32[]{:S(2)}) collective-permute-start(bf16[5,192,256]{2,1,0:T(8,128)(2,1)S(1)} %get-tuple-element.22), channel_id=1, source_target_pairs={{128,0},{144,16},{160,32},{176,48},{192,64},{208,80},{224,96},{240... | collective-permute-start | bytes 1474568 | tf_op jit(solution)/shard_map/ppermute | solution.py:35
  108.4 8.9 %collective-permute-start.16 = (bf16[288,256]{1,0:T(8,128)(2,1)S(1)}, bf16[288,256]{1,0:T(8,128)(2,1)S(1)}, u32[]{:S(2)}, u32[]{:S(2)}) collective-permute-start(bf16[288,256]{1,0:T(8,128)(2,1)S(1)} %pad_maximum_fusion.9), channel_id=1, source_target_pairs={{0,96},{16,112},{32,0},{48,16},{64,32},{80,48},{96,64},{112,80},{1... | collective-permute-start | bytes 442376 | tf_op jit(solution)/shard_map/ppermute | solution.py:25
  112.3 24.3 %copy-start.5 = (bf16[192,1024]{1,0:T(8,128)(2,1)S(1)}, bf16[192,1024]{1,0:T(8,128)(2,1)}, u32[]{:S(2)}) copy-start(bf16[192,1024]{1,0:T(8,128)(2,1)} %copy-done.4) | copy-start | bytes 1179652
  112.3 9.3 %collective-permute-start.14 = (bf16[288,256]{1,0:T(8,128)(2,1)S(1)}, bf16[288,256]{1,0:T(8,128)(2,1)S(1)}, u32[]{:S(2)}, u32[]{:S(2)}) collective-permute-start(bf16[288,256]{1,0:T(8,128)(2,1)S(1)} %pad_maximum_fusion.8), channel_id=1, source_target_pairs={{0,32},{16,48},{32,64},{48,80},{64,96},{80,112},{96,0},{112,16},{1... | collective-permute-start | bytes 442376 | tf_op jit(solution)/shard_map/ppermute | solution.py:25
  121.8 7.5 %collective-permute-start.15 = (bf16[192,256]{1,0:T(8,128)(2,1)S(1)}, bf16[192,256]{1,0:T(8,128)(2,1)S(1)}, u32[]{:S(2)}, u32[]{:S(2)}) collective-permute-start(bf16[192,256]{1,0:T(8,128)(2,1)S(1)} %get-tuple-element.14), channel_id=1, source_target_pairs={{0,16},{16,32},{32,48},{48,64},{64,80},{80,96},{96,112},{112,0},{1... | collective-permute-start | bytes 294920 | tf_op jit(solution)/shard_map/ppermute | solution.py:25
  122.2 7.1 %collective-permute-start.19 = (bf16[192,256]{1,0:T(8,128)(2,1)S(1)}, bf16[192,256]{1,0:T(8,128)(2,1)S(1)}, u32[]{:S(2)}, u32[]{:S(2)}) collective-permute-start(bf16[192,256]{1,0:T(8,128)(2,1)S(1)} %get-tuple-element.15), channel_id=1, source_target_pairs={{0,96},{16,112},{32,0},{48,16},{64,32},{80,48},{96,64},{112,80},{1... | collective-permute-start | bytes 294920 | tf_op jit(solution)/shard_map/ppermute | solution.py:25
  123.1 8.0 %collective-permute-start.18 = (bf16[192,256]{1,0:T(8,128)(2,1)S(1)}, bf16[192,256]{1,0:T(8,128)(2,1)S(1)}, u32[]{:S(2)}, u32[]{:S(2)}) collective-permute-start(bf16[192,256]{1,0:T(8,128)(2,1)S(1)} %get-tuple-element.16), channel_id=1, source_target_pairs={{0,32},{16,48},{32,64},{48,80},{64,96},{80,112},{96,0},{112,16},{1... | collective-permute-start | bytes 294920 | tf_op jit(solution)/shard_map/ppermute | solution.py:25
  125.1 6.3 %collective-permute-start.17 = (bf16[192,256]{1,0:T(8,128)(2,1)S(1)}, bf16[192,256]{1,0:T(8,128)(2,1)S(1)}, u32[]{:S(2)}, u32[]{:S(2)}) collective-permute-start(bf16[192,256]{1,0:T(8,128)(2,1)S(1)} %get-tuple-element.17), channel_id=1, source_target_pairs={{0,112},{16,0},{32,16},{48,32},{64,48},{80,64},{96,80},{112,96},{1... | collective-permute-start | bytes 294920 | tf_op jit(solution)/shard_map/ppermute | solution.py:25
  131.5 5.0 %collective-permute-start.20 = (bf16[192,256]{1,0:T(8,128)(2,1)S(1)}, bf16[192,256]{1,0:T(8,128)(2,1)S(1)}, u32[]{:S(2)}, u32[]{:S(2)}) collective-permute-start(bf16[192,256]{1,0:T(8,128)(2,1)S(1)} %fusion.34), channel_id=1, source_target_pairs={{0,16},{16,0},{32,48},{48,32},{64,80},{80,64},{96,112},{112,96},{1... | collective-permute-start | bytes 294920 | tf_op jit(solution)/shard_map/ppermute | solution.py:8

commit v5 on v4

--- a/solution.py
+++ b/solution.py
@@ -45,29 +45,30 @@
 
     def put(stack, block, which, distance):
         place = which * ring + (spot + distance) % ring
-        return lax.dynamic_update_index_in_dim(stack, block, place, 0)
-
-    near = {0: own}
-    for distance in (1, -1, 2, -2):
-        near[distance] = along_ring(own, -distance)
-    behind = along_ring(jnp.concatenate([near[-1], near[-2][:half]], 0), 2)
-    ahead = along_ring(jnp.concatenate([near[1], near[2][half:]], 0), -2)
-    near_order = list(near)
-    near_crossed = to_later_plane(jnp.stack([near[d] for d in near_order], 0))
+        at = (place % 2) * ring + place // 2
+        return lax.dynamic_update_index_in_dim(stack, block, at, 0)
+
+    near = {0: own, 1: along_ring(own, -1), -1: along_ring(own, 1)}
+    bundles = [near]
+    crossed = [to_later_plane(jnp.stack(list(near.values()), 0))]
+    middle = {2: along_ring(own, -2), -2: along_ring(own, 2)}
+    ready, middle = lax.optimization_barrier((near, middle))
+    behind = along_ring(jnp.concatenate([ready[-1], middle[-2][:half]], 0), 2)
+    ahead = along_ring(jnp.concatenate([ready[1], middle[2][half:]], 0), -2)
+    bundles.append(middle)
+    crossed.append(to_later_plane(jnp.stack(list(middle.values()), 0)))
     far = {
         -3: behind[: 2 * half],
         3: ahead[: 2 * half],
         4: jnp.concatenate([behind[2 * half :], ahead[2 * half :]], 0),
     }
-    far_order = list(far)
-    far_crossed = to_later_plane(jnp.stack([far[d] for d in far_order], 0))
-    for blocks, crossed, order in (
-        (near, near_crossed, near_order),
-        (far, far_crossed, far_order),
-    ):
-        for at, distance in enumerate(order):
+    far, crossed[0] = lax.optimization_barrier((far, crossed[0]))
+    bundles.append(far)
+    crossed.append(to_later_plane(jnp.stack(list(far.values()), 0)))
+    for blocks, others in zip(bundles, crossed):
+        for at, distance in enumerate(blocks):
             stack = put(stack, blocks[distance], plane, distance)
-            stack = put(stack, crossed[at], 1 - plane, distance)
+            stack = put(stack, others[at], 1 - plane, distance)
     return stack
 
 
@@ -79,10 +80,15 @@
 
 
 def terms_to_layers(lower, own, spot, ring, tie):
-    half = own.shape[1] // 2
+    rows = own[0].shape[1]
+    half = rows // 2
 
     def at(blocks, distance):
-        return lax.dynamic_index_in_dim(blocks, (spot + distance) % ring, 0, keepdims=False)
+        place = (spot + distance) % ring
+        even, odd = [
+            lax.dynamic_index_in_dim(part, place // 2, 0, keepdims=False) for part in blocks
+        ]
+        return jnp.where(place % 2 == 0, even, odd)
 
     first, second = (4, 3, -3), (1, -1, 2, -2, 0)
     early = to_earlier_plane(jnp.stack([at(lower, d) for d in first], 0))
@@ -112,23 +118,21 @@
     return total, tie
 
 
-def rows_of_all(x):
+def own_core_rows(x):
     size = lax.axis_size("latent")
     chips = size // 2
     rows, width = x.shape
     copies = jnp.broadcast_to(x[None], (chips, rows, width))
-    own = exchanged(copies, "latent", same_core_groups(size)).reshape(chips * rows, width)
-    other = from_partner(own, "latent", 1)
-    return jnp.concatenate([own, other], 0)
-
-
-def rows_summed(x):
+    return exchanged(copies, "latent", same_core_groups(size)).reshape(chips * rows, width)
+
+
+def rows_summed(own, other):
     size = lax.axis_size("latent")
     chips = size // 2
-    half = x.shape[0] // 2
-    theirs = from_partner(x[half:].astype(jnp.bfloat16), "latent", 1)
-    both = (x[:half] + theirs.astype(jnp.float32)).astype(jnp.bfloat16)
-    parts = both.reshape(chips, half // chips, x.shape[1])
+    theirs = from_partner(other.astype(jnp.bfloat16), "latent", 1)
+    own, theirs = lax.optimization_barrier((own, theirs))
+    both = (own + theirs.astype(jnp.float32)).astype(jnp.bfloat16)
+    parts = both.reshape(chips, own.shape[0] // chips, own.shape[1])
     arrived = exchanged(parts, "latent", same_core_groups(size))
     return arrived.astype(jnp.float32).sum(axis=0)
 
@@ -141,7 +145,8 @@
     layer_count = places // 2
     latent_cols = enc_weight.shape[1]
 
-    inputs_half = rows_of_all(layer_inputs)
+    inputs_own = own_core_rows(layer_inputs)
+    inputs_half = jnp.concatenate([inputs_own, from_partner(inputs_own, "latent", 1)], 0)
     total_rows = inputs_half.shape[0]
     half_rows = total_rows // 2
     own_part = jnp.dot(inputs_half, enc_weight, preferred_element_type=jnp.float32)
@@ -154,30 +159,35 @@
     ring = places // 2
     plane, spot = position // ring, position % ring
     gathered = latents_of_all(latents_half, plane, spot, ring)
-    gathered = gathered.reshape(layer_count, total_rows, latent_cols)
+    gathered = gathered.reshape(2, layer_count, half_rows, latent_cols)
     used = lax.broadcasted_iota(jnp.int32, (layer_count, 1, 1), 0) <= layer_now
     latents = jnp.where(used, gathered, jnp.zeros_like(gathered))
 
-    recon = lax.dot_general(
-        latents, dec_weight, (((0, 2), (0, 1)), ((), ())), preferred_element_type=jnp.float32
-    )
-    recon_own = rows_summed(recon)
+    def decoded(part):
+        return lax.dot_general(
+            part, dec_weight, (((0, 2), (0, 1)), ((), ())), preferred_element_type=jnp.float32
+        )
+
+    recon_own = rows_summed(decoded(latents[0]), decoded(latents[1]))
     rscale = total_rows ** (-0.5)
     grad_own = ((recon_own - mlp_outputs.astype(jnp.float32)) * rscale).astype(jnp.bfloat16)
-    out_grad = rows_of_all(grad_own)
+    grad_same = own_core_rows(grad_own)
+    grad_other = from_partner(grad_same, "latent", 1)
 
     near = layer_count // 2
-    lower = layer_terms(out_grad, dec_weight[:near], used[:near])
-    lower, grad_after = lax.optimization_barrier((lower, out_grad))
-    upper = layer_terms(grad_after, dec_weight[near:], used[near:])
-    own_terms = jnp.where(plane == 1, upper, lower)
+    lower_same = layer_terms(grad_same, dec_weight[:near], used[:near])
+    lower_same, grad_other = lax.optimization_barrier((lower_same, grad_other))
+    lower = (lower_same, layer_terms(grad_other, dec_weight[:near], used[:near]))
+    lower, grads = lax.optimization_barrier((lower, (grad_same, grad_other)))
+    upper = [layer_terms(grad, dec_weight[near:], used[near:]) for grad in grads]
+    own_terms = [jnp.where(plane == 1, high, low) for high, low in zip(upper, lower)]
     dec_grad = lax.dot_general(
-        latents, grad_after, (((1,), (0,)), ((), ())), preferred_element_type=jnp.float32
+        latents,
+        jnp.stack(grads, 0),
+        (((0, 2), (0, 1)), ((), ())),
+        preferred_element_type=jnp.float32,
     ).astype(jnp.bfloat16)
-    places_shape = (ring, half_rows, latent_cols)
-    lat_grad, dec_grad = terms_to_layers(
-        lower.reshape(places_shape), own_terms.reshape(places_shape), spot, ring, dec_grad
-    )
+    lat_grad, dec_grad = terms_to_layers(lower, own_terms, spot, ring, dec_grad)
     pre_grad = jnp.where(latents_half > 0, lat_grad, 0.0).astype(jnp.bfloat16)
     pre_other = from_partner(pre_grad, "layer", 1)
     first = which_half == 0

time: 139 us -> 144 us (1.036)
  blocking collectives: 42.3 us -> 29.5 us
  matrix products: 11.6 us -> 15.9 us
  waiting for transfers between devices: 42.9 us -> 46.9 us
  local copies, waits for them, and re-layouts: 2.34 us -> 5.95 us
  other arithmetic: 0.95 us -> 3.31 us
  starting transfers between devices: 36.8 us -> 39 us
    all_to_all x3 -> x2, blocking collectives: 42.3 us -> 29.5 us  [exchanged(): lax.all_to_all(parts, axis, split_axis=0, concat_axis=0, tiled=True, axis...]
    all_to_all x0 -> x1, waiting for transfers between devices: none -> 8.83 us  [exchanged(): lax.all_to_all(parts, axis, split_axis=0, concat_axis=0, tiled=True, axis...]
    all_to_all x0 -> x1, starting transfers between devices: none -> 4.53 us  [exchanged(): lax.all_to_all(parts, axis, split_axis=0, concat_axis=0, tiled=True, axis...]
    dot_general x2 -> x4, matrix products: 3.63 us -> 6.75 us  [layer_terms(): lax.dot_general(weight, out_grad, (((2,), (1,)), ((), ())), preferred_ele...]
    ppermute x5, starting transfers between devices: 4.49 us -> 2.2 us  [from_partner(): lax.ppermute(x, axis, [(i, i ^ bit) for i in range(lax.axis_size(axis))])]
    ppermute x2 -> x3, waiting for transfers between devices: 6.61 us -> 4.38 us  [to_later_plane(): return lax.ppermute(x, 'layer', [(i, i + ring) for i in range(ring)])]
    ppermute x2 -> x3, starting transfers between devices: 5.21 us -> 6.39 us  [to_later_plane(): return lax.ppermute(x, 'layer', [(i, i + ring) for i in range(ring)])]
    dot_general x2 -> x3, matrix products: 6.19 us -> 6.36 us  [the longest x1 4.4 us: local(): lax.dot_general(latents, jnp.stack(grads, 0), (((0, 2), (0, 1)), ((), ())...]
  transfers between devices with their start and end apart: 21 -> 23, of which waited for: 16 -> 15; matrix products, arithmetic and copies ran while one was open for 5% -> 10% of each run, Pallas kernels for 0% -> 0%
where the time goes in v5:
time: 144 us; the launch traced here: 142 us
  waiting for transfers between devices  46.9 us (33%)
  starting transfers between devices  39 us (27%)
  blocking collectives  29.5 us (20%)
  matrix products  15.9 us (11%)
  local copies, waits for them, and re-layouts  5.95 us (4%)
  other arithmetic  3.31 us (2%)
    all_to_all x2, blocking collectives, exchanged(): lax.all_to_all(parts, axis, split_axis=0, concat_axis=0, tiled=True, axis...  29.5 us
    ppermute x12, starting transfers between devices, along_ring(): return lax.ppermute(x, 'layer', pairs)  23.3 us
    ppermute x12, waiting for transfers between devices, along_ring(): return lax.ppermute(x, 'layer', pairs)  19.6 us
    ppermute x5, waiting for transfers between devices, from_partner(): lax.ppermute(x, axis, [(i, i ^ bit) for i in range(lax.axis_size(axis))])  11.5 us
    all_to_all x1, waiting for transfers between devices, exchanged(): lax.all_to_all(parts, axis, split_axis=0, concat_axis=0, tiled=True, axis...  8.83 us
    dot_general x4, matrix products, layer_terms(): lax.dot_general(weight, out_grad, (((2,), (1,)), ((), ())), preferred_ele...  6.75 us
    ppermute x3, starting transfers between devices, to_later_plane(): return lax.ppermute(x, 'layer', [(i, i + ring) for i in range(ring)])  6.39 us
    all_to_all x1, starting transfers between devices, exchanged(): lax.all_to_all(parts, axis, split_axis=0, concat_axis=0, tiled=True, axis...  4.53 us
  transfers between devices with their start and end apart: 23, of which 15 were waited for; matrix products, arithmetic and copies ran while one was open for 10% of the time, Pallas kernels for 0%

profile of v5, /device:TPU:2, one launch (start us, length us, event | category | flops | bytes accessed | tf_op | source)
XLA Modules:
  0.0 142.0 jit_solution(7349616709093423509)
XLA Ops:
  1.5 16.3 %all_to_all.15 = bf16[8,24,1024]{2,1,0:T(8,128)(2,1)S(1)} all-to-all(bf16[8,24,1024]{2,1,0:T(8,128)(2,1)S(1)} %broadcast_in_dim.82), channel_id=1, replica_groups={{0,2,4,6,8,10,12,14},{1,3,5,7,9,11,13,15},{16,18,20,22,24,26,28,30},{17..., dimensions={0} | all-to-all | bytes 786432 | tf_op jit(solution)/shard_map/all_to_all | solution.py:16
  17.8 1.7 %collective-permute-done = bf16[192,1024]{1,0:T(8,128)(2,1)S(1)} collective-permute-done((bf16[192,1024]{1,0:T(8,128)(2,1)S(1)}, bf16[192,1024]{1,0:T(8,128)(2,1)S(1)}, u32[]{:S(2)}, u32[]{:S(2)}) %collective-permute-start) | collective-permute-done | bytes 393248 | tf_op jit(solution)/shard_map/ppermute | solution.py:8
  20.7 2.0 %collective-permute-start.1 = (f32[192,256]{1,0:T(8,128)S(1)}, f32[192,256]{1,0:T(8,128)S(1)}, u32[]{:S(2)}, u32[]{:S(2)}) collective-permute-start(f32[192,256]{1,0:T(8,128)S(1)} %constant_dynamic-slice_fusion.1), channel_id=1, source_target_pairs={{0,16},{16,0},{32,48},{48,32},{64,80},{80,64},{96,112},{112,96},{1... | collective-permute-start | bytes 589832 | tf_op jit(solution)/shard_map/ppermute | solution.py:8
  23.4 4.5 %collective-permute-done.1 = f32[192,256]{1,0:T(8,128)S(1)} collective-permute-done((f32[192,256]{1,0:T(8,128)S(1)}, f32[192,256]{1,0:T(8,128)S(1)}, u32[]{:S(2)}, u32[]{:S(2)}) %collective-permute-start.1) | collective-permute-done | bytes 196640 | tf_op jit(solution)/shard_map/ppermute | solution.py:8
  28.1 5.8 %collective-permute-start.3 = (bf16[192,256]{1,0:T(8,128)(2,1)S(1)}, bf16[192,256]{1,0:T(8,128)(2,1)S(1)}, u32[]{:S(2)}, u32[]{:S(2)}) collective-permute-start(bf16[192,256]{1,0:T(8,128)(2,1)S(1)} %get-tuple-element.43), channel_id=1, source_target_pairs={{0,112},{16,0},{32,16},{48,32},{64,48},{80,64},{96,80},{112,96},{1... | collective-permute-start | bytes 294920 | tf_op jit(solution)/shard_map/ppermute | solution.py:25
  33.9 4.1 %collective-permute-start.5 = (bf16[192,256]{1,0:T(8,128)(2,1)S(1)}, bf16[192,256]{1,0:T(8,128)(2,1)S(1)}, u32[]{:S(2)}, u32[]{:S(2)}) collective-permute-start(bf16[192,256]{1,0:T(8,128)(2,1)S(1)} %get-tuple-element.43), channel_id=1, source_target_pairs={{0,96},{16,112},{32,0},{48,16},{64,32},{80,48},{96,64},{112,80},{1... | collective-permute-start | bytes 294920 | tf_op jit(solution)/shard_map/ppermute | solution.py:25
  38.0 4.0 %collective-permute-done.2 = bf16[192,256]{1,0:T(8,128)(2,1)S(1)} collective-permute-done((bf16[192,256]{1,0:T(8,128)(2,1)S(1)}, bf16[192,256]{1,0:T(8,128)(2,1)S(1)}, u32[]{:S(2)}, u32[]{:S(2)}) %collective-permute-start.2) | collective-permute-done | bytes 98336 | tf_op jit(solution)/shard_map/ppermute | solution.py:25
  42.7 2.6 %collective-permute-start.8 = (bf16[3,192,256]{2,1,0:T(8,128)(2,1)}, bf16[3,192,256]{2,1,0:T(8,128)(2,1)S(1)}, u32[]{:S(2)}, u32[]{:S(2)}) collective-permute-start(bf16[3,192,256]{2,1,0:T(8,128)(2,1)} %pad_maximum_fusion.3), channel_id=1, source_target_pairs={{0,128},{16,144},{32,160},{48,176},{64,192},{80,208},{96,224},{112... | collective-permute-start | bytes 884744 | tf_op jit(solution)/shard_map/ppermute | solution.py:30
  47.5 2.1 %collective-permute-start.6 = (bf16[288,256]{1,0:T(8,128)(2,1)}, bf16[288,256]{1,0:T(8,128)(2,1)}, u32[]{:S(2)}, u32[]{:S(2)}) collective-permute-start(bf16[288,256]{1,0:T(8,128)(2,1)} %pad_maximum_fusion.7), channel_id=1, source_target_pairs={{0,32},{16,48},{32,64},{48,80},{64,96},{80,112},{96,0},{112,16},{1... | collective-permute-start | bytes 442376 | tf_op jit(solution)/shard_map/ppermute | solution.py:25
  49.6 1.3 collective-permute-start.9
  50.9 1.8 %collective-permute-done.7 = bf16[288,256]{1,0:T(8,128)(2,1)S(1)} collective-permute-done((bf16[288,256]{1,0:T(8,128)(2,1)}, bf16[288,256]{1,0:T(8,128)(2,1)S(1)}, u32[]{:S(2)}, u32[]{:S(2)}) %collective-permute-start.7) | collective-permute-done | bytes 147488 | tf_op jit(solution)/shard_map/ppermute | solution.py:25
  52.8 3.1 %collective-permute-done.6 = bf16[288,256]{1,0:T(8,128)(2,1)} collective-permute-done((bf16[288,256]{1,0:T(8,128)(2,1)}, bf16[288,256]{1,0:T(8,128)(2,1)}, u32[]{:S(2)}, u32[]{:S(2)}) %collective-permute-start.6) | collective-permute-done | bytes 147488 | tf_op jit(solution)/shard_map/ppermute | solution.py:25
  57.7 2.5 %collective-permute-start.10 = (bf16[3,192,256]{2,1,0:T(8,128)(2,1)S(1)}, bf16[3,192,256]{2,1,0:T(8,128)(2,1)S(1)}, u32[]{:S(2)}, u32[]{:S(2)}) collective-permute-start(bf16[3,192,256]{2,1,0:T(8,128)(2,1)S(1)} %pad_maximum_fusion.4), channel_id=1, source_target_pairs={{0,128},{16,144},{32,160},{48,176},{64,192},{80,208},{96,224},{112... | collective-permute-start | bytes 884744 | tf_op jit(solution)/shard_map/ppermute | solution.py:30
  60.5 4.4 %collective-permute-done.10 = bf16[3,192,256]{2,1,0:T(8,128)(2,1)S(1)} collective-permute-done((bf16[3,192,256]{2,1,0:T(8,128)(2,1)S(1)}, bf16[3,192,256]{2,1,0:T(8,128)(2,1)S(1)}, u32[]{:S(2)}, u32[]{:S(2)}) %collective-permute-start.10) | collective-permute-done | bytes 294944 | tf_op jit(solution)/shard_map/ppermute | solution.py:30
  68.0 13.2 %all_to_all.16 = bf16[8,24,1024]{2,1,0:T(8,128)(2,1)S(1)} all-to-all(bf16[8,24,1024]{2,1,0:T(8,128)(2,1)S(1)} %bitcast.111), channel_id=1, replica_groups={{0,2,4,6,8,10,12,14},{1,3,5,7,9,11,13,15},{16,18,20,22,24,26,28,30},{17..., dimensions={0} | all-to-all | bytes 786432 | tf_op jit(solution)/shard_map/all_to_all | solution.py:16
  82.1 4.5 %all-to-all-start.2 = ((bf16[8,24,1024]{2,1,0:T(8,128)(2,1)}), bf16[8,24,1024]{2,1,0:T(8,128)(2,1)S(1)}, u32[]{:S(2)}, u32[]{:S(2)}) async-start(bf16[8,24,1024]{2,1,0:T(8,128)(2,1)} %broadcast_in_dim.91), calls=%async_computation.2 | async-start | bytes 786432 | tf_op jit(solution)/shard_map/all_to_all | solution.py:16
  86.7 8.8 %all-to-all-done.2 = bf16[8,24,1024]{2,1,0:T(8,128)(2,1)S(1)} async-done(((bf16[8,24,1024]{2,1,0:T(8,128)(2,1)}), bf16[8,24,1024]{2,1,0:T(8,128)(2,1)S(1)}, u32[]{:S(2)}, u32[]{:S(2)}) %all-to-all-start.2) | async-done | bytes 393248 | tf_op jit(solution)/shard_map/all_to_all | solution.py:16
  95.8 2.4 %fusion.33 = bf16[4,192,256]{2,1,0:T(8,128)(2,1)S(1)} fusion(bf16[192,1024,1]{1,0,2:T(8,128)(2,1)S(1)} %bitcast.124, bf16[8,256,1024]{2,1,0:T(8,128)(2,1)} %param.9, pred[4]{0:T(512)(128)(4,1)S(1)} %get-tuple-element.60), kind=kOutput, calls=%fused_computation.21 | convolution fusion | flops 403046400 | bytes 2883588 | tf_op jit(solution)/shard_map/dot_general | solution.py:76
  98.3 2.6 %fusion.36 = bf16[4,192,256]{2,1,0:T(8,128)(2,1)S(1)} fusion(bf16[8,256,1024]{2,1,0:T(8,128)(2,1)} %param.9, bf16[192,1024]{1,0:T(8,128)(2,1)S(1)} %collective-permute-done.12, pred[4]{0:T(512)(128)(4,1)S(1)} %get-tuple-element.60), kind=kOutput, calls=%fused_computation.22 | convolution fusion | flops 403046400 | bytes 2883588 | tf_op jit(solution)/shard_map/dot_general | solution.py:76
  101.3 1.3 collective-permute-start.13
  102.6 1.3 collective-permute-start.14
  105.3 4.4 %bitcast_convert_fusion = bf16[8,256,1024]{2,1,0:T(8,128)(2,1)} fusion(bf16[2,8,192,256]{3,2,1,0:T(8,128)(2,1)S(1)} %copy-done.2, bf16[1,192,1024]{2,1,0:T(8,128)(2,1)S(1)} %bitcast.128, bf16[1,192,1024]{2,1,0:T(8,128)(2,1)S(1)} %bitcast.125), kind=kOutput, calls=%fused_computation | convolution fusion | flops 1613103104 | bytes 6553600 | tf_op jit(solution)/shard_map/dot_general | solution.py:184
  110.6 2.4 %collective-permute-done.13 = bf16[3,192,256]{2,1,0:T(8,128)(2,1)S(1)} collective-permute-done((bf16[3,192,256]{2,1,0:T(8,128)(2,1)S(1)}, bf16[3,192,256]{2,1,0:T(8,128)(2,1)S(1)}, u32[]{:S(2)}, u32[]{:S(2)}) %collective-permute-start.13) | collective-permute-done | bytes 294944 | tf_op jit(solution)/shard_map/ppermute | solution.py:35
  114.1 2.2 %collective-permute-start.15 = (bf16[288,256]{1,0:T(8,128)(2,1)S(1)}, bf16[288,256]{1,0:T(8,128)(2,1)S(1)}, u32[]{:S(2)}, u32[]{:S(2)}) collective-permute-start(bf16[288,256]{1,0:T(8,128)(2,1)S(1)} %pad_maximum_fusion.9), channel_id=1, source_target_pairs={{0,32},{16,48},{32,64},{48,80},{64,96},{80,112},{96,0},{112,16},{1... | collective-permute-start | bytes 442376 | tf_op jit(solution)/shard_map/ppermute | solution.py:25
  116.2 5.5 %collective-permute-done.17 = bf16[288,256]{1,0:T(8,128)(2,1)S(1)} collective-permute-done((bf16[288,256]{1,0:T(8,128)(2,1)S(1)}, bf16[288,256]{1,0:T(8,128)(2,1)S(1)}, u32[]{:S(2)}, u32[]{:S(2)}) %collective-permute-start.17) | collective-permute-done | bytes 147488 | tf_op jit(solution)/shard_map/ppermute | solution.py:25
  121.7 1.1 collective-permute-done.15
  123.2 1.6 %collective-permute-start.16 = (bf16[192,256]{1,0:T(8,128)(2,1)S(1)}, bf16[192,256]{1,0:T(8,128)(2,1)S(1)}, u32[]{:S(2)}, u32[]{:S(2)}) collective-permute-start(bf16[192,256]{1,0:T(8,128)(2,1)S(1)} %get-tuple-element.44), channel_id=1, source_target_pairs={{0,16},{16,32},{32,48},{48,64},{64,80},{80,96},{96,112},{112,0},{1... | collective-permute-start | bytes 294920 | tf_op jit(solution)/shard_map/ppermute | solution.py:25
  124.8 1.7 %collective-permute-start.18 = (bf16[192,256]{1,0:T(8,128)(2,1)S(1)}, bf16[192,256]{1,0:T(8,128)(2,1)S(1)}, u32[]{:S(2)}, u32[]{:S(2)}) collective-permute-start(bf16[192,256]{1,0:T(8,128)(2,1)S(1)} %get-tuple-element.47), channel_id=1, source_target_pairs={{0,112},{16,0},{32,16},{48,32},{64,48},{80,64},{96,80},{112,96},{1... | collective-permute-start | bytes 294920 | tf_op jit(solution)/shard_map/ppermute | solution.py:25
  126.5 4.1 %collective-permute-start.20 = (bf16[192,256]{1,0:T(8,128)(2,1)S(1)}, bf16[192,256]{1,0:T(8,128)(2,1)S(1)}, u32[]{:S(2)}, u32[]{:S(2)}) collective-permute-start(bf16[192,256]{1,0:T(8,128)(2,1)S(1)} %get-tuple-element.45), channel_id=1, source_target_pairs={{0,96},{16,112},{32,0},{48,16},{64,32},{80,48},{96,64},{112,80},{1... | collective-permute-start | bytes 294920 | tf_op jit(solution)/shard_map/ppermute | solution.py:25
  130.7 3.4 %collective-permute-done.19 = bf16[192,256]{1,0:T(8,128)(2,1)S(1)} collective-permute-done((bf16[192,256]{1,0:T(8,128)(2,1)S(1)}, bf16[192,256]{1,0:T(8,128)(2,1)S(1)}, u32[]{:S(2)}, u32[]{:S(2)}) %collective-permute-start.19) | collective-permute-done | bytes 98336 | tf_op jit(solution)/shard_map/ppermute | solution.py:25
  135.0 4.6 %collective-permute-done.21 = bf16[192,256]{1,0:T(8,128)(2,1)S(1)} collective-permute-done((bf16[192,256]{1,0:T(8,128)(2,1)S(1)}, bf16[192,256]{1,0:T(8,128)(2,1)S(1)}, u32[]{:S(2)}, u32[]{:S(2)}) %collective-permute-start.21) | collective-permute-done | bytes 98336 | tf_op jit(solution)/shard_map/ppermute | solution.py:8
  139.6 2.4 %fusion.53 = f32[1024,256]{1,0:T(8,128)} fusion(bf16[192,1024]{1,0:T(8,128)(2,1)} %copy-done.6, bf16[192,1024]{1,0:T(8,128)(2,1)S(1)} %bitcast.122, bf16[192,256]{1,0:T(8,128)(2,1)S(1)} %get-tuple-element.56, bf16[192,256]{1,0:T(8,128)(2,1)S(1)} %get-tuple-element.55), kind=kOutput, calls=%fused_computation.35 | convolution fusion | flops 203292672 | bytes 2031616 | tf_op jit(solution)/shard_map/dot_general | solution.py:197
  (98 shorter events, 16.7 us)
Async XLA Ops:
  0.6 19.7 %copy-start = (bf16[1024,256]{1,0:T(8,128)(2,1)S(1)}, bf16[1024,256]{1,0:T(8,128)(2,1)}, u32[]{:S(2)}) copy-start(bf16[1024,256]{1,0:T(8,128)(2,1)} %param.7) | copy-start | bytes 1572868
  17.8 1.7 %collective-permute-start = (bf16[192,1024]{1,0:T(8,128)(2,1)S(1)}, bf16[192,1024]{1,0:T(8,128)(2,1)S(1)}, u32[]{:S(2)}, u32[]{:S(2)}) collective-permute-start(bf16[192,1024]{1,0:T(8,128)(2,1)S(1)} %bitcast.120), channel_id=1, source_target_pairs={{0,1},{1,0},{2,3},{3,2},{4,5},{5,4},{6,7},{7,6},{8,9},{9,8},{10,11... | collective-permute-start | bytes 1179656 | tf_op jit(solution)/shard_map/ppermute | solution.py:8
  19.5 0.7 copy-start.6
  20.7 7.2 %collective-permute-start.1 = (f32[192,256]{1,0:T(8,128)S(1)}, f32[192,256]{1,0:T(8,128)S(1)}, u32[]{:S(2)}, u32[]{:S(2)}) collective-permute-start(f32[192,256]{1,0:T(8,128)S(1)} %constant_dynamic-slice_fusion.1), channel_id=1, source_target_pairs={{0,16},{16,0},{32,48},{48,32},{64,80},{80,64},{96,112},{112,96},{1... | collective-permute-start | bytes 589832 | tf_op jit(solution)/shard_map/ppermute | solution.py:8
  28.1 9.9 %collective-permute-start.3 = (bf16[192,256]{1,0:T(8,128)(2,1)S(1)}, bf16[192,256]{1,0:T(8,128)(2,1)S(1)}, u32[]{:S(2)}, u32[]{:S(2)}) collective-permute-start(bf16[192,256]{1,0:T(8,128)(2,1)S(1)} %get-tuple-element.43), channel_id=1, source_target_pairs={{0,112},{16,0},{32,16},{48,32},{64,48},{80,64},{96,80},{112,96},{1... | collective-permute-start | bytes 294920 | tf_op jit(solution)/shard_map/ppermute | solution.py:25
  33.9 8.1 %collective-permute-start.2 = (bf16[192,256]{1,0:T(8,128)(2,1)S(1)}, bf16[192,256]{1,0:T(8,128)(2,1)S(1)}, u32[]{:S(2)}, u32[]{:S(2)}) collective-permute-start(bf16[192,256]{1,0:T(8,128)(2,1)S(1)} %get-tuple-element.43), channel_id=1, source_target_pairs={{0,16},{16,32},{32,48},{48,64},{64,80},{80,96},{96,112},{112,0},{1... | collective-permute-start | bytes 294920 | tf_op jit(solution)/shard_map/ppermute | solution.py:25
  33.9 11.4 %collective-permute-start.4 = (bf16[192,256]{1,0:T(8,128)(2,1)S(1)}, bf16[192,256]{1,0:T(8,128)(2,1)S(1)}, u32[]{:S(2)}, u32[]{:S(2)}) collective-permute-start(bf16[192,256]{1,0:T(8,128)(2,1)S(1)} %get-tuple-element.43), channel_id=1, source_target_pairs={{0,32},{16,48},{32,64},{48,80},{64,96},{80,112},{96,0},{112,16},{1... | collective-permute-start | bytes 294920 | tf_op jit(solution)/shard_map/ppermute | solution.py:25
  33.9 11.4 %collective-permute-start.5 = (bf16[192,256]{1,0:T(8,128)(2,1)S(1)}, bf16[192,256]{1,0:T(8,128)(2,1)S(1)}, u32[]{:S(2)}, u32[]{:S(2)}) collective-permute-start(bf16[192,256]{1,0:T(8,128)(2,1)S(1)} %get-tuple-element.43), channel_id=1, source_target_pairs={{0,96},{16,112},{32,0},{48,16},{64,32},{80,48},{96,64},{112,80},{1... | collective-permute-start | bytes 294920 | tf_op jit(solution)/shard_map/ppermute | solution.py:25
  42.7 14.9 %collective-permute-start.8 = (bf16[3,192,256]{2,1,0:T(8,128)(2,1)}, bf16[3,192,256]{2,1,0:T(8,128)(2,1)S(1)}, u32[]{:S(2)}, u32[]{:S(2)}) collective-permute-start(bf16[3,192,256]{2,1,0:T(8,128)(2,1)} %pad_maximum_fusion.3), channel_id=1, source_target_pairs={{0,128},{16,144},{32,160},{48,176},{64,192},{80,208},{96,224},{112... | collective-permute-start | bytes 884744 | tf_op jit(solution)/shard_map/ppermute | solution.py:30
  46.0 6.8 %collective-permute-start.7 = (bf16[288,256]{1,0:T(8,128)(2,1)}, bf16[288,256]{1,0:T(8,128)(2,1)S(1)}, u32[]{:S(2)}, u32[]{:S(2)}) collective-permute-start(bf16[288,256]{1,0:T(8,128)(2,1)} %pad_maximum_fusion.8), channel_id=1, source_target_pairs={{0,96},{16,112},{32,0},{48,16},{64,32},{80,48},{96,64},{112,80},{1... | collective-permute-start | bytes 442376 | tf_op jit(solution)/shard_map/ppermute | solution.py:25
  47.5 8.5 %collective-permute-start.6 = (bf16[288,256]{1,0:T(8,128)(2,1)}, bf16[288,256]{1,0:T(8,128)(2,1)}, u32[]{:S(2)}, u32[]{:S(2)}) collective-permute-start(bf16[288,256]{1,0:T(8,128)(2,1)} %pad_maximum_fusion.7), channel_id=1, source_target_pairs={{0,32},{16,48},{32,64},{48,80},{64,96},{80,112},{96,0},{112,16},{1... | collective-permute-start | bytes 442376 | tf_op jit(solution)/shard_map/ppermute | solution.py:25
  49.6 10.7 %collective-permute-start.9 = (bf16[2,192,256]{2,1,0:T(8,128)(2,1)S(1)}, bf16[2,192,256]{2,1,0:T(8,128)(2,1)S(1)}, u32[]{:S(2)}, u32[]{:S(2)}) collective-permute-start(bf16[2,192,256]{2,1,0:T(8,128)(2,1)S(1)} %pad_maximum_fusion.6), channel_id=1, source_target_pairs={{0,128},{16,144},{32,160},{48,176},{64,192},{80,208},{96,224},{112... | collective-permute-start | bytes 589832 | tf_op jit(solution)/shard_map/ppermute | solution.py:30
  57.7 7.1 %collective-permute-start.10 = (bf16[3,192,256]{2,1,0:T(8,128)(2,1)S(1)}, bf16[3,192,256]{2,1,0:T(8,128)(2,1)S(1)}, u32[]{:S(2)}, u32[]{:S(2)}) collective-permute-start(bf16[3,192,256]{2,1,0:T(8,128)(2,1)S(1)} %pad_maximum_fusion.4), channel_id=1, source_target_pairs={{0,128},{16,144},{32,160},{48,176},{64,192},{80,208},{96,224},{112... | collective-permute-start | bytes 884744 | tf_op jit(solution)/shard_map/ppermute | solution.py:30
  60.4 4.7 %copy-start.4 = (bf16[8,256,1024]{2,1,0:T(8,128)(2,1)S(1)}, bf16[8,256,1024]{2,1,0:T(8,128)(2,1)}, u32[]{:S(2)}) copy-start(bf16[8,256,1024]{2,1,0:T(8,128)(2,1)} %param.9) | copy-start | bytes 12582916
  65.1 1.1 copy-start.1
  66.1 1.8 %collective-permute-start.11 = (bf16[192,1024]{1,0:T(8,128)(2,1)S(1)}, bf16[192,1024]{1,0:T(8,128)(2,1)S(1)}, u32[]{:S(2)}, u32[]{:S(2)}) collective-permute-start(bf16[192,1024]{1,0:T(8,128)(2,1)S(1)} %fusion.20), channel_id=1, source_target_pairs={{0,1},{1,0},{2,3},{3,2},{4,5},{5,4},{6,7},{7,6},{8,9},{9,8},{10,11... | collective-permute-start | bytes 1179656 | tf_op jit(solution)/shard_map/ppermute | solution.py:8
  67.3 14.0 %copy-start.3 = (bf16[24,1024]{1,0:T(8,128)(2,1)S(1)}, bf16[24,1024]{1,0:T(8,128)(2,1)}, u32[]{:S(2)}) copy-start(bf16[24,1024]{1,0:T(8,128)(2,1)} %param.6) | copy-start | bytes 147460
  82.1 13.4 %all-to-all-start.2 = ((bf16[8,24,1024]{2,1,0:T(8,128)(2,1)}), bf16[8,24,1024]{2,1,0:T(8,128)(2,1)S(1)}, u32[]{:S(2)}, u32[]{:S(2)}) async-start(bf16[8,24,1024]{2,1,0:T(8,128)(2,1)} %broadcast_in_dim.91), calls=%async_computation.2 | async-start | bytes 786432 | tf_op jit(solution)/shard_map/all_to_all | solution.py:16
  95.5 2.8 %collective-permute-start.12 = (bf16[192,1024]{1,0:T(8,128)(2,1)S(1)}, bf16[192,1024]{1,0:T(8,128)(2,1)S(1)}, u32[]{:S(2)}, u32[]{:S(2)}) collective-permute-start(bf16[192,1024]{1,0:T(8,128)(2,1)S(1)} %bitcast.123), channel_id=1, source_target_pairs={{0,1},{1,0},{2,3},{3,2},{4,5},{5,4},{6,7},{7,6},{8,9},{9,8},{10,11... | collective-permute-start | bytes 1179656 | tf_op jit(solution)/shard_map/ppermute | solution.py:8
  98.3 2.6 %copy-start.7 = (bf16[192,1024]{1,0:T(8,128)(2,1)}, bf16[192,1024]{1,0:T(8,128)(2,1)S(1)}, u32[]{:S(2)}) copy-start(bf16[192,1024]{1,0:T(8,128)(2,1)S(1)} %collective-permute-done.12) | copy-start | bytes 1179652
  98.3 5.6 %copy-start.5 = (bf16[8,256,1024]{2,1,0:T(8,128)(2,1)S(1)}, bf16[8,256,1024]{2,1,0:T(8,128)(2,1)}, u32[]{:S(2)}) copy-start(bf16[8,256,1024]{2,1,0:T(8,128)(2,1)} %param.9) | copy-start | bytes 12582916
  101.0 2.9 %copy-start.8 = (bf16[192,1024]{1,0:T(8,128)(2,1)S(1)}, bf16[192,1024]{1,0:T(8,128)(2,1)}, u32[]{:S(2)}) copy-start(bf16[192,1024]{1,0:T(8,128)(2,1)} %copy-done.7) | copy-start | bytes 1179652
  101.3 11.7 %collective-permute-start.13 = (bf16[3,192,256]{2,1,0:T(8,128)(2,1)S(1)}, bf16[3,192,256]{2,1,0:T(8,128)(2,1)S(1)}, u32[]{:S(2)}, u32[]{:S(2)}) collective-permute-start(bf16[3,192,256]{2,1,0:T(8,128)(2,1)S(1)} %pad_maximum_fusion.5), channel_id=1, source_target_pairs={{128,0},{144,16},{160,32},{176,48},{192,64},{208,80},{224,96},{240... | collective-permute-start | bytes 884744 | tf_op jit(solution)/shard_map/ppermute | solution.py:35
  102.6 20.4 %collective-permute-start.14 = (bf16[5,192,256]{2,1,0:T(8,128)(2,1)S(1)}, bf16[5,192,256]{2,1,0:T(8,128)(2,1)S(1)}, u32[]{:S(2)}, u32[]{:S(2)}) collective-permute-start(bf16[5,192,256]{2,1,0:T(8,128)(2,1)S(1)} %get-tuple-element.52), channel_id=1, source_target_pairs={{128,0},{144,16},{160,32},{176,48},{192,64},{208,80},{224,96},{240... | collective-permute-start | bytes 1474568 | tf_op jit(solution)/shard_map/ppermute | solution.py:35
  103.9 1.4 copy-start.2
  113.1 8.6 %collective-permute-start.17 = (bf16[288,256]{1,0:T(8,128)(2,1)S(1)}, bf16[288,256]{1,0:T(8,128)(2,1)S(1)}, u32[]{:S(2)}, u32[]{:S(2)}) collective-permute-start(bf16[288,256]{1,0:T(8,128)(2,1)S(1)} %pad_maximum_fusion.10), channel_id=1, source_target_pairs={{0,96},{16,112},{32,0},{48,16},{64,32},{80,48},{96,64},{112,80},{1... | collective-permute-start | bytes 442376 | tf_op jit(solution)/shard_map/ppermute | solution.py:25
  114.1 8.8 %collective-permute-start.15 = (bf16[288,256]{1,0:T(8,128)(2,1)S(1)}, bf16[288,256]{1,0:T(8,128)(2,1)S(1)}, u32[]{:S(2)}, u32[]{:S(2)}) collective-permute-start(bf16[288,256]{1,0:T(8,128)(2,1)S(1)} %pad_maximum_fusion.9), channel_id=1, source_target_pairs={{0,32},{16,48},{32,64},{48,80},{64,96},{80,112},{96,0},{112,16},{1... | collective-permute-start | bytes 442376 | tf_op jit(solution)/shard_map/ppermute | solution.py:25
  123.2 7.5 %collective-permute-start.16 = (bf16[192,256]{1,0:T(8,128)(2,1)S(1)}, bf16[192,256]{1,0:T(8,128)(2,1)S(1)}, u32[]{:S(2)}, u32[]{:S(2)}) collective-permute-start(bf16[192,256]{1,0:T(8,128)(2,1)S(1)} %get-tuple-element.44), channel_id=1, source_target_pairs={{0,16},{16,32},{32,48},{48,64},{64,80},{80,96},{96,112},{112,0},{1... | collective-permute-start | bytes 294920 | tf_op jit(solution)/shard_map/ppermute | solution.py:25
  124.8 5.9 %collective-permute-start.18 = (bf16[192,256]{1,0:T(8,128)(2,1)S(1)}, bf16[192,256]{1,0:T(8,128)(2,1)S(1)}, u32[]{:S(2)}, u32[]{:S(2)}) collective-permute-start(bf16[192,256]{1,0:T(8,128)(2,1)S(1)} %get-tuple-element.47), channel_id=1, source_target_pairs={{0,112},{16,0},{32,16},{48,32},{64,48},{80,64},{96,80},{112,96},{1... | collective-permute-start | bytes 294920 | tf_op jit(solution)/shard_map/ppermute | solution.py:25
  126.5 7.5 %collective-permute-start.19 = (bf16[192,256]{1,0:T(8,128)(2,1)S(1)}, bf16[192,256]{1,0:T(8,128)(2,1)S(1)}, u32[]{:S(2)}, u32[]{:S(2)}) collective-permute-start(bf16[192,256]{1,0:T(8,128)(2,1)S(1)} %get-tuple-element.46), channel_id=1, source_target_pairs={{0,32},{16,48},{32,64},{48,80},{64,96},{80,112},{96,0},{112,16},{1... | collective-permute-start | bytes 294920 | tf_op jit(solution)/shard_map/ppermute | solution.py:25
  126.5 8.2 %collective-permute-start.20 = (bf16[192,256]{1,0:T(8,128)(2,1)S(1)}, bf16[192,256]{1,0:T(8,128)(2,1)S(1)}, u32[]{:S(2)}, u32[]{:S(2)}) collective-permute-start(bf16[192,256]{1,0:T(8,128)(2,1)S(1)} %get-tuple-element.45), channel_id=1, source_target_pairs={{0,96},{16,112},{32,0},{48,16},{64,32},{80,48},{96,64},{112,80},{1... | collective-permute-start | bytes 294920 | tf_op jit(solution)/shard_map/ppermute | solution.py:25
  134.9 4.7 %collective-permute-start.21 = (bf16[192,256]{1,0:T(8,128)(2,1)S(1)}, bf16[192,256]{1,0:T(8,128)(2,1)S(1)}, u32[]{:S(2)}, u32[]{:S(2)}) collective-permute-start(bf16[192,256]{1,0:T(8,128)(2,1)S(1)} %fusion.69), channel_id=1, source_target_pairs={{0,16},{16,0},{32,48},{48,32},{64,80},{80,64},{96,112},{112,96},{1... | collective-permute-start | bytes 294920 | tf_op jit(solution)/shard_map/ppermute | solution.py:8

commit v6 on v4

--- a/solution.py
+++ b/solution.py
@@ -59,6 +59,7 @@
         3: ahead[: 2 * half],
         4: jnp.concatenate([behind[2 * half :], ahead[2 * half :]], 0),
     }
+    far, near_crossed = lax.optimization_barrier((far, near_crossed))
     far_order = list(far)
     far_crossed = to_later_plane(jnp.stack([far[d] for d in far_order], 0))
     for blocks, crossed, order in (
@@ -122,13 +123,14 @@
     return jnp.concatenate([own, other], 0)
 
 
-def rows_summed(x):
+def rows_summed(own, other):
     size = lax.axis_size("latent")
     chips = size // 2
-    half = x.shape[0] // 2
-    theirs = from_partner(x[half:].astype(jnp.bfloat16), "latent", 1)
-    both = (x[:half] + theirs.astype(jnp.float32)).astype(jnp.bfloat16)
-    parts = both.reshape(chips, half // chips, x.shape[1])
+    half = own.shape[0]
+    theirs = from_partner(other.astype(jnp.bfloat16), "latent", 1)
+    own, theirs = lax.optimization_barrier((own, theirs))
+    both = (own + theirs.astype(jnp.float32)).astype(jnp.bfloat16)
+    parts = both.reshape(chips, half // chips, own.shape[1])
     arrived = exchanged(parts, "latent", same_core_groups(size))
     return arrived.astype(jnp.float32).sum(axis=0)
 
@@ -158,10 +160,14 @@
     used = lax.broadcasted_iota(jnp.int32, (layer_count, 1, 1), 0) <= layer_now
     latents = jnp.where(used, gathered, jnp.zeros_like(gathered))
 
-    recon = lax.dot_general(
-        latents, dec_weight, (((0, 2), (0, 1)), ((), ())), preferred_element_type=jnp.float32
-    )
-    recon_own = rows_summed(recon)
+    def decoded(part):
+        return lax.dot_general(
+            part, dec_weight, (((0, 2), (0, 1)), ((), ())), preferred_element_type=jnp.float32
+        )
+
+    recon_own = rows_summed(
+        decoded(latents[:, :half_rows]), decoded(latents[:, half_rows:])
+    )
     rscale = total_rows ** (-0.5)
     grad_own = ((recon_own - mlp_outputs.astype(jnp.float32)) * rscale).astype(jnp.bfloat16)
     out_grad = rows_of_all(grad_own)

time: 139 us -> 138 us (level)
  waiting for transfers between devices: 42.9 us -> 41.3 us
    ppermute x2, waiting for transfers between devices: 6.61 us -> 3.98 us  [to_later_plane(): return lax.ppermute(x, 'layer', [(i, i + ring) for i in range(ring)])]
    ppermute x12, waiting for transfers between devices: 20.9 us -> 22.9 us  [along_ring(): return lax.ppermute(x, 'layer', pairs)]
  transfers between devices with their start and end apart: 21 -> 21, of which waited for: 16 -> 14; matrix products, arithmetic and copies ran while one was open for 5% -> 6% of each run, Pallas kernels for 0% -> 0%
where the time goes in v6:
time: 138 us; the launch traced here: 137 us
  blocking collectives  42.3 us (31%)
  waiting for transfers between devices  41.3 us (30%)
  starting transfers between devices  36.8 us (27%)
  matrix products  11.8 us (9%)
  local copies, waits for them, and re-layouts  3.06 us (2%)
    all_to_all x3, blocking collectives, exchanged(): lax.all_to_all(parts, axis, split_axis=0, concat_axis=0, tiled=True, axis...  42.3 us
    ppermute x12, starting transfers between devices, along_ring(): return lax.ppermute(x, 'layer', pairs)  23.5 us
    ppermute x12, waiting for transfers between devices, along_ring(): return lax.ppermute(x, 'layer', pairs)  22.9 us
    ppermute x5, waiting for transfers between devices, from_partner(): lax.ppermute(x, axis, [(i, i ^ bit) for i in range(lax.axis_size(axis))])  11.2 us
    ppermute x2, starting transfers between devices, to_later_plane(): return lax.ppermute(x, 'layer', [(i, i + ring) for i in range(ring)])  5.97 us
    dot_general x1, matrix products, local(): lax.dot_general(latents, grad_after, (((1,), (0,)), ((), ())), preferred_...  4.4 us
    ppermute x5, starting transfers between devices, from_partner(): lax.ppermute(x, axis, [(i, i ^ bit) for i in range(lax.axis_size(axis))])  4.33 us
    ppermute x2, waiting for transfers between devices, to_later_plane(): return lax.ppermute(x, 'layer', [(i, i + ring) for i in range(ring)])  3.98 us
  transfers between devices with their start and end apart: 21, of which 14 were waited for; matrix products, arithmetic and copies ran while one was open for 6% of the time, Pallas kernels for 0%

profile of v6, /device:TPU:2, one launch (start us, length us, event | category | flops | bytes accessed | tf_op | source)
XLA Modules:
  0.0 137.4 jit_solution(1439120089191477693)
XLA Ops:
  1.5 16.3 %all_to_all.15 = bf16[8,24,1024]{2,1,0:T(8,128)(2,1)S(1)} all-to-all(bf16[8,24,1024]{2,1,0:T(8,128)(2,1)S(1)} %broadcast_in_dim.72), channel_id=1, replica_groups={{0,2,4,6,8,10,12,14},{1,3,5,7,9,11,13,15},{16,18,20,22,24,26,28,30},{17..., dimensions={0} | all-to-all | bytes 786432 | tf_op jit(solution)/shard_map/all_to_all | solution.py:16
  17.8 1.7 %collective-permute-done = bf16[192,1024]{1,0:T(8,128)(2,1)S(1)} collective-permute-done((bf16[192,1024]{1,0:T(8,128)(2,1)S(1)}, bf16[192,1024]{1,0:T(8,128)(2,1)S(1)}, u32[]{:S(2)}, u32[]{:S(2)}) %collective-permute-start) | collective-permute-done | bytes 393248 | tf_op jit(solution)/shard_map/ppermute | solution.py:8
  20.7 2.0 %collective-permute-start.1 = (f32[192,256]{1,0:T(8,128)S(1)}, f32[192,256]{1,0:T(8,128)S(1)}, u32[]{:S(2)}, u32[]{:S(2)}) collective-permute-start(f32[192,256]{1,0:T(8,128)S(1)} %constant_dynamic-slice_fusion.4), channel_id=1, source_target_pairs={{0,16},{16,0},{32,48},{48,32},{64,80},{80,64},{96,112},{112,96},{1... | collective-permute-start | bytes 589832 | tf_op jit(solution)/shard_map/ppermute | solution.py:8
  23.4 4.5 %collective-permute-done.1 = f32[192,256]{1,0:T(8,128)S(1)} collective-permute-done((f32[192,256]{1,0:T(8,128)S(1)}, f32[192,256]{1,0:T(8,128)S(1)}, u32[]{:S(2)}, u32[]{:S(2)}) %collective-permute-start.1) | collective-permute-done | bytes 196640 | tf_op jit(solution)/shard_map/ppermute | solution.py:8
  27.9 5.8 %collective-permute-start.5 = (bf16[192,256]{1,0:T(8,128)(2,1)S(1)}, bf16[192,256]{1,0:T(8,128)(2,1)S(1)}, u32[]{:S(2)}, u32[]{:S(2)}) collective-permute-start(bf16[192,256]{1,0:T(8,128)(2,1)S(1)} %get-tuple-element.25), channel_id=1, source_target_pairs={{0,112},{16,0},{32,16},{48,32},{64,48},{80,64},{96,80},{112,96},{1... | collective-permute-start | bytes 294920 | tf_op jit(solution)/shard_map/ppermute | solution.py:25
  33.7 1.5 %collective-permute-start.6 = (bf16[192,256]{1,0:T(8,128)(2,1)S(1)}, bf16[192,256]{1,0:T(8,128)(2,1)S(1)}, u32[]{:S(2)}, u32[]{:S(2)}) collective-permute-start(bf16[192,256]{1,0:T(8,128)(2,1)S(1)} %get-tuple-element.25), channel_id=1, source_target_pairs={{0,96},{16,112},{32,0},{48,16},{64,32},{80,48},{96,64},{112,80},{1... | collective-permute-start | bytes 294920 | tf_op jit(solution)/shard_map/ppermute | solution.py:25
  35.2 1.5 %collective-permute-start.3 = (bf16[192,256]{1,0:T(8,128)(2,1)S(1)}, bf16[192,256]{1,0:T(8,128)(2,1)S(1)}, u32[]{:S(2)}, u32[]{:S(2)}) collective-permute-start(bf16[192,256]{1,0:T(8,128)(2,1)S(1)} %get-tuple-element.25), channel_id=1, source_target_pairs={{0,32},{16,48},{32,64},{48,80},{64,96},{80,112},{96,0},{112,16},{1... | collective-permute-start | bytes 294920 | tf_op jit(solution)/shard_map/ppermute | solution.py:25
  37.8 6.7 %collective-permute-done.2 = bf16[192,256]{1,0:T(8,128)(2,1)S(1)} collective-permute-done((bf16[192,256]{1,0:T(8,128)(2,1)S(1)}, bf16[192,256]{1,0:T(8,128)(2,1)S(1)}, u32[]{:S(2)}, u32[]{:S(2)}) %collective-permute-start.2) | collective-permute-done | bytes 98336 | tf_op jit(solution)/shard_map/ppermute | solution.py:25
  44.5 2.6 %collective-permute-start.8 = (bf16[5,192,256]{2,1,0:T(8,128)(2,1)S(1)}, bf16[5,192,256]{2,1,0:T(8,128)(2,1)S(1)}, u32[]{:S(2)}, u32[]{:S(2)}) collective-permute-start(bf16[5,192,256]{2,1,0:T(8,128)(2,1)S(1)} %bitcast_dynamic-update-slice_fusion.1), channel_id=1, source_target_pairs={{0,128},{16,144},{32,160},{48,176},{64,192},{80,208},{96,224},{112... | collective-permute-start | bytes 1474568 | tf_op jit(solution)/shard_map/ppermute | solution.py:30
  47.3 4.2 %collective-permute-start.7 = (bf16[288,256]{1,0:T(8,128)(2,1)S(1)}, bf16[288,256]{1,0:T(8,128)(2,1)S(1)}, u32[]{:S(2)}, u32[]{:S(2)}) collective-permute-start(bf16[288,256]{1,0:T(8,128)(2,1)S(1)} %pad_maximum_fusion.7), channel_id=1, source_target_pairs={{0,96},{16,112},{32,0},{48,16},{64,32},{80,48},{96,64},{112,80},{1... | collective-permute-start | bytes 442376 | tf_op jit(solution)/shard_map/ppermute | solution.py:25
  51.7 5.0 %collective-permute-done.4 = bf16[288,256]{1,0:T(8,128)(2,1)S(1)} collective-permute-done((bf16[288,256]{1,0:T(8,128)(2,1)S(1)}, bf16[288,256]{1,0:T(8,128)(2,1)S(1)}, u32[]{:S(2)}, u32[]{:S(2)}) %collective-permute-start.4) | collective-permute-done | bytes 147488 | tf_op jit(solution)/shard_map/ppermute | solution.py:25
  56.8 3.4 %collective-permute-start.9 = (bf16[3,192,256]{2,1,0:T(8,128)(2,1)S(1)}, bf16[3,192,256]{2,1,0:T(8,128)(2,1)S(1)}, u32[]{:S(2)}, u32[]{:S(2)}) collective-permute-start(bf16[3,192,256]{2,1,0:T(8,128)(2,1)S(1)} %pad_maximum_fusion.4), channel_id=1, source_target_pairs={{0,128},{16,144},{32,160},{48,176},{64,192},{80,208},{96,224},{112... | collective-permute-start | bytes 884744 | tf_op jit(solution)/shard_map/ppermute | solution.py:30
  60.4 4.0 %collective-permute-done.9 = bf16[3,192,256]{2,1,0:T(8,128)(2,1)S(1)} collective-permute-done((bf16[3,192,256]{2,1,0:T(8,128)(2,1)S(1)}, bf16[3,192,256]{2,1,0:T(8,128)(2,1)S(1)}, u32[]{:S(2)}, u32[]{:S(2)}) %collective-permute-start.9) | collective-permute-done | bytes 294944 | tf_op jit(solution)/shard_map/ppermute | solution.py:30
  67.6 13.6 %all_to_all.16 = bf16[8,24,1024]{2,1,0:T(8,128)(2,1)S(1)} all-to-all(bf16[8,24,1024]{2,1,0:T(8,128)(2,1)S(1)} %bitcast.98), channel_id=1, replica_groups={{0,2,4,6,8,10,12,14},{1,3,5,7,9,11,13,15},{16,18,20,22,24,26,28,30},{17..., dimensions={0} | all-to-all | bytes 786432 | tf_op jit(solution)/shard_map/all_to_all | solution.py:16
  81.4 12.4 %all_to_all.17 = bf16[8,24,1024]{2,1,0:T(8,128)(2,1)S(1)} all-to-all(bf16[8,24,1024]{2,1,0:T(8,128)(2,1)S(1)} %broadcast_in_dim.80), channel_id=1, replica_groups={{0,2,4,6,8,10,12,14},{1,3,5,7,9,11,13,15},{16,18,20,22,24,26,28,30},{17..., dimensions={0} | all-to-all | bytes 786432 | tf_op jit(solution)/shard_map/all_to_all | solution.py:16
  93.8 1.6 %collective-permute-done.11 = bf16[192,1024]{1,0:T(8,128)(2,1)S(1)} collective-permute-done((bf16[192,1024]{1,0:T(8,128)(2,1)S(1)}, bf16[192,1024]{1,0:T(8,128)(2,1)S(1)}, u32[]{:S(2)}, u32[]{:S(2)}) %collective-permute-start.11) | collective-permute-done | bytes 393248 | tf_op jit(solution)/shard_map/ppermute | solution.py:8
  95.5 2.6 %fusion.8 = bf16[4,384,256]{2,1,0:T(8,128)(2,1)S(1)} fusion(bf16[8,256,1024]{2,1,0:T(8,128)(2,1)} %param.9, pred[4]{0:T(512)(128)(4,1)S(1)} %get-tuple-element.42, bf16[192,1024]{1,0:T(8,128)(2,1)S(1)} %collective-permute-done.11, bf16[192,1024]{1,0:T(8,128)(2,1)S(1)} %bitcast.97), kind=kOutput, calls=%fused_computation.8 | convolution fusion | flops 807665664 | bytes 3670020 | tf_op jit(solution)/shard_map/dot_general | solution.py:76
  98.3 1.3 collective-permute-start.12
  99.6 1.7 %collective-permute-start.13 = (bf16[5,192,256]{2,1,0:T(8,128)(2,1)S(1)}, bf16[5,192,256]{2,1,0:T(8,128)(2,1)S(1)}, u32[]{:S(2)}, u32[]{:S(2)}) collective-permute-start(bf16[5,192,256]{2,1,0:T(8,128)(2,1)S(1)} %get-tuple-element.34), channel_id=1, source_target_pairs={{128,0},{144,16},{160,32},{176,48},{192,64},{208,80},{224,96},{240... | collective-permute-start | bytes 1474568 | tf_op jit(solution)/shard_map/ppermute | solution.py:35
  101.3 4.4 %convolution_convert_fusion = bf16[8,256,1024]{2,1,0:T(8,128)(2,1)} fusion(bf16[8,384,256]{2,1,0:T(8,128)(2,1)S(1)} %bitcast_select_fusion, bf16[384,1024]{1,0:T(8,128)(2,1)S(1)} %pad_maximum_fusion.1), kind=kOutput, calls=%fused_computation | convolution fusion | flops 1612709888 | bytes 6553600 | tf_op jit(solution)/shard_map/dot_general | solution.py:180
  106.8 3.3 %collective-permute-done.12 = bf16[3,192,256]{2,1,0:T(8,128)(2,1)S(1)} collective-permute-done((bf16[3,192,256]{2,1,0:T(8,128)(2,1)S(1)}, bf16[3,192,256]{2,1,0:T(8,128)(2,1)S(1)}, u32[]{:S(2)}, u32[]{:S(2)}) %collective-permute-start.12) | collective-permute-done | bytes 294944 | tf_op jit(solution)/shard_map/ppermute | solution.py:35
  110.2 1.6 %collective-permute-start.16 = (bf16[288,256]{1,0:T(8,128)(2,1)S(1)}, bf16[288,256]{1,0:T(8,128)(2,1)S(1)}, u32[]{:S(2)}, u32[]{:S(2)}) collective-permute-start(bf16[288,256]{1,0:T(8,128)(2,1)S(1)} %pad_maximum_fusion.9), channel_id=1, source_target_pairs={{0,96},{16,112},{32,0},{48,16},{64,32},{80,48},{96,64},{112,80},{1... | collective-permute-start | bytes 442376 | tf_op jit(solution)/shard_map/ppermute | solution.py:25
  111.7 1.5 %collective-permute-start.14 = (bf16[288,256]{1,0:T(8,128)(2,1)S(1)}, bf16[288,256]{1,0:T(8,128)(2,1)S(1)}, u32[]{:S(2)}, u32[]{:S(2)}) collective-permute-start(bf16[288,256]{1,0:T(8,128)(2,1)S(1)} %pad_maximum_fusion.8), channel_id=1, source_target_pairs={{0,32},{16,48},{32,64},{48,80},{64,96},{80,112},{96,0},{112,16},{1... | collective-permute-start | bytes 442376 | tf_op jit(solution)/shard_map/ppermute | solution.py:25
  113.3 4.3 %collective-permute-done.16 = bf16[288,256]{1,0:T(8,128)(2,1)S(1)} collective-permute-done((bf16[288,256]{1,0:T(8,128)(2,1)S(1)}, bf16[288,256]{1,0:T(8,128)(2,1)S(1)}, u32[]{:S(2)}, u32[]{:S(2)}) %collective-permute-start.16) | collective-permute-done | bytes 147488 | tf_op jit(solution)/shard_map/ppermute | solution.py:25
  117.5 3.5 %collective-permute-done.14 = bf16[288,256]{1,0:T(8,128)(2,1)S(1)} collective-permute-done((bf16[288,256]{1,0:T(8,128)(2,1)S(1)}, bf16[288,256]{1,0:T(8,128)(2,1)S(1)}, u32[]{:S(2)}, u32[]{:S(2)}) %collective-permute-start.14) | collective-permute-done | bytes 147488 | tf_op jit(solution)/shard_map/ppermute | solution.py:25
  121.2 2.2 %collective-permute-start.15 = (bf16[192,256]{1,0:T(8,128)(2,1)S(1)}, bf16[192,256]{1,0:T(8,128)(2,1)S(1)}, u32[]{:S(2)}, u32[]{:S(2)}) collective-permute-start(bf16[192,256]{1,0:T(8,128)(2,1)S(1)} %get-tuple-element.26), channel_id=1, source_target_pairs={{0,16},{16,32},{32,48},{48,64},{64,80},{80,96},{96,112},{112,0},{1... | collective-permute-start | bytes 294920 | tf_op jit(solution)/shard_map/ppermute | solution.py:25
  123.9 2.5 %collective-permute-start.18 = (bf16[192,256]{1,0:T(8,128)(2,1)S(1)}, bf16[192,256]{1,0:T(8,128)(2,1)S(1)}, u32[]{:S(2)}, u32[]{:S(2)}) collective-permute-start(bf16[192,256]{1,0:T(8,128)(2,1)S(1)} %get-tuple-element.28), channel_id=1, source_target_pairs={{0,32},{16,48},{32,64},{48,80},{64,96},{80,112},{96,0},{112,16},{1... | collective-permute-start | bytes 294920 | tf_op jit(solution)/shard_map/ppermute | solution.py:25
  126.3 2.3 %collective-permute-start.17 = (bf16[192,256]{1,0:T(8,128)(2,1)S(1)}, bf16[192,256]{1,0:T(8,128)(2,1)S(1)}, u32[]{:S(2)}, u32[]{:S(2)}) collective-permute-start(bf16[192,256]{1,0:T(8,128)(2,1)S(1)} %get-tuple-element.29), channel_id=1, source_target_pairs={{0,112},{16,0},{32,16},{48,32},{64,48},{80,64},{96,80},{112,96},{1... | collective-permute-start | bytes 294920 | tf_op jit(solution)/shard_map/ppermute | solution.py:25
  129.6 1.4 collective-permute-done.18
  131.1 2.2 %collective-permute-start.20 = (bf16[192,256]{1,0:T(8,128)(2,1)S(1)}, bf16[192,256]{1,0:T(8,128)(2,1)S(1)}, u32[]{:S(2)}, u32[]{:S(2)}) collective-permute-start(bf16[192,256]{1,0:T(8,128)(2,1)S(1)} %fusion.36), channel_id=1, source_target_pairs={{0,16},{16,0},{32,48},{48,32},{64,80},{80,64},{96,112},{112,96},{1... | collective-permute-start | bytes 294920 | tf_op jit(solution)/shard_map/ppermute | solution.py:8
  133.3 2.6 %collective-permute-done.20 = bf16[192,256]{1,0:T(8,128)(2,1)S(1)} collective-permute-done((bf16[192,256]{1,0:T(8,128)(2,1)S(1)}, bf16[192,256]{1,0:T(8,128)(2,1)S(1)}, u32[]{:S(2)}, u32[]{:S(2)}) %collective-permute-start.20) | collective-permute-done | bytes 98336 | tf_op jit(solution)/shard_map/ppermute | solution.py:8
  135.9 1.4 %fusion.23 = f32[1024,256]{1,0:T(8,128)} fusion(bf16[192,1024]{1,0:T(8,128)(2,1)S(1)} %copy-done.5, bf16[192,1024]{1,0:T(8,128)(2,1)S(1)} %bitcast.112, bf16[192,256]{1,0:T(8,128)(2,1)S(1)} %get-tuple-element.38, bf16[192,256]{1,0:T(8,128)(2,1)S(1)} %get-tuple-element.37), kind=kOutput, calls=%fused_computation.23 | convolution fusion | flops 203292672 | bytes 2031616 | tf_op jit(solution)/shard_map/dot_general | solution.py:193
  (91 shorter events, 10.8 us)
Async XLA Ops:
  0.6 19.7 %copy-start = (bf16[1024,256]{1,0:T(8,128)(2,1)S(1)}, bf16[1024,256]{1,0:T(8,128)(2,1)}, u32[]{:S(2)}) copy-start(bf16[1024,256]{1,0:T(8,128)(2,1)} %param.7) | copy-start | bytes 1572868
  17.8 1.7 %collective-permute-start = (bf16[192,1024]{1,0:T(8,128)(2,1)S(1)}, bf16[192,1024]{1,0:T(8,128)(2,1)S(1)}, u32[]{:S(2)}, u32[]{:S(2)}) collective-permute-start(bf16[192,1024]{1,0:T(8,128)(2,1)S(1)} %bitcast.110), channel_id=1, source_target_pairs={{0,1},{1,0},{2,3},{3,2},{4,5},{5,4},{6,7},{7,6},{8,9},{9,8},{10,11... | collective-permute-start | bytes 1179656 | tf_op jit(solution)/shard_map/ppermute | solution.py:8
  19.5 0.7 copy-start.4
  20.7 7.2 %collective-permute-start.1 = (f32[192,256]{1,0:T(8,128)S(1)}, f32[192,256]{1,0:T(8,128)S(1)}, u32[]{:S(2)}, u32[]{:S(2)}) collective-permute-start(f32[192,256]{1,0:T(8,128)S(1)} %constant_dynamic-slice_fusion.4), channel_id=1, source_target_pairs={{0,16},{16,0},{32,48},{48,32},{64,80},{80,64},{96,112},{112,96},{1... | collective-permute-start | bytes 589832 | tf_op jit(solution)/shard_map/ppermute | solution.py:8
  27.9 9.8 %collective-permute-start.5 = (bf16[192,256]{1,0:T(8,128)(2,1)S(1)}, bf16[192,256]{1,0:T(8,128)(2,1)S(1)}, u32[]{:S(2)}, u32[]{:S(2)}) collective-permute-start(bf16[192,256]{1,0:T(8,128)(2,1)S(1)} %get-tuple-element.25), channel_id=1, source_target_pairs={{0,112},{16,0},{32,16},{48,32},{64,48},{80,64},{96,80},{112,96},{1... | collective-permute-start | bytes 294920 | tf_op jit(solution)/shard_map/ppermute | solution.py:25
  33.7 10.8 %collective-permute-start.6 = (bf16[192,256]{1,0:T(8,128)(2,1)S(1)}, bf16[192,256]{1,0:T(8,128)(2,1)S(1)}, u32[]{:S(2)}, u32[]{:S(2)}) collective-permute-start(bf16[192,256]{1,0:T(8,128)(2,1)S(1)} %get-tuple-element.25), channel_id=1, source_target_pairs={{0,96},{16,112},{32,0},{48,16},{64,32},{80,48},{96,64},{112,80},{1... | collective-permute-start | bytes 294920 | tf_op jit(solution)/shard_map/ppermute | solution.py:25
  35.2 9.4 %collective-permute-start.3 = (bf16[192,256]{1,0:T(8,128)(2,1)S(1)}, bf16[192,256]{1,0:T(8,128)(2,1)S(1)}, u32[]{:S(2)}, u32[]{:S(2)}) collective-permute-start(bf16[192,256]{1,0:T(8,128)(2,1)S(1)} %get-tuple-element.25), channel_id=1, source_target_pairs={{0,32},{16,48},{32,64},{48,80},{64,96},{80,112},{96,0},{112,16},{1... | collective-permute-start | bytes 294920 | tf_op jit(solution)/shard_map/ppermute | solution.py:25
  36.6 7.9 %collective-permute-start.2 = (bf16[192,256]{1,0:T(8,128)(2,1)S(1)}, bf16[192,256]{1,0:T(8,128)(2,1)S(1)}, u32[]{:S(2)}, u32[]{:S(2)}) collective-permute-start(bf16[192,256]{1,0:T(8,128)(2,1)S(1)} %get-tuple-element.25), channel_id=1, source_target_pairs={{0,16},{16,32},{32,48},{48,64},{64,80},{80,96},{96,112},{112,0},{1... | collective-permute-start | bytes 294920 | tf_op jit(solution)/shard_map/ppermute | solution.py:25
  44.5 12.2 %collective-permute-start.8 = (bf16[5,192,256]{2,1,0:T(8,128)(2,1)S(1)}, bf16[5,192,256]{2,1,0:T(8,128)(2,1)S(1)}, u32[]{:S(2)}, u32[]{:S(2)}) collective-permute-start(bf16[5,192,256]{2,1,0:T(8,128)(2,1)S(1)} %bitcast_dynamic-update-slice_fusion.1), channel_id=1, source_target_pairs={{0,128},{16,144},{32,160},{48,176},{64,192},{80,208},{96,224},{112... | collective-permute-start | bytes 1474568 | tf_op jit(solution)/shard_map/ppermute | solution.py:30
  47.2 9.5 %collective-permute-start.4 = (bf16[288,256]{1,0:T(8,128)(2,1)S(1)}, bf16[288,256]{1,0:T(8,128)(2,1)S(1)}, u32[]{:S(2)}, u32[]{:S(2)}) collective-permute-start(bf16[288,256]{1,0:T(8,128)(2,1)S(1)} %pad_maximum_fusion.6), channel_id=1, source_target_pairs={{0,32},{16,48},{32,64},{48,80},{64,96},{80,112},{96,0},{112,16},{1... | collective-permute-start | bytes 442376 | tf_op jit(solution)/shard_map/ppermute | solution.py:25
  47.3 9.4 %collective-permute-start.7 = (bf16[288,256]{1,0:T(8,128)(2,1)S(1)}, bf16[288,256]{1,0:T(8,128)(2,1)S(1)}, u32[]{:S(2)}, u32[]{:S(2)}) collective-permute-start(bf16[288,256]{1,0:T(8,128)(2,1)S(1)} %pad_maximum_fusion.7), channel_id=1, source_target_pairs={{0,96},{16,112},{32,0},{48,16},{64,32},{80,48},{96,64},{112,80},{1... | collective-permute-start | bytes 442376 | tf_op jit(solution)/shard_map/ppermute | solution.py:25
  56.8 7.6 %collective-permute-start.9 = (bf16[3,192,256]{2,1,0:T(8,128)(2,1)S(1)}, bf16[3,192,256]{2,1,0:T(8,128)(2,1)S(1)}, u32[]{:S(2)}, u32[]{:S(2)}) collective-permute-start(bf16[3,192,256]{2,1,0:T(8,128)(2,1)S(1)} %pad_maximum_fusion.4), channel_id=1, source_target_pairs={{0,128},{16,144},{32,160},{48,176},{64,192},{80,208},{96,224},{112... | collective-permute-start | bytes 884744 | tf_op jit(solution)/shard_map/ppermute | solution.py:30
  60.4 4.3 %copy-start.2 = (bf16[8,256,1024]{2,1,0:T(8,128)(2,1)S(1)}, bf16[8,256,1024]{2,1,0:T(8,128)(2,1)}, u32[]{:S(2)}) copy-start(bf16[8,256,1024]{2,1,0:T(8,128)(2,1)} %param.9) | copy-start | bytes 12582916
  65.7 1.8 %collective-permute-start.10 = (bf16[192,1024]{1,0:T(8,128)(2,1)S(1)}, bf16[192,1024]{1,0:T(8,128)(2,1)S(1)}, u32[]{:S(2)}, u32[]{:S(2)}) collective-permute-start(bf16[192,1024]{1,0:T(8,128)(2,1)S(1)} %fusion.14), channel_id=1, source_target_pairs={{0,1},{1,0},{2,3},{3,2},{4,5},{5,4},{6,7},{7,6},{8,9},{9,8},{10,11... | collective-permute-start | bytes 1179656 | tf_op jit(solution)/shard_map/ppermute | solution.py:8
  66.8 14.5 %copy-start.1 = (bf16[24,1024]{1,0:T(8,128)(2,1)S(1)}, bf16[24,1024]{1,0:T(8,128)(2,1)}, u32[]{:S(2)}) copy-start(bf16[24,1024]{1,0:T(8,128)(2,1)} %param.6) | copy-start | bytes 147460
  93.7 1.7 %collective-permute-start.11 = (bf16[192,1024]{1,0:T(8,128)(2,1)S(1)}, bf16[192,1024]{1,0:T(8,128)(2,1)S(1)}, u32[]{:S(2)}, u32[]{:S(2)}) collective-permute-start(bf16[192,1024]{1,0:T(8,128)(2,1)S(1)} %bitcast.95), channel_id=1, source_target_pairs={{0,1},{1,0},{2,3},{3,2},{4,5},{5,4},{6,7},{7,6},{8,9},{9,8},{10,11... | collective-permute-start | bytes 1179656 | tf_op jit(solution)/shard_map/ppermute | solution.py:8
  98.3 11.7 %collective-permute-start.12 = (bf16[3,192,256]{2,1,0:T(8,128)(2,1)S(1)}, bf16[3,192,256]{2,1,0:T(8,128)(2,1)S(1)}, u32[]{:S(2)}, u32[]{:S(2)}) collective-permute-start(bf16[3,192,256]{2,1,0:T(8,128)(2,1)S(1)} %pad_maximum_fusion.5), channel_id=1, source_target_pairs={{128,0},{144,16},{160,32},{176,48},{192,64},{208,80},{224,96},{240... | collective-permute-start | bytes 884744 | tf_op jit(solution)/shard_map/ppermute | solution.py:35
  99.6 6.2 %copy-start.3 = (bf16[8,256,1024]{2,1,0:T(8,128)(2,1)S(1)}, bf16[8,256,1024]{2,1,0:T(8,128)(2,1)}, u32[]{:S(2)}) copy-start(bf16[8,256,1024]{2,1,0:T(8,128)(2,1)} %param.9) | copy-start | bytes 12582916
  99.6 21.4 %collective-permute-start.13 = (bf16[5,192,256]{2,1,0:T(8,128)(2,1)S(1)}, bf16[5,192,256]{2,1,0:T(8,128)(2,1)S(1)}, u32[]{:S(2)}, u32[]{:S(2)}) collective-permute-start(bf16[5,192,256]{2,1,0:T(8,128)(2,1)S(1)} %get-tuple-element.34), channel_id=1, source_target_pairs={{128,0},{144,16},{160,32},{176,48},{192,64},{208,80},{224,96},{240... | collective-permute-start | bytes 1474568 | tf_op jit(solution)/shard_map/ppermute | solution.py:35
  110.2 7.4 %collective-permute-start.16 = (bf16[288,256]{1,0:T(8,128)(2,1)S(1)}, bf16[288,256]{1,0:T(8,128)(2,1)S(1)}, u32[]{:S(2)}, u32[]{:S(2)}) collective-permute-start(bf16[288,256]{1,0:T(8,128)(2,1)S(1)} %pad_maximum_fusion.9), channel_id=1, source_target_pairs={{0,96},{16,112},{32,0},{48,16},{64,32},{80,48},{96,64},{112,80},{1... | collective-permute-start | bytes 442376 | tf_op jit(solution)/shard_map/ppermute | solution.py:25
  111.7 24.2 %copy-start.5 = (bf16[192,1024]{1,0:T(8,128)(2,1)S(1)}, bf16[192,1024]{1,0:T(8,128)(2,1)}, u32[]{:S(2)}) copy-start(bf16[192,1024]{1,0:T(8,128)(2,1)} %copy-done.4) | copy-start | bytes 1179652
  111.7 9.3 %collective-permute-start.14 = (bf16[288,256]{1,0:T(8,128)(2,1)S(1)}, bf16[288,256]{1,0:T(8,128)(2,1)S(1)}, u32[]{:S(2)}, u32[]{:S(2)}) collective-permute-start(bf16[288,256]{1,0:T(8,128)(2,1)S(1)} %pad_maximum_fusion.8), channel_id=1, source_target_pairs={{0,32},{16,48},{32,64},{48,80},{64,96},{80,112},{96,0},{112,16},{1... | collective-permute-start | bytes 442376 | tf_op jit(solution)/shard_map/ppermute | solution.py:25
  121.2 7.5 %collective-permute-start.15 = (bf16[192,256]{1,0:T(8,128)(2,1)S(1)}, bf16[192,256]{1,0:T(8,128)(2,1)S(1)}, u32[]{:S(2)}, u32[]{:S(2)}) collective-permute-start(bf16[192,256]{1,0:T(8,128)(2,1)S(1)} %get-tuple-element.26), channel_id=1, source_target_pairs={{0,16},{16,32},{32,48},{48,64},{64,80},{80,96},{96,112},{112,0},{1... | collective-permute-start | bytes 294920 | tf_op jit(solution)/shard_map/ppermute | solution.py:25
  123.4 6.1 %collective-permute-start.19 = (bf16[192,256]{1,0:T(8,128)(2,1)S(1)}, bf16[192,256]{1,0:T(8,128)(2,1)S(1)}, u32[]{:S(2)}, u32[]{:S(2)}) collective-permute-start(bf16[192,256]{1,0:T(8,128)(2,1)S(1)} %get-tuple-element.27), channel_id=1, source_target_pairs={{0,96},{16,112},{32,0},{48,16},{64,32},{80,48},{96,64},{112,80},{1... | collective-permute-start | bytes 294920 | tf_op jit(solution)/shard_map/ppermute | solution.py:25
  123.9 7.1 %collective-permute-start.18 = (bf16[192,256]{1,0:T(8,128)(2,1)S(1)}, bf16[192,256]{1,0:T(8,128)(2,1)S(1)}, u32[]{:S(2)}, u32[]{:S(2)}) collective-permute-start(bf16[192,256]{1,0:T(8,128)(2,1)S(1)} %get-tuple-element.28), channel_id=1, source_target_pairs={{0,32},{16,48},{32,64},{48,80},{64,96},{80,112},{96,0},{112,16},{1... | collective-permute-start | bytes 294920 | tf_op jit(solution)/shard_map/ppermute | solution.py:25
  126.3 4.6 %collective-permute-start.17 = (bf16[192,256]{1,0:T(8,128)(2,1)S(1)}, bf16[192,256]{1,0:T(8,128)(2,1)S(1)}, u32[]{:S(2)}, u32[]{:S(2)}) collective-permute-start(bf16[192,256]{1,0:T(8,128)(2,1)S(1)} %get-tuple-element.29), channel_id=1, source_target_pairs={{0,112},{16,0},{32,16},{48,32},{64,48},{80,64},{96,80},{112,96},{1... | collective-permute-start | bytes 294920 | tf_op jit(solution)/shard_map/ppermute | solution.py:25
  131.1 4.8 %collective-permute-start.20 = (bf16[192,256]{1,0:T(8,128)(2,1)S(1)}, bf16[192,256]{1,0:T(8,128)(2,1)S(1)}, u32[]{:S(2)}, u32[]{:S(2)}) collective-permute-start(bf16[192,256]{1,0:T(8,128)(2,1)S(1)} %fusion.36), channel_id=1, source_target_pairs={{0,16},{16,0},{32,48},{48,32},{64,80},{80,64},{96,112},{112,96},{1... | collective-permute-start | bytes 294920 | tf_op jit(solution)/shard_map/ppermute | solution.py:8

commit v7 on v6

--- a/solution.py
+++ b/solution.py
@@ -48,7 +48,7 @@
         return lax.dynamic_update_index_in_dim(stack, block, place, 0)
 
     near = {0: own}
-    for distance in (1, -1, 2, -2):
+    for distance in (-2, 1, -1, 2):
         near[distance] = along_ring(own, -distance)
     behind = along_ring(jnp.concatenate([near[-1], near[-2][:half]], 0), 2)
     ahead = along_ring(jnp.concatenate([near[1], near[2][half:]], 0), -2)
@@ -67,7 +67,9 @@
         (far, far_crossed, far_order),
     ):
         for at, distance in enumerate(order):
-            stack = put(stack, blocks[distance], plane, distance)
+            earlier = (spot + distance) % ring // 2 <= spot // 2
+            block = jnp.where(earlier, blocks[distance], jnp.zeros_like(own))
+            stack = put(stack, block, plane, distance)
             stack = put(stack, crossed[at], 1 - plane, distance)
     return stack
 
@@ -156,9 +158,8 @@
     ring = places // 2
     plane, spot = position // ring, position % ring
     gathered = latents_of_all(latents_half, plane, spot, ring)
-    gathered = gathered.reshape(layer_count, total_rows, latent_cols)
+    latents = gathered.reshape(layer_count, total_rows, latent_cols)
     used = lax.broadcasted_iota(jnp.int32, (layer_count, 1, 1), 0) <= layer_now
-    latents = jnp.where(used, gathered, jnp.zeros_like(gathered))
 
     def decoded(part):
         return lax.dot_general(

time: 138 us -> 138 us (level)
  transfers between devices with their start and end apart: 21 -> 21, of which waited for: 14 -> 15; matrix products, arithmetic and copies ran while one was open for 6% -> 6% of each run, Pallas kernels for 0% -> 0%
where the time goes in v7:
time: 138 us; the launch traced here: 137 us
  blocking collectives  42.3 us (31%)
  waiting for transfers between devices  41.2 us (30%)
  starting transfers between devices  36.7 us (27%)
  matrix products  11.9 us (9%)
  local copies, waits for them, and re-layouts  2.94 us (2%)
    all_to_all x3, blocking collectives, exchanged(): lax.all_to_all(parts, axis, split_axis=0, concat_axis=0, tiled=True, axis...  42.3 us
    ppermute x12, starting transfers between devices, along_ring(): return lax.ppermute(x, 'layer', pairs)  24 us
    ppermute x12, waiting for transfers between devices, along_ring(): return lax.ppermute(x, 'layer', pairs)  21.9 us
    ppermute x5, waiting for transfers between devices, from_partner(): lax.ppermute(x, axis, [(i, i ^ bit) for i in range(lax.axis_size(axis))])  12 us
    ppermute x2, starting transfers between devices, to_later_plane(): return lax.ppermute(x, 'layer', [(i, i + ring) for i in range(ring)])  6.39 us
    dot_general x1, matrix products, local(): lax.dot_general(latents, grad_after, (((1,), (0,)), ((), ())), preferred_...  4.4 us
    ppermute x2, waiting for transfers between devices, to_later_plane(): return lax.ppermute(x, 'layer', [(i, i + ring) for i in range(ring)])  3.95 us
    dot_general x2, matrix products, layer_terms(): lax.dot_general(weight, out_grad, (((2,), (1,)), ((), ())), preferred_ele...  3.63 us
  transfers between devices with their start and end apart: 21, of which 15 were waited for; matrix products, arithmetic and copies ran while one was open for 6% of the time, Pallas kernels for 0%

profile of v7, /device:TPU:2, one launch (start us, length us, event | category | flops | bytes accessed | tf_op | source)
XLA Modules:
  0.0 137.0 jit_solution(5916092647377266078)
XLA Ops:
  1.5 16.3 %all_to_all.15 = bf16[8,24,1024]{2,1,0:T(8,128)(2,1)S(1)} all-to-all(bf16[8,24,1024]{2,1,0:T(8,128)(2,1)S(1)} %broadcast_in_dim.73), channel_id=1, replica_groups={{0,2,4,6,8,10,12,14},{1,3,5,7,9,11,13,15},{16,18,20,22,24,26,28,30},{17..., dimensions={0} | all-to-all | bytes 786432 | tf_op jit(solution)/shard_map/all_to_all | solution.py:16
  17.8 1.7 %collective-permute-done = bf16[192,1024]{1,0:T(8,128)(2,1)S(1)} collective-permute-done((bf16[192,1024]{1,0:T(8,128)(2,1)S(1)}, bf16[192,1024]{1,0:T(8,128)(2,1)S(1)}, u32[]{:S(2)}, u32[]{:S(2)}) %collective-permute-start) | collective-permute-done | bytes 393248 | tf_op jit(solution)/shard_map/ppermute | solution.py:8
  20.7 2.0 %collective-permute-start.1 = (f32[192,256]{1,0:T(8,128)S(1)}, f32[192,256]{1,0:T(8,128)S(1)}, u32[]{:S(2)}, u32[]{:S(2)}) collective-permute-start(f32[192,256]{1,0:T(8,128)S(1)} %constant_dynamic-slice_fusion.4), channel_id=1, source_target_pairs={{0,16},{16,0},{32,48},{48,32},{64,80},{80,64},{96,112},{112,96},{1... | collective-permute-start | bytes 589832 | tf_op jit(solution)/shard_map/ppermute | solution.py:8
  23.4 4.5 %collective-permute-done.1 = f32[192,256]{1,0:T(8,128)S(1)} collective-permute-done((f32[192,256]{1,0:T(8,128)S(1)}, f32[192,256]{1,0:T(8,128)S(1)}, u32[]{:S(2)}, u32[]{:S(2)}) %collective-permute-start.1) | collective-permute-done | bytes 196640 | tf_op jit(solution)/shard_map/ppermute | solution.py:8
  27.9 3.3 %collective-permute-start.3 = (bf16[192,256]{1,0:T(8,128)(2,1)S(1)}, bf16[192,256]{1,0:T(8,128)(2,1)S(1)}, u32[]{:S(2)}, u32[]{:S(2)}) collective-permute-start(bf16[192,256]{1,0:T(8,128)(2,1)S(1)} %get-tuple-element.25), channel_id=1, source_target_pairs={{0,32},{16,48},{32,64},{48,80},{64,96},{80,112},{96,0},{112,16},{1... | collective-permute-start | bytes 294920 | tf_op jit(solution)/shard_map/ppermute | solution.py:25
  31.3 3.5 %collective-permute-start.6 = (bf16[192,256]{1,0:T(8,128)(2,1)S(1)}, bf16[192,256]{1,0:T(8,128)(2,1)S(1)}, u32[]{:S(2)}, u32[]{:S(2)}) collective-permute-start(bf16[192,256]{1,0:T(8,128)(2,1)S(1)} %get-tuple-element.25), channel_id=1, source_target_pairs={{0,96},{16,112},{32,0},{48,16},{64,32},{80,48},{96,64},{112,80},{1... | collective-permute-start | bytes 294920 | tf_op jit(solution)/shard_map/ppermute | solution.py:25
  34.8 1.9 %collective-permute-start.5 = (bf16[192,256]{1,0:T(8,128)(2,1)S(1)}, bf16[192,256]{1,0:T(8,128)(2,1)S(1)}, u32[]{:S(2)}, u32[]{:S(2)}) collective-permute-start(bf16[192,256]{1,0:T(8,128)(2,1)S(1)} %get-tuple-element.25), channel_id=1, source_target_pairs={{0,112},{16,0},{32,16},{48,32},{64,48},{80,64},{96,80},{112,96},{1... | collective-permute-start | bytes 294920 | tf_op jit(solution)/shard_map/ppermute | solution.py:25
  37.3 4.5 %collective-permute-done.5 = bf16[192,256]{1,0:T(8,128)(2,1)S(1)} collective-permute-done((bf16[192,256]{1,0:T(8,128)(2,1)S(1)}, bf16[192,256]{1,0:T(8,128)(2,1)S(1)}, u32[]{:S(2)}, u32[]{:S(2)}) %collective-permute-start.5) | collective-permute-done | bytes 98336 | tf_op jit(solution)/shard_map/ppermute | solution.py:25
  42.5 2.6 %collective-permute-start.8 = (bf16[5,192,256]{2,1,0:T(8,128)(2,1)S(1)}, bf16[5,192,256]{2,1,0:T(8,128)(2,1)S(1)}, u32[]{:S(2)}, u32[]{:S(2)}) collective-permute-start(bf16[5,192,256]{2,1,0:T(8,128)(2,1)S(1)} %bitcast_dynamic-update-slice_fusion.7), channel_id=1, source_target_pairs={{0,128},{16,144},{32,160},{48,176},{64,192},{80,208},{96,224},{112... | collective-permute-start | bytes 1474568 | tf_op jit(solution)/shard_map/ppermute | solution.py:30
  45.1 2.2 %collective-permute-start.4 = (bf16[288,256]{1,0:T(8,128)(2,1)S(1)}, bf16[288,256]{1,0:T(8,128)(2,1)S(1)}, u32[]{:S(2)}, u32[]{:S(2)}) collective-permute-start(bf16[288,256]{1,0:T(8,128)(2,1)S(1)} %pad_maximum_fusion.6), channel_id=1, source_target_pairs={{0,32},{16,48},{32,64},{48,80},{64,96},{80,112},{96,0},{112,16},{1... | collective-permute-start | bytes 442376 | tf_op jit(solution)/shard_map/ppermute | solution.py:25
  47.3 2.1 %collective-permute-start.7 = (bf16[288,256]{1,0:T(8,128)(2,1)S(1)}, bf16[288,256]{1,0:T(8,128)(2,1)S(1)}, u32[]{:S(2)}, u32[]{:S(2)}) collective-permute-start(bf16[288,256]{1,0:T(8,128)(2,1)S(1)} %pad_maximum_fusion.7), channel_id=1, source_target_pairs={{0,96},{16,112},{32,0},{48,16},{64,32},{80,48},{96,64},{112,80},{1... | collective-permute-start | bytes 442376 | tf_op jit(solution)/shard_map/ppermute | solution.py:25
  49.6 4.7 %collective-permute-done.4 = bf16[288,256]{1,0:T(8,128)(2,1)S(1)} collective-permute-done((bf16[288,256]{1,0:T(8,128)(2,1)S(1)}, bf16[288,256]{1,0:T(8,128)(2,1)S(1)}, u32[]{:S(2)}, u32[]{:S(2)}) %collective-permute-start.4) | collective-permute-done | bytes 147488 | tf_op jit(solution)/shard_map/ppermute | solution.py:25
  54.4 3.8 %collective-permute-start.9 = (bf16[3,192,256]{2,1,0:T(8,128)(2,1)S(1)}, bf16[3,192,256]{2,1,0:T(8,128)(2,1)S(1)}, u32[]{:S(2)}, u32[]{:S(2)}) collective-permute-start(bf16[3,192,256]{2,1,0:T(8,128)(2,1)S(1)} %pad_maximum_fusion.4), channel_id=1, source_target_pairs={{0,128},{16,144},{32,160},{48,176},{64,192},{80,208},{96,224},{112... | collective-permute-start | bytes 884744 | tf_op jit(solution)/shard_map/ppermute | solution.py:30
  58.5 3.9 %collective-permute-done.9 = bf16[3,192,256]{2,1,0:T(8,128)(2,1)S(1)} collective-permute-done((bf16[3,192,256]{2,1,0:T(8,128)(2,1)S(1)}, bf16[3,192,256]{2,1,0:T(8,128)(2,1)S(1)}, u32[]{:S(2)}, u32[]{:S(2)}) %collective-permute-start.9) | collective-permute-done | bytes 294944 | tf_op jit(solution)/shard_map/ppermute | solution.py:30
  65.5 13.6 %all_to_all.16 = bf16[8,24,1024]{2,1,0:T(8,128)(2,1)S(1)} all-to-all(bf16[8,24,1024]{2,1,0:T(8,128)(2,1)S(1)} %bitcast.106), channel_id=1, replica_groups={{0,2,4,6,8,10,12,14},{1,3,5,7,9,11,13,15},{16,18,20,22,24,26,28,30},{17..., dimensions={0} | all-to-all | bytes 786432 | tf_op jit(solution)/shard_map/all_to_all | solution.py:16
  79.3 12.4 %all_to_all.17 = bf16[8,24,1024]{2,1,0:T(8,128)(2,1)S(1)} all-to-all(bf16[8,24,1024]{2,1,0:T(8,128)(2,1)S(1)} %broadcast_in_dim.85), channel_id=1, replica_groups={{0,2,4,6,8,10,12,14},{1,3,5,7,9,11,13,15},{16,18,20,22,24,26,28,30},{17..., dimensions={0} | all-to-all | bytes 786432 | tf_op jit(solution)/shard_map/all_to_all | solution.py:16
  91.7 1.6 %collective-permute-done.11 = bf16[192,1024]{1,0:T(8,128)(2,1)S(1)} collective-permute-done((bf16[192,1024]{1,0:T(8,128)(2,1)S(1)}, bf16[192,1024]{1,0:T(8,128)(2,1)S(1)}, u32[]{:S(2)}, u32[]{:S(2)}) %collective-permute-start.11) | collective-permute-done | bytes 393248 | tf_op jit(solution)/shard_map/ppermute | solution.py:8
  93.4 2.6 %fusion.8 = bf16[4,384,256]{2,1,0:T(8,128)(2,1)S(1)} fusion(bf16[8,256,1024]{2,1,0:T(8,128)(2,1)} %param.9, pred[4]{0:T(512)(128)(4,1)S(1)} %get-tuple-element.42, bf16[192,1024]{1,0:T(8,128)(2,1)S(1)} %collective-permute-done.11, bf16[192,1024]{1,0:T(8,128)(2,1)S(1)} %bitcast.105), kind=kOutput, calls=%fused_computation.7 | convolution fusion | flops 807665664 | bytes 3670020 | tf_op jit(solution)/shard_map/dot_general | solution.py:78
  96.2 1.3 collective-permute-start.12
  97.5 1.7 %collective-permute-start.13 = (bf16[5,192,256]{2,1,0:T(8,128)(2,1)S(1)}, bf16[5,192,256]{2,1,0:T(8,128)(2,1)S(1)}, u32[]{:S(2)}, u32[]{:S(2)}) collective-permute-start(bf16[5,192,256]{2,1,0:T(8,128)(2,1)S(1)} %get-tuple-element.34), channel_id=1, source_target_pairs={{128,0},{144,16},{160,32},{176,48},{192,64},{208,80},{224,96},{240... | collective-permute-start | bytes 1474568 | tf_op jit(solution)/shard_map/ppermute | solution.py:35
  99.3 4.4 %convolution_convert_fusion = bf16[8,256,1024]{2,1,0:T(8,128)(2,1)} fusion(bf16[8,384,256]{2,1,0:T(8,128)(2,1)S(1)} %bitcast.102, bf16[384,1024]{1,0:T(8,128)(2,1)S(1)} %pad_maximum_fusion.1), kind=kOutput, calls=%fused_computation | convolution fusion | flops 1612709888 | bytes 6553600 | tf_op jit(solution)/shard_map/dot_general | solution.py:181
  104.7 3.3 %collective-permute-done.12 = bf16[3,192,256]{2,1,0:T(8,128)(2,1)S(1)} collective-permute-done((bf16[3,192,256]{2,1,0:T(8,128)(2,1)S(1)}, bf16[3,192,256]{2,1,0:T(8,128)(2,1)S(1)}, u32[]{:S(2)}, u32[]{:S(2)}) %collective-permute-start.12) | collective-permute-done | bytes 294944 | tf_op jit(solution)/shard_map/ppermute | solution.py:35
  108.1 2.1 %collective-permute-start.16 = (bf16[288,256]{1,0:T(8,128)(2,1)S(1)}, bf16[288,256]{1,0:T(8,128)(2,1)S(1)}, u32[]{:S(2)}, u32[]{:S(2)}) collective-permute-start(bf16[288,256]{1,0:T(8,128)(2,1)S(1)} %pad_maximum_fusion.9), channel_id=1, source_target_pairs={{0,96},{16,112},{32,0},{48,16},{64,32},{80,48},{96,64},{112,80},{1... | collective-permute-start | bytes 442376 | tf_op jit(solution)/shard_map/ppermute | solution.py:25
  111.4 4.1 %collective-permute-done.16 = bf16[288,256]{1,0:T(8,128)(2,1)S(1)} collective-permute-done((bf16[288,256]{1,0:T(8,128)(2,1)S(1)}, bf16[288,256]{1,0:T(8,128)(2,1)S(1)}, u32[]{:S(2)}, u32[]{:S(2)}) %collective-permute-start.16) | collective-permute-done | bytes 147488 | tf_op jit(solution)/shard_map/ppermute | solution.py:25
  115.5 3.9 %collective-permute-done.14 = bf16[288,256]{1,0:T(8,128)(2,1)S(1)} collective-permute-done((bf16[288,256]{1,0:T(8,128)(2,1)S(1)}, bf16[288,256]{1,0:T(8,128)(2,1)S(1)}, u32[]{:S(2)}, u32[]{:S(2)}) %collective-permute-start.14) | collective-permute-done | bytes 147488 | tf_op jit(solution)/shard_map/ppermute | solution.py:25
  119.6 1.8 %collective-permute-start.15 = (bf16[192,256]{1,0:T(8,128)(2,1)S(1)}, bf16[192,256]{1,0:T(8,128)(2,1)S(1)}, u32[]{:S(2)}, u32[]{:S(2)}) collective-permute-start(bf16[192,256]{1,0:T(8,128)(2,1)S(1)} %get-tuple-element.26), channel_id=1, source_target_pairs={{0,16},{16,32},{32,48},{48,64},{64,80},{80,96},{96,112},{112,0},{1... | collective-permute-start | bytes 294920 | tf_op jit(solution)/shard_map/ppermute | solution.py:25
  121.4 1.4 collective-permute-start.19
  122.7 1.6 %collective-permute-start.18 = (bf16[192,256]{1,0:T(8,128)(2,1)S(1)}, bf16[192,256]{1,0:T(8,128)(2,1)S(1)}, u32[]{:S(2)}, u32[]{:S(2)}) collective-permute-start(bf16[192,256]{1,0:T(8,128)(2,1)S(1)} %get-tuple-element.28), channel_id=1, source_target_pairs={{0,32},{16,48},{32,64},{48,80},{64,96},{80,112},{96,0},{112,16},{1... | collective-permute-start | bytes 294920 | tf_op jit(solution)/shard_map/ppermute | solution.py:25
  124.3 2.7 %collective-permute-start.17 = (bf16[192,256]{1,0:T(8,128)(2,1)S(1)}, bf16[192,256]{1,0:T(8,128)(2,1)S(1)}, u32[]{:S(2)}, u32[]{:S(2)}) collective-permute-start(bf16[192,256]{1,0:T(8,128)(2,1)S(1)} %get-tuple-element.29), channel_id=1, source_target_pairs={{0,112},{16,0},{32,16},{48,32},{64,48},{80,64},{96,80},{112,96},{1... | collective-permute-start | bytes 294920 | tf_op jit(solution)/shard_map/ppermute | solution.py:25
  127.4 3.3 %collective-permute-done.18 = bf16[192,256]{1,0:T(8,128)(2,1)S(1)} collective-permute-done((bf16[192,256]{1,0:T(8,128)(2,1)S(1)}, bf16[192,256]{1,0:T(8,128)(2,1)S(1)}, u32[]{:S(2)}, u32[]{:S(2)}) %collective-permute-start.18) | collective-permute-done | bytes 98336 | tf_op jit(solution)/shard_map/ppermute | solution.py:25
  132.0 3.5 %collective-permute-done.20 = bf16[192,256]{1,0:T(8,128)(2,1)S(1)} collective-permute-done((bf16[192,256]{1,0:T(8,128)(2,1)S(1)}, bf16[192,256]{1,0:T(8,128)(2,1)S(1)}, u32[]{:S(2)}, u32[]{:S(2)}) %collective-permute-start.20) | collective-permute-done | bytes 98336 | tf_op jit(solution)/shard_map/ppermute | solution.py:8
  135.5 1.4 %fusion.23 = f32[1024,256]{1,0:T(8,128)} fusion(bf16[192,1024]{1,0:T(8,128)(2,1)S(1)} %copy-done.5, bf16[192,1024]{1,0:T(8,128)(2,1)S(1)} %bitcast.120, bf16[192,256]{1,0:T(8,128)(2,1)S(1)} %get-tuple-element.38, bf16[192,256]{1,0:T(8,128)(2,1)S(1)} %get-tuple-element.37), kind=kOutput, calls=%fused_computation.22 | convolution fusion | flops 203292672 | bytes 2031616 | tf_op jit(solution)/shard_map/dot_general | solution.py:194
  (89 shorter events, 12.2 us)
Async XLA Ops:
  0.6 19.7 %copy-start = (bf16[1024,256]{1,0:T(8,128)(2,1)S(1)}, bf16[1024,256]{1,0:T(8,128)(2,1)}, u32[]{:S(2)}) copy-start(bf16[1024,256]{1,0:T(8,128)(2,1)} %param.7) | copy-start | bytes 1572868
  17.8 1.7 %collective-permute-start = (bf16[192,1024]{1,0:T(8,128)(2,1)S(1)}, bf16[192,1024]{1,0:T(8,128)(2,1)S(1)}, u32[]{:S(2)}, u32[]{:S(2)}) collective-permute-start(bf16[192,1024]{1,0:T(8,128)(2,1)S(1)} %bitcast.118), channel_id=1, source_target_pairs={{0,1},{1,0},{2,3},{3,2},{4,5},{5,4},{6,7},{7,6},{8,9},{9,8},{10,11... | collective-permute-start | bytes 1179656 | tf_op jit(solution)/shard_map/ppermute | solution.py:8
  19.5 0.7 copy-start.4
  20.7 7.2 %collective-permute-start.1 = (f32[192,256]{1,0:T(8,128)S(1)}, f32[192,256]{1,0:T(8,128)S(1)}, u32[]{:S(2)}, u32[]{:S(2)}) collective-permute-start(f32[192,256]{1,0:T(8,128)S(1)} %constant_dynamic-slice_fusion.4), channel_id=1, source_target_pairs={{0,16},{16,0},{32,48},{48,32},{64,80},{80,64},{96,112},{112,96},{1... | collective-permute-start | bytes 589832 | tf_op jit(solution)/shard_map/ppermute | solution.py:8
  27.9 9.4 %collective-permute-start.3 = (bf16[192,256]{1,0:T(8,128)(2,1)S(1)}, bf16[192,256]{1,0:T(8,128)(2,1)S(1)}, u32[]{:S(2)}, u32[]{:S(2)}) collective-permute-start(bf16[192,256]{1,0:T(8,128)(2,1)S(1)} %get-tuple-element.25), channel_id=1, source_target_pairs={{0,32},{16,48},{32,64},{48,80},{64,96},{80,112},{96,0},{112,16},{1... | collective-permute-start | bytes 294920 | tf_op jit(solution)/shard_map/ppermute | solution.py:25
  31.3 11.2 %collective-permute-start.6 = (bf16[192,256]{1,0:T(8,128)(2,1)S(1)}, bf16[192,256]{1,0:T(8,128)(2,1)S(1)}, u32[]{:S(2)}, u32[]{:S(2)}) collective-permute-start(bf16[192,256]{1,0:T(8,128)(2,1)S(1)} %get-tuple-element.25), channel_id=1, source_target_pairs={{0,96},{16,112},{32,0},{48,16},{64,32},{80,48},{96,64},{112,80},{1... | collective-permute-start | bytes 294920 | tf_op jit(solution)/shard_map/ppermute | solution.py:25
  34.8 7.1 %collective-permute-start.5 = (bf16[192,256]{1,0:T(8,128)(2,1)S(1)}, bf16[192,256]{1,0:T(8,128)(2,1)S(1)}, u32[]{:S(2)}, u32[]{:S(2)}) collective-permute-start(bf16[192,256]{1,0:T(8,128)(2,1)S(1)} %get-tuple-element.25), channel_id=1, source_target_pairs={{0,112},{16,0},{32,16},{48,32},{64,48},{80,64},{96,80},{112,96},{1... | collective-permute-start | bytes 294920 | tf_op jit(solution)/shard_map/ppermute | solution.py:25
  36.6 5.8 %collective-permute-start.2 = (bf16[192,256]{1,0:T(8,128)(2,1)S(1)}, bf16[192,256]{1,0:T(8,128)(2,1)S(1)}, u32[]{:S(2)}, u32[]{:S(2)}) collective-permute-start(bf16[192,256]{1,0:T(8,128)(2,1)S(1)} %get-tuple-element.25), channel_id=1, source_target_pairs={{0,16},{16,32},{32,48},{48,64},{64,80},{80,96},{96,112},{112,0},{1... | collective-permute-start | bytes 294920 | tf_op jit(solution)/shard_map/ppermute | solution.py:25
  42.5 11.9 %collective-permute-start.8 = (bf16[5,192,256]{2,1,0:T(8,128)(2,1)S(1)}, bf16[5,192,256]{2,1,0:T(8,128)(2,1)S(1)}, u32[]{:S(2)}, u32[]{:S(2)}) collective-permute-start(bf16[5,192,256]{2,1,0:T(8,128)(2,1)S(1)} %bitcast_dynamic-update-slice_fusion.7), channel_id=1, source_target_pairs={{0,128},{16,144},{32,160},{48,176},{64,192},{80,208},{96,224},{112... | collective-permute-start | bytes 1474568 | tf_op jit(solution)/shard_map/ppermute | solution.py:30
  45.1 9.2 %collective-permute-start.4 = (bf16[288,256]{1,0:T(8,128)(2,1)S(1)}, bf16[288,256]{1,0:T(8,128)(2,1)S(1)}, u32[]{:S(2)}, u32[]{:S(2)}) collective-permute-start(bf16[288,256]{1,0:T(8,128)(2,1)S(1)} %pad_maximum_fusion.6), channel_id=1, source_target_pairs={{0,32},{16,48},{32,64},{48,80},{64,96},{80,112},{96,0},{112,16},{1... | collective-permute-start | bytes 442376 | tf_op jit(solution)/shard_map/ppermute | solution.py:25
  47.3 7.0 %collective-permute-start.7 = (bf16[288,256]{1,0:T(8,128)(2,1)S(1)}, bf16[288,256]{1,0:T(8,128)(2,1)S(1)}, u32[]{:S(2)}, u32[]{:S(2)}) collective-permute-start(bf16[288,256]{1,0:T(8,128)(2,1)S(1)} %pad_maximum_fusion.7), channel_id=1, source_target_pairs={{0,96},{16,112},{32,0},{48,16},{64,32},{80,48},{96,64},{112,80},{1... | collective-permute-start | bytes 442376 | tf_op jit(solution)/shard_map/ppermute | solution.py:25
  54.3 8.2 %copy-start.2 = (bf16[8,256,1024]{2,1,0:T(8,128)(2,1)S(1)}, bf16[8,256,1024]{2,1,0:T(8,128)(2,1)}, u32[]{:S(2)}) copy-start(bf16[8,256,1024]{2,1,0:T(8,128)(2,1)} %param.9) | copy-start | bytes 12582916
  54.4 8.0 %collective-permute-start.9 = (bf16[3,192,256]{2,1,0:T(8,128)(2,1)S(1)}, bf16[3,192,256]{2,1,0:T(8,128)(2,1)S(1)}, u32[]{:S(2)}, u32[]{:S(2)}) collective-permute-start(bf16[3,192,256]{2,1,0:T(8,128)(2,1)S(1)} %pad_maximum_fusion.4), channel_id=1, source_target_pairs={{0,128},{16,144},{32,160},{48,176},{64,192},{80,208},{96,224},{112... | collective-permute-start | bytes 884744 | tf_op jit(solution)/shard_map/ppermute | solution.py:30
  63.6 1.8 %collective-permute-start.10 = (bf16[192,1024]{1,0:T(8,128)(2,1)S(1)}, bf16[192,1024]{1,0:T(8,128)(2,1)S(1)}, u32[]{:S(2)}, u32[]{:S(2)}) collective-permute-start(bf16[192,1024]{1,0:T(8,128)(2,1)S(1)} %fusion.14), channel_id=1, source_target_pairs={{0,1},{1,0},{2,3},{3,2},{4,5},{5,4},{6,7},{7,6},{8,9},{9,8},{10,11... | collective-permute-start | bytes 1179656 | tf_op jit(solution)/shard_map/ppermute | solution.py:8
  64.7 14.5 %copy-start.1 = (bf16[24,1024]{1,0:T(8,128)(2,1)S(1)}, bf16[24,1024]{1,0:T(8,128)(2,1)}, u32[]{:S(2)}) copy-start(bf16[24,1024]{1,0:T(8,128)(2,1)} %param.6) | copy-start | bytes 147460
  91.6 1.7 %collective-permute-start.11 = (bf16[192,1024]{1,0:T(8,128)(2,1)S(1)}, bf16[192,1024]{1,0:T(8,128)(2,1)S(1)}, u32[]{:S(2)}, u32[]{:S(2)}) collective-permute-start(bf16[192,1024]{1,0:T(8,128)(2,1)S(1)} %bitcast.103), channel_id=1, source_target_pairs={{0,1},{1,0},{2,3},{3,2},{4,5},{5,4},{6,7},{7,6},{8,9},{9,8},{10,11... | collective-permute-start | bytes 1179656 | tf_op jit(solution)/shard_map/ppermute | solution.py:8
  96.2 11.7 %collective-permute-start.12 = (bf16[3,192,256]{2,1,0:T(8,128)(2,1)S(1)}, bf16[3,192,256]{2,1,0:T(8,128)(2,1)S(1)}, u32[]{:S(2)}, u32[]{:S(2)}) collective-permute-start(bf16[3,192,256]{2,1,0:T(8,128)(2,1)S(1)} %pad_maximum_fusion.5), channel_id=1, source_target_pairs={{128,0},{144,16},{160,32},{176,48},{192,64},{208,80},{224,96},{240... | collective-permute-start | bytes 884744 | tf_op jit(solution)/shard_map/ppermute | solution.py:35
  97.5 6.2 %copy-start.3 = (bf16[8,256,1024]{2,1,0:T(8,128)(2,1)S(1)}, bf16[8,256,1024]{2,1,0:T(8,128)(2,1)}, u32[]{:S(2)}) copy-start(bf16[8,256,1024]{2,1,0:T(8,128)(2,1)} %param.9) | copy-start | bytes 12582916
  97.5 21.9 %collective-permute-start.13 = (bf16[5,192,256]{2,1,0:T(8,128)(2,1)S(1)}, bf16[5,192,256]{2,1,0:T(8,128)(2,1)S(1)}, u32[]{:S(2)}, u32[]{:S(2)}) collective-permute-start(bf16[5,192,256]{2,1,0:T(8,128)(2,1)S(1)} %get-tuple-element.34), channel_id=1, source_target_pairs={{128,0},{144,16},{160,32},{176,48},{192,64},{208,80},{224,96},{240... | collective-permute-start | bytes 1474568 | tf_op jit(solution)/shard_map/ppermute | solution.py:35
  108.1 7.5 %collective-permute-start.16 = (bf16[288,256]{1,0:T(8,128)(2,1)S(1)}, bf16[288,256]{1,0:T(8,128)(2,1)S(1)}, u32[]{:S(2)}, u32[]{:S(2)}) collective-permute-start(bf16[288,256]{1,0:T(8,128)(2,1)S(1)} %pad_maximum_fusion.9), channel_id=1, source_target_pairs={{0,96},{16,112},{32,0},{48,16},{64,32},{80,48},{96,64},{112,80},{1... | collective-permute-start | bytes 442376 | tf_op jit(solution)/shard_map/ppermute | solution.py:25
  110.2 25.4 %copy-start.5 = (bf16[192,1024]{1,0:T(8,128)(2,1)S(1)}, bf16[192,1024]{1,0:T(8,128)(2,1)}, u32[]{:S(2)}) copy-start(bf16[192,1024]{1,0:T(8,128)(2,1)} %copy-done.4) | copy-start | bytes 1179652
  110.2 9.2 %collective-permute-start.14 = (bf16[288,256]{1,0:T(8,128)(2,1)S(1)}, bf16[288,256]{1,0:T(8,128)(2,1)S(1)}, u32[]{:S(2)}, u32[]{:S(2)}) collective-permute-start(bf16[288,256]{1,0:T(8,128)(2,1)S(1)} %pad_maximum_fusion.8), channel_id=1, source_target_pairs={{0,32},{16,48},{32,64},{48,80},{64,96},{80,112},{96,0},{112,16},{1... | collective-permute-start | bytes 442376 | tf_op jit(solution)/shard_map/ppermute | solution.py:25
  119.6 7.8 %collective-permute-start.15 = (bf16[192,256]{1,0:T(8,128)(2,1)S(1)}, bf16[192,256]{1,0:T(8,128)(2,1)S(1)}, u32[]{:S(2)}, u32[]{:S(2)}) collective-permute-start(bf16[192,256]{1,0:T(8,128)(2,1)S(1)} %get-tuple-element.26), channel_id=1, source_target_pairs={{0,16},{16,32},{32,48},{48,64},{64,80},{80,96},{96,112},{112,0},{1... | collective-permute-start | bytes 294920 | tf_op jit(solution)/shard_map/ppermute | solution.py:25
  121.4 6.0 %collective-permute-start.19 = (bf16[192,256]{1,0:T(8,128)(2,1)S(1)}, bf16[192,256]{1,0:T(8,128)(2,1)S(1)}, u32[]{:S(2)}, u32[]{:S(2)}) collective-permute-start(bf16[192,256]{1,0:T(8,128)(2,1)S(1)} %get-tuple-element.27), channel_id=1, source_target_pairs={{0,96},{16,112},{32,0},{48,16},{64,32},{80,48},{96,64},{112,80},{1... | collective-permute-start | bytes 294920 | tf_op jit(solution)/shard_map/ppermute | solution.py:25
  122.7 8.0 %collective-permute-start.18 = (bf16[192,256]{1,0:T(8,128)(2,1)S(1)}, bf16[192,256]{1,0:T(8,128)(2,1)S(1)}, u32[]{:S(2)}, u32[]{:S(2)}) collective-permute-start(bf16[192,256]{1,0:T(8,128)(2,1)S(1)} %get-tuple-element.28), channel_id=1, source_target_pairs={{0,32},{16,48},{32,64},{48,80},{64,96},{80,112},{96,0},{112,16},{1... | collective-permute-start | bytes 294920 | tf_op jit(solution)/shard_map/ppermute | solution.py:25
  124.3 6.4 %collective-permute-start.17 = (bf16[192,256]{1,0:T(8,128)(2,1)S(1)}, bf16[192,256]{1,0:T(8,128)(2,1)S(1)}, u32[]{:S(2)}, u32[]{:S(2)}) collective-permute-start(bf16[192,256]{1,0:T(8,128)(2,1)S(1)} %get-tuple-element.29), channel_id=1, source_target_pairs={{0,112},{16,0},{32,16},{48,32},{64,48},{80,64},{96,80},{112,96},{1... | collective-permute-start | bytes 294920 | tf_op jit(solution)/shard_map/ppermute | solution.py:25
  130.8 4.7 %collective-permute-start.20 = (bf16[192,256]{1,0:T(8,128)(2,1)S(1)}, bf16[192,256]{1,0:T(8,128)(2,1)S(1)}, u32[]{:S(2)}, u32[]{:S(2)}) collective-permute-start(bf16[192,256]{1,0:T(8,128)(2,1)S(1)} %fusion.36), channel_id=1, source_target_pairs={{0,16},{16,0},{32,48},{48,32},{64,80},{80,64},{96,112},{112,96},{1... | collective-permute-start | bytes 294920 | tf_op jit(solution)/shard_map/ppermute | solution.py:8

commit v8 on v6

--- a/solution.py
+++ b/solution.py
@@ -48,7 +48,7 @@
         return lax.dynamic_update_index_in_dim(stack, block, place, 0)
 
     near = {0: own}
-    for distance in (1, -1, 2, -2):
+    for distance in (-2, 2, -1, 1):
         near[distance] = along_ring(own, -distance)
     behind = along_ring(jnp.concatenate([near[-1], near[-2][:half]], 0), 2)
     ahead = along_ring(jnp.concatenate([near[1], near[2][half:]], 0), -2)
@@ -119,8 +119,7 @@
     rows, width = x.shape
     copies = jnp.broadcast_to(x[None], (chips, rows, width))
     own = exchanged(copies, "latent", same_core_groups(size)).reshape(chips * rows, width)
-    other = from_partner(own, "latent", 1)
-    return jnp.concatenate([own, other], 0)
+    return own, from_partner(own, "latent", 1)
 
 
 def rows_summed(own, other):
@@ -143,12 +142,15 @@
     layer_count = places // 2
     latent_cols = enc_weight.shape[1]
 
-    inputs_half = rows_of_all(layer_inputs)
-    total_rows = inputs_half.shape[0]
-    half_rows = total_rows // 2
-    own_part = jnp.dot(inputs_half, enc_weight, preferred_element_type=jnp.float32)
-    kept = lax.dynamic_slice_in_dim(own_part, which_half * half_rows, half_rows, 0)
-    given = lax.dynamic_slice_in_dim(own_part, (1 - which_half) * half_rows, half_rows, 0)
+    inputs_pair = rows_of_all(layer_inputs)
+    half_rows = inputs_pair[0].shape[0]
+    total_rows = 2 * half_rows
+    parts = [
+        jnp.dot(rows, enc_weight, preferred_element_type=jnp.float32) for rows in inputs_pair
+    ]
+    first = which_half == 0
+    kept = jnp.where(first, parts[0], parts[1])
+    given = jnp.where(first, parts[1], parts[0])
     bias = lax.dynamic_slice_in_dim(enc_bias, layer_now, 1, 0)
     pre_half = kept + from_partner(given, "layer", 1) + bias
     latents_half = jnp.maximum(pre_half, 0.0).astype(jnp.bfloat16)
@@ -170,7 +172,7 @@
     )
     rscale = total_rows ** (-0.5)
     grad_own = ((recon_own - mlp_outputs.astype(jnp.float32)) * rscale).astype(jnp.bfloat16)
-    out_grad = rows_of_all(grad_own)
+    out_grad = jnp.concatenate(rows_of_all(grad_own), 0)
 
     near = layer_count // 2
     lower = layer_terms(out_grad, dec_weight[:near], used[:near])
@@ -186,12 +188,11 @@
     )
     pre_grad = jnp.where(latents_half > 0, lat_grad, 0.0).astype(jnp.bfloat16)
     pre_other = from_partner(pre_grad, "layer", 1)
-    first = which_half == 0
     pre_all = jnp.concatenate(
         [jnp.where(first, pre_grad, pre_other), jnp.where(first, pre_other, pre_grad)], 0
     )
     enc_grad = lax.dot_general(
-        inputs_half, pre_all, (((0,), (0,)), ((), ())), preferred_element_type=jnp.float32
+        jnp.concatenate(inputs_pair, 0), pre_all, (((0,), (0,)), ((), ())), preferred_element_type=jnp.float32
     )
     return (enc_grad, dec_grad)
 

time: 138 us -> 138 us (level)
  transfers between devices with their start and end apart: 21 -> 21, of which waited for: 14 -> 15; matrix products, arithmetic and copies ran while one was open for 6% -> 6% of each run, Pallas kernels for 0% -> 0%
where the time goes in v8:
time: 138 us; the launch traced here: 137 us
  blocking collectives  42.3 us (31%)
  waiting for transfers between devices  41.3 us (30%)
  starting transfers between devices  36.2 us (26%)
  matrix products  12.1 us (9%)
  local copies, waits for them, and re-layouts  2.29 us (2%)
  other arithmetic  1.93 us (1%)
    all_to_all x3, blocking collectives, exchanged(): lax.all_to_all(parts, axis, split_axis=0, concat_axis=0, tiled=True, axis...  42.3 us
    ppermute x12, starting transfers between devices, along_ring(): return lax.ppermute(x, 'layer', pairs)  23.5 us
    ppermute x12, waiting for transfers between devices, along_ring(): return lax.ppermute(x, 'layer', pairs)  22.2 us
    ppermute x5, waiting for transfers between devices, from_partner(): lax.ppermute(x, axis, [(i, i ^ bit) for i in range(lax.axis_size(axis))])  11.9 us
    ppermute x2, starting transfers between devices, to_later_plane(): return lax.ppermute(x, 'layer', [(i, i + ring) for i in range(ring)])  6.35 us
    dot_general x1, matrix products, local(): lax.dot_general(latents, grad_after, (((1,), (0,)), ((), ())), preferred_...  4.4 us
    ppermute x2, waiting for transfers between devices, to_later_plane(): return lax.ppermute(x, 'layer', [(i, i + ring) for i in range(ring)])  3.98 us
    dot_general x2, matrix products, layer_terms(): lax.dot_general(weight, out_grad, (((2,), (1,)), ((), ())), preferred_ele...  3.77 us
  transfers between devices with their start and end apart: 21, of which 15 were waited for; matrix products, arithmetic and copies ran while one was open for 6% of the time, Pallas kernels for 0%

profile of v8, /device:TPU:2, one launch (start us, length us, event | category | flops | bytes accessed | tf_op | source)
XLA Modules:
  0.0 137.3 jit_solution(4179285261956306641)
XLA Ops:
  1.5 16.3 %all_to_all.15 = bf16[8,24,1024]{2,1,0:T(8,128)(2,1)S(1)} all-to-all(bf16[8,24,1024]{2,1,0:T(8,128)(2,1)S(1)} %broadcast_in_dim.72), channel_id=1, replica_groups={{0,2,4,6,8,10,12,14},{1,3,5,7,9,11,13,15},{16,18,20,22,24,26,28,30},{17..., dimensions={0} | all-to-all | bytes 786432 | tf_op jit(solution)/shard_map/all_to_all | solution.py:16
  18.1 1.4 %collective-permute-done = bf16[192,1024]{1,0:T(8,128)(2,1)S(1)} collective-permute-done((bf16[192,1024]{1,0:T(8,128)(2,1)S(1)}, bf16[192,1024]{1,0:T(8,128)(2,1)S(1)}, u32[]{:S(2)}, u32[]{:S(2)}) %collective-permute-start) | collective-permute-done | bytes 393248 | tf_op jit(solution)/shard_map/ppermute | solution.py:8
  19.8 2.0 %collective-permute-start.1 = (f32[192,256]{1,0:T(8,128)S(1)}, f32[192,256]{1,0:T(8,128)S(1)}, u32[]{:S(2)}, u32[]{:S(2)}) collective-permute-start(f32[192,256]{1,0:T(8,128)S(1)} %get-tuple-element.43), channel_id=1, source_target_pairs={{0,16},{16,0},{32,48},{48,32},{64,80},{80,64},{96,112},{112,96},{1... | collective-permute-start | bytes 589832 | tf_op jit(solution)/shard_map/ppermute | solution.py:8
  22.5 4.5 %collective-permute-done.1 = f32[192,256]{1,0:T(8,128)S(1)} collective-permute-done((f32[192,256]{1,0:T(8,128)S(1)}, f32[192,256]{1,0:T(8,128)S(1)}, u32[]{:S(2)}, u32[]{:S(2)}) %collective-permute-start.1) | collective-permute-done | bytes 196640 | tf_op jit(solution)/shard_map/ppermute | solution.py:8
  27.1 3.3 %collective-permute-start.3 = (bf16[192,256]{1,0:T(8,128)(2,1)S(1)}, bf16[192,256]{1,0:T(8,128)(2,1)S(1)}, u32[]{:S(2)}, u32[]{:S(2)}) collective-permute-start(bf16[192,256]{1,0:T(8,128)(2,1)S(1)} %get-tuple-element.25), channel_id=1, source_target_pairs={{0,32},{16,48},{32,64},{48,80},{64,96},{80,112},{96,0},{112,16},{1... | collective-permute-start | bytes 294920 | tf_op jit(solution)/shard_map/ppermute | solution.py:25
  30.4 2.9 %collective-permute-start.6 = (bf16[192,256]{1,0:T(8,128)(2,1)S(1)}, bf16[192,256]{1,0:T(8,128)(2,1)S(1)}, u32[]{:S(2)}, u32[]{:S(2)}) collective-permute-start(bf16[192,256]{1,0:T(8,128)(2,1)S(1)} %get-tuple-element.25), channel_id=1, source_target_pairs={{0,96},{16,112},{32,0},{48,16},{64,32},{80,48},{96,64},{112,80},{1... | collective-permute-start | bytes 294920 | tf_op jit(solution)/shard_map/ppermute | solution.py:25
  33.4 2.4 %collective-permute-start.5 = (bf16[192,256]{1,0:T(8,128)(2,1)S(1)}, bf16[192,256]{1,0:T(8,128)(2,1)S(1)}, u32[]{:S(2)}, u32[]{:S(2)}) collective-permute-start(bf16[192,256]{1,0:T(8,128)(2,1)S(1)} %get-tuple-element.25), channel_id=1, source_target_pairs={{0,112},{16,0},{32,16},{48,32},{64,48},{80,64},{96,80},{112,96},{1... | collective-permute-start | bytes 294920 | tf_op jit(solution)/shard_map/ppermute | solution.py:25
  36.4 3.1 %collective-permute-done.6 = bf16[192,256]{1,0:T(8,128)(2,1)S(1)} collective-permute-done((bf16[192,256]{1,0:T(8,128)(2,1)S(1)}, bf16[192,256]{1,0:T(8,128)(2,1)S(1)}, u32[]{:S(2)}, u32[]{:S(2)}) %collective-permute-start.6) | collective-permute-done | bytes 98336 | tf_op jit(solution)/shard_map/ppermute | solution.py:25
  39.5 2.1 %collective-permute-done.2 = bf16[192,256]{1,0:T(8,128)(2,1)S(1)} collective-permute-done((bf16[192,256]{1,0:T(8,128)(2,1)S(1)}, bf16[192,256]{1,0:T(8,128)(2,1)S(1)}, u32[]{:S(2)}, u32[]{:S(2)}) %collective-permute-start.2) | collective-permute-done | bytes 98336 | tf_op jit(solution)/shard_map/ppermute | solution.py:25
  41.6 2.6 %collective-permute-start.8 = (bf16[5,192,256]{2,1,0:T(8,128)(2,1)S(1)}, bf16[5,192,256]{2,1,0:T(8,128)(2,1)S(1)}, u32[]{:S(2)}, u32[]{:S(2)}) collective-permute-start(bf16[5,192,256]{2,1,0:T(8,128)(2,1)S(1)} %bitcast_dynamic-update-slice_fusion.1), channel_id=1, source_target_pairs={{0,128},{16,144},{32,160},{48,176},{64,192},{80,208},{96,224},{112... | collective-permute-start | bytes 1474568 | tf_op jit(solution)/shard_map/ppermute | solution.py:30
  44.3 2.2 %collective-permute-start.4 = (bf16[288,256]{1,0:T(8,128)(2,1)S(1)}, bf16[288,256]{1,0:T(8,128)(2,1)S(1)}, u32[]{:S(2)}, u32[]{:S(2)}) collective-permute-start(bf16[288,256]{1,0:T(8,128)(2,1)S(1)} %pad_maximum_fusion.3), channel_id=1, source_target_pairs={{0,32},{16,48},{32,64},{48,80},{64,96},{80,112},{96,0},{112,16},{1... | collective-permute-start | bytes 442376 | tf_op jit(solution)/shard_map/ppermute | solution.py:25
  46.6 2.0 %collective-permute-start.7 = (bf16[288,256]{1,0:T(8,128)(2,1)S(1)}, bf16[288,256]{1,0:T(8,128)(2,1)S(1)}, u32[]{:S(2)}, u32[]{:S(2)}) collective-permute-start(bf16[288,256]{1,0:T(8,128)(2,1)S(1)} %pad_maximum_fusion.4), channel_id=1, source_target_pairs={{0,96},{16,112},{32,0},{48,16},{64,32},{80,48},{96,64},{112,80},{1... | collective-permute-start | bytes 442376 | tf_op jit(solution)/shard_map/ppermute | solution.py:25
  48.8 4.5 %collective-permute-done.4 = bf16[288,256]{1,0:T(8,128)(2,1)S(1)} collective-permute-done((bf16[288,256]{1,0:T(8,128)(2,1)S(1)}, bf16[288,256]{1,0:T(8,128)(2,1)S(1)}, u32[]{:S(2)}, u32[]{:S(2)}) %collective-permute-start.4) | collective-permute-done | bytes 147488 | tf_op jit(solution)/shard_map/ppermute | solution.py:25
  53.4 3.7 %collective-permute-start.9 = (bf16[3,192,256]{2,1,0:T(8,128)(2,1)S(1)}, bf16[3,192,256]{2,1,0:T(8,128)(2,1)S(1)}, u32[]{:S(2)}, u32[]{:S(2)}) collective-permute-start(bf16[3,192,256]{2,1,0:T(8,128)(2,1)S(1)} %pad_maximum_fusion.1), channel_id=1, source_target_pairs={{0,128},{16,144},{32,160},{48,176},{64,192},{80,208},{96,224},{112... | collective-permute-start | bytes 884744 | tf_op jit(solution)/shard_map/ppermute | solution.py:30
  57.4 4.0 %collective-permute-done.9 = bf16[3,192,256]{2,1,0:T(8,128)(2,1)S(1)} collective-permute-done((bf16[3,192,256]{2,1,0:T(8,128)(2,1)S(1)}, bf16[3,192,256]{2,1,0:T(8,128)(2,1)S(1)}, u32[]{:S(2)}, u32[]{:S(2)}) %collective-permute-start.9) | collective-permute-done | bytes 294944 | tf_op jit(solution)/shard_map/ppermute | solution.py:30
  64.5 13.6 %all_to_all.16 = bf16[8,24,1024]{2,1,0:T(8,128)(2,1)S(1)} all-to-all(bf16[8,24,1024]{2,1,0:T(8,128)(2,1)S(1)} %bitcast.104), channel_id=1, replica_groups={{0,2,4,6,8,10,12,14},{1,3,5,7,9,11,13,15},{16,18,20,22,24,26,28,30},{17..., dimensions={0} | all-to-all | bytes 786432 | tf_op jit(solution)/shard_map/all_to_all | solution.py:16
  78.3 12.4 %all_to_all.17 = bf16[8,24,1024]{2,1,0:T(8,128)(2,1)S(1)} all-to-all(bf16[8,24,1024]{2,1,0:T(8,128)(2,1)S(1)} %broadcast_in_dim.80), channel_id=1, replica_groups={{0,2,4,6,8,10,12,14},{1,3,5,7,9,11,13,15},{16,18,20,22,24,26,28,30},{17..., dimensions={0} | all-to-all | bytes 786432 | tf_op jit(solution)/shard_map/all_to_all | solution.py:16
  90.7 1.8 %collective-permute-done.11 = bf16[192,1024]{1,0:T(8,128)(2,1)} collective-permute-done((bf16[192,1024]{1,0:T(8,128)(2,1)S(1)}, bf16[192,1024]{1,0:T(8,128)(2,1)}, u32[]{:S(2)}, u32[]{:S(2)}) %collective-permute-start.11) | collective-permute-done | bytes 393248 | tf_op jit(solution)/shard_map/ppermute | solution.py:8
  93.5 2.7 %fusion.8 = bf16[4,384,256]{2,1,0:T(8,128)(2,1)S(1)} fusion(bf16[8,256,1024]{2,1,0:T(8,128)(2,1)} %param.9, pred[4]{0:T(512)(128)(4,1)S(1)} %get-tuple-element.42, bf16[192,1024]{1,0:T(8,128)(2,1)} %collective-permute-done.11, bf16[192,1024]{1,0:T(8,128)(2,1)S(1)} %bitcast.103), kind=kOutput, calls=%fused_computation.8 | convolution fusion | flops 807665664 | bytes 3670020 | tf_op jit(solution)/shard_map/dot_general | solution.py:76
  96.5 1.3 collective-permute-start.12
  97.8 1.7 %collective-permute-start.13 = (bf16[5,192,256]{2,1,0:T(8,128)(2,1)S(1)}, bf16[5,192,256]{2,1,0:T(8,128)(2,1)S(1)}, u32[]{:S(2)}, u32[]{:S(2)}) collective-permute-start(bf16[5,192,256]{2,1,0:T(8,128)(2,1)S(1)} %get-tuple-element.34), channel_id=1, source_target_pairs={{128,0},{144,16},{160,32},{176,48},{192,64},{208,80},{224,96},{240... | collective-permute-start | bytes 1474568 | tf_op jit(solution)/shard_map/ppermute | solution.py:35
  99.5 4.4 %convolution_convert_fusion = bf16[8,256,1024]{2,1,0:T(8,128)(2,1)} fusion(bf16[8,384,256]{2,1,0:T(8,128)(2,1)S(1)} %bitcast_select_fusion, bf16[384,1024]{1,0:T(8,128)(2,1)S(1)} %pad_maximum_fusion), kind=kOutput, calls=%fused_computation | convolution fusion | flops 1612709888 | bytes 6553600 | tf_op jit(solution)/shard_map/dot_general | solution.py:182
  105.0 3.3 %collective-permute-done.12 = bf16[3,192,256]{2,1,0:T(8,128)(2,1)S(1)} collective-permute-done((bf16[3,192,256]{2,1,0:T(8,128)(2,1)S(1)}, bf16[3,192,256]{2,1,0:T(8,128)(2,1)S(1)}, u32[]{:S(2)}, u32[]{:S(2)}) %collective-permute-start.12) | collective-permute-done | bytes 294944 | tf_op jit(solution)/shard_map/ppermute | solution.py:35
  108.4 2.8 %collective-permute-start.16 = (bf16[288,256]{1,0:T(8,128)(2,1)S(1)}, bf16[288,256]{1,0:T(8,128)(2,1)S(1)}, u32[]{:S(2)}, u32[]{:S(2)}) collective-permute-start(bf16[288,256]{1,0:T(8,128)(2,1)S(1)} %pad_maximum_fusion.6), channel_id=1, source_target_pairs={{0,96},{16,112},{32,0},{48,16},{64,32},{80,48},{96,64},{112,80},{1... | collective-permute-start | bytes 442376 | tf_op jit(solution)/shard_map/ppermute | solution.py:25
  111.4 4.0 %collective-permute-done.16 = bf16[288,256]{1,0:T(8,128)(2,1)S(1)} collective-permute-done((bf16[288,256]{1,0:T(8,128)(2,1)S(1)}, bf16[288,256]{1,0:T(8,128)(2,1)S(1)}, u32[]{:S(2)}, u32[]{:S(2)}) %collective-permute-start.16) | collective-permute-done | bytes 147488 | tf_op jit(solution)/shard_map/ppermute | solution.py:25
  115.4 4.4 %collective-permute-done.14 = bf16[288,256]{1,0:T(8,128)(2,1)S(1)} collective-permute-done((bf16[288,256]{1,0:T(8,128)(2,1)S(1)}, bf16[288,256]{1,0:T(8,128)(2,1)S(1)}, u32[]{:S(2)}, u32[]{:S(2)}) %collective-permute-start.14) | collective-permute-done | bytes 147488 | tf_op jit(solution)/shard_map/ppermute | solution.py:25
  121.0 2.0 %collective-permute-start.19 = (bf16[192,256]{1,0:T(8,128)(2,1)S(1)}, bf16[192,256]{1,0:T(8,128)(2,1)S(1)}, u32[]{:S(2)}, u32[]{:S(2)}) collective-permute-start(bf16[192,256]{1,0:T(8,128)(2,1)S(1)} %get-tuple-element.27), channel_id=1, source_target_pairs={{0,96},{16,112},{32,0},{48,16},{64,32},{80,48},{96,64},{112,80},{1... | collective-permute-start | bytes 294920 | tf_op jit(solution)/shard_map/ppermute | solution.py:25
  124.0 3.5 %collective-permute-start.17 = (bf16[192,256]{1,0:T(8,128)(2,1)S(1)}, bf16[192,256]{1,0:T(8,128)(2,1)S(1)}, u32[]{:S(2)}, u32[]{:S(2)}) collective-permute-start(bf16[192,256]{1,0:T(8,128)(2,1)S(1)} %get-tuple-element.29), channel_id=1, source_target_pairs={{0,112},{16,0},{32,16},{48,32},{64,48},{80,64},{96,80},{112,96},{1... | collective-permute-start | bytes 294920 | tf_op jit(solution)/shard_map/ppermute | solution.py:25
  128.0 3.0 %collective-permute-done.18 = bf16[192,256]{1,0:T(8,128)(2,1)S(1)} collective-permute-done((bf16[192,256]{1,0:T(8,128)(2,1)S(1)}, bf16[192,256]{1,0:T(8,128)(2,1)S(1)}, u32[]{:S(2)}, u32[]{:S(2)}) %collective-permute-start.18) | collective-permute-done | bytes 98336 | tf_op jit(solution)/shard_map/ppermute | solution.py:25
  131.1 1.2 collective-permute-start.20
  132.3 3.5 %collective-permute-done.20 = bf16[192,256]{1,0:T(8,128)(2,1)S(1)} collective-permute-done((bf16[192,256]{1,0:T(8,128)(2,1)S(1)}, bf16[192,256]{1,0:T(8,128)(2,1)S(1)}, u32[]{:S(2)}, u32[]{:S(2)}) %collective-permute-start.20) | collective-permute-done | bytes 98336 | tf_op jit(solution)/shard_map/ppermute | solution.py:8
  135.8 1.4 %fusion.20 = f32[1024,256]{1,0:T(8,128)} fusion(bf16[192,1024]{1,0:T(8,128)(2,1)S(1)} %copy-done.2, bf16[192,1024]{1,0:T(8,128)(2,1)S(1)} %bitcast.100, bf16[192,256]{1,0:T(8,128)(2,1)S(1)} %get-tuple-element.38, bf16[192,256]{1,0:T(8,128)(2,1)S(1)} %get-tuple-element.37), kind=kOutput, calls=%fused_computation.16 | convolution fusion | flops 203292672 | bytes 2031616 | tf_op jit(solution)/shard_map/dot_general | solution.py:194
  (91 shorter events, 12.0 us)
Async XLA Ops:
  0.6 17.2 %copy-start = (bf16[1024,256]{1,0:T(8,128)(2,1)S(1)}, bf16[1024,256]{1,0:T(8,128)(2,1)}, u32[]{:S(2)}) copy-start(bf16[1024,256]{1,0:T(8,128)(2,1)} %param.7) | copy-start | bytes 1572868
  17.8 1.7 %collective-permute-start = (bf16[192,1024]{1,0:T(8,128)(2,1)S(1)}, bf16[192,1024]{1,0:T(8,128)(2,1)S(1)}, u32[]{:S(2)}, u32[]{:S(2)}) collective-permute-start(bf16[192,1024]{1,0:T(8,128)(2,1)S(1)} %bitcast.98), channel_id=1, source_target_pairs={{0,1},{1,0},{2,3},{3,2},{4,5},{5,4},{6,7},{7,6},{8,9},{9,8},{10,11... | collective-permute-start | bytes 1179656 | tf_op jit(solution)/shard_map/ppermute | solution.py:8
  19.5 22.1 %copy-start.1 = (bf16[192,1024]{1,0:T(8,128)(2,1)}, bf16[192,1024]{1,0:T(8,128)(2,1)S(1)}, u32[]{:S(2)}) copy-start(bf16[192,1024]{1,0:T(8,128)(2,1)S(1)} %collective-permute-done) | copy-start | bytes 1179652
  19.8 7.2 %collective-permute-start.1 = (f32[192,256]{1,0:T(8,128)S(1)}, f32[192,256]{1,0:T(8,128)S(1)}, u32[]{:S(2)}, u32[]{:S(2)}) collective-permute-start(f32[192,256]{1,0:T(8,128)S(1)} %get-tuple-element.43), channel_id=1, source_target_pairs={{0,16},{16,0},{32,48},{48,32},{64,80},{80,64},{96,112},{112,96},{1... | collective-permute-start | bytes 589832 | tf_op jit(solution)/shard_map/ppermute | solution.py:8
  27.1 9.3 %collective-permute-start.3 = (bf16[192,256]{1,0:T(8,128)(2,1)S(1)}, bf16[192,256]{1,0:T(8,128)(2,1)S(1)}, u32[]{:S(2)}, u32[]{:S(2)}) collective-permute-start(bf16[192,256]{1,0:T(8,128)(2,1)S(1)} %get-tuple-element.25), channel_id=1, source_target_pairs={{0,32},{16,48},{32,64},{48,80},{64,96},{80,112},{96,0},{112,16},{1... | collective-permute-start | bytes 294920 | tf_op jit(solution)/shard_map/ppermute | solution.py:25
  30.4 9.1 %collective-permute-start.6 = (bf16[192,256]{1,0:T(8,128)(2,1)S(1)}, bf16[192,256]{1,0:T(8,128)(2,1)S(1)}, u32[]{:S(2)}, u32[]{:S(2)}) collective-permute-start(bf16[192,256]{1,0:T(8,128)(2,1)S(1)} %get-tuple-element.25), channel_id=1, source_target_pairs={{0,96},{16,112},{32,0},{48,16},{64,32},{80,48},{96,64},{112,80},{1... | collective-permute-start | bytes 294920 | tf_op jit(solution)/shard_map/ppermute | solution.py:25
  33.4 8.2 %collective-permute-start.5 = (bf16[192,256]{1,0:T(8,128)(2,1)S(1)}, bf16[192,256]{1,0:T(8,128)(2,1)S(1)}, u32[]{:S(2)}, u32[]{:S(2)}) collective-permute-start(bf16[192,256]{1,0:T(8,128)(2,1)S(1)} %get-tuple-element.25), channel_id=1, source_target_pairs={{0,112},{16,0},{32,16},{48,32},{64,48},{80,64},{96,80},{112,96},{1... | collective-permute-start | bytes 294920 | tf_op jit(solution)/shard_map/ppermute | solution.py:25
  35.8 5.8 %collective-permute-start.2 = (bf16[192,256]{1,0:T(8,128)(2,1)S(1)}, bf16[192,256]{1,0:T(8,128)(2,1)S(1)}, u32[]{:S(2)}, u32[]{:S(2)}) collective-permute-start(bf16[192,256]{1,0:T(8,128)(2,1)S(1)} %get-tuple-element.25), channel_id=1, source_target_pairs={{0,16},{16,32},{32,48},{48,64},{64,80},{80,96},{96,112},{112,0},{1... | collective-permute-start | bytes 294920 | tf_op jit(solution)/shard_map/ppermute | solution.py:25
  41.6 11.7 %collective-permute-start.8 = (bf16[5,192,256]{2,1,0:T(8,128)(2,1)S(1)}, bf16[5,192,256]{2,1,0:T(8,128)(2,1)S(1)}, u32[]{:S(2)}, u32[]{:S(2)}) collective-permute-start(bf16[5,192,256]{2,1,0:T(8,128)(2,1)S(1)} %bitcast_dynamic-update-slice_fusion.1), channel_id=1, source_target_pairs={{0,128},{16,144},{32,160},{48,176},{64,192},{80,208},{96,224},{112... | collective-permute-start | bytes 1474568 | tf_op jit(solution)/shard_map/ppermute | solution.py:30
  44.3 9.0 %collective-permute-start.4 = (bf16[288,256]{1,0:T(8,128)(2,1)S(1)}, bf16[288,256]{1,0:T(8,128)(2,1)S(1)}, u32[]{:S(2)}, u32[]{:S(2)}) collective-permute-start(bf16[288,256]{1,0:T(8,128)(2,1)S(1)} %pad_maximum_fusion.3), channel_id=1, source_target_pairs={{0,32},{16,48},{32,64},{48,80},{64,96},{80,112},{96,0},{112,16},{1... | collective-permute-start | bytes 442376 | tf_op jit(solution)/shard_map/ppermute | solution.py:25
  46.6 6.7 %collective-permute-start.7 = (bf16[288,256]{1,0:T(8,128)(2,1)S(1)}, bf16[288,256]{1,0:T(8,128)(2,1)S(1)}, u32[]{:S(2)}, u32[]{:S(2)}) collective-permute-start(bf16[288,256]{1,0:T(8,128)(2,1)S(1)} %pad_maximum_fusion.4), channel_id=1, source_target_pairs={{0,96},{16,112},{32,0},{48,16},{64,32},{80,48},{96,64},{112,80},{1... | collective-permute-start | bytes 442376 | tf_op jit(solution)/shard_map/ppermute | solution.py:25
  53.4 8.0 %collective-permute-start.9 = (bf16[3,192,256]{2,1,0:T(8,128)(2,1)S(1)}, bf16[3,192,256]{2,1,0:T(8,128)(2,1)S(1)}, u32[]{:S(2)}, u32[]{:S(2)}) collective-permute-start(bf16[3,192,256]{2,1,0:T(8,128)(2,1)S(1)} %pad_maximum_fusion.1), channel_id=1, source_target_pairs={{0,128},{16,144},{32,160},{48,176},{64,192},{80,208},{96,224},{112... | collective-permute-start | bytes 884744 | tf_op jit(solution)/shard_map/ppermute | solution.py:30
  57.3 4.3 %copy-start.4 = (bf16[8,256,1024]{2,1,0:T(8,128)(2,1)S(1)}, bf16[8,256,1024]{2,1,0:T(8,128)(2,1)}, u32[]{:S(2)}) copy-start(bf16[8,256,1024]{2,1,0:T(8,128)(2,1)} %param.9) | copy-start | bytes 12582916
  62.6 1.8 %collective-permute-start.10 = (bf16[192,1024]{1,0:T(8,128)(2,1)S(1)}, bf16[192,1024]{1,0:T(8,128)(2,1)S(1)}, u32[]{:S(2)}, u32[]{:S(2)}) collective-permute-start(bf16[192,1024]{1,0:T(8,128)(2,1)S(1)} %fusion.14), channel_id=1, source_target_pairs={{0,1},{1,0},{2,3},{3,2},{4,5},{5,4},{6,7},{7,6},{8,9},{9,8},{10,11... | collective-permute-start | bytes 1179656 | tf_op jit(solution)/shard_map/ppermute | solution.py:8
  63.7 14.5 %copy-start.3 = (bf16[24,1024]{1,0:T(8,128)(2,1)S(1)}, bf16[24,1024]{1,0:T(8,128)(2,1)}, u32[]{:S(2)}) copy-start(bf16[24,1024]{1,0:T(8,128)(2,1)} %param.6) | copy-start | bytes 147460
  90.6 1.9 %collective-permute-start.11 = (bf16[192,1024]{1,0:T(8,128)(2,1)S(1)}, bf16[192,1024]{1,0:T(8,128)(2,1)}, u32[]{:S(2)}, u32[]{:S(2)}) collective-permute-start(bf16[192,1024]{1,0:T(8,128)(2,1)S(1)} %bitcast.101), channel_id=1, source_target_pairs={{0,1},{1,0},{2,3},{3,2},{4,5},{5,4},{6,7},{7,6},{8,9},{9,8},{10,11... | collective-permute-start | bytes 1179656 | tf_op jit(solution)/shard_map/ppermute | solution.py:8
  96.5 11.7 %collective-permute-start.12 = (bf16[3,192,256]{2,1,0:T(8,128)(2,1)S(1)}, bf16[3,192,256]{2,1,0:T(8,128)(2,1)S(1)}, u32[]{:S(2)}, u32[]{:S(2)}) collective-permute-start(bf16[3,192,256]{2,1,0:T(8,128)(2,1)S(1)} %pad_maximum_fusion.2), channel_id=1, source_target_pairs={{128,0},{144,16},{160,32},{176,48},{192,64},{208,80},{224,96},{240... | collective-permute-start | bytes 884744 | tf_op jit(solution)/shard_map/ppermute | solution.py:35
  97.8 6.2 %copy-start.5 = (bf16[8,256,1024]{2,1,0:T(8,128)(2,1)S(1)}, bf16[8,256,1024]{2,1,0:T(8,128)(2,1)}, u32[]{:S(2)}) copy-start(bf16[8,256,1024]{2,1,0:T(8,128)(2,1)} %param.9) | copy-start | bytes 12582916
  97.8 22.1 %collective-permute-start.13 = (bf16[5,192,256]{2,1,0:T(8,128)(2,1)S(1)}, bf16[5,192,256]{2,1,0:T(8,128)(2,1)S(1)}, u32[]{:S(2)}, u32[]{:S(2)}) collective-permute-start(bf16[5,192,256]{2,1,0:T(8,128)(2,1)S(1)} %get-tuple-element.34), channel_id=1, source_target_pairs={{128,0},{144,16},{160,32},{176,48},{192,64},{208,80},{224,96},{240... | collective-permute-start | bytes 1474568 | tf_op jit(solution)/shard_map/ppermute | solution.py:35
  108.4 7.1 %collective-permute-start.16 = (bf16[288,256]{1,0:T(8,128)(2,1)S(1)}, bf16[288,256]{1,0:T(8,128)(2,1)S(1)}, u32[]{:S(2)}, u32[]{:S(2)}) collective-permute-start(bf16[288,256]{1,0:T(8,128)(2,1)S(1)} %pad_maximum_fusion.6), channel_id=1, source_target_pairs={{0,96},{16,112},{32,0},{48,16},{64,32},{80,48},{96,64},{112,80},{1... | collective-permute-start | bytes 442376 | tf_op jit(solution)/shard_map/ppermute | solution.py:25
  111.1 24.7 %copy-start.2 = (bf16[192,1024]{1,0:T(8,128)(2,1)S(1)}, bf16[192,1024]{1,0:T(8,128)(2,1)}, u32[]{:S(2)}) copy-start(bf16[192,1024]{1,0:T(8,128)(2,1)} %copy-done.1) | copy-start | bytes 1179652
  111.1 8.7 %collective-permute-start.14 = (bf16[288,256]{1,0:T(8,128)(2,1)S(1)}, bf16[288,256]{1,0:T(8,128)(2,1)S(1)}, u32[]{:S(2)}, u32[]{:S(2)}) collective-permute-start(bf16[288,256]{1,0:T(8,128)(2,1)S(1)} %pad_maximum_fusion.5), channel_id=1, source_target_pairs={{0,32},{16,48},{32,64},{48,80},{64,96},{80,112},{96,0},{112,16},{1... | collective-permute-start | bytes 442376 | tf_op jit(solution)/shard_map/ppermute | solution.py:25
  120.0 8.0 %collective-permute-start.15 = (bf16[192,256]{1,0:T(8,128)(2,1)S(1)}, bf16[192,256]{1,0:T(8,128)(2,1)S(1)}, u32[]{:S(2)}, u32[]{:S(2)}) collective-permute-start(bf16[192,256]{1,0:T(8,128)(2,1)S(1)} %get-tuple-element.26), channel_id=1, source_target_pairs={{0,16},{16,32},{32,48},{48,64},{64,80},{80,96},{96,112},{112,0},{1... | collective-permute-start | bytes 294920 | tf_op jit(solution)/shard_map/ppermute | solution.py:25
  121.0 7.0 %collective-permute-start.19 = (bf16[192,256]{1,0:T(8,128)(2,1)S(1)}, bf16[192,256]{1,0:T(8,128)(2,1)S(1)}, u32[]{:S(2)}, u32[]{:S(2)}) collective-permute-start(bf16[192,256]{1,0:T(8,128)(2,1)S(1)} %get-tuple-element.27), channel_id=1, source_target_pairs={{0,96},{16,112},{32,0},{48,16},{64,32},{80,48},{96,64},{112,80},{1... | collective-permute-start | bytes 294920 | tf_op jit(solution)/shard_map/ppermute | solution.py:25
  123.1 7.9 %collective-permute-start.18 = (bf16[192,256]{1,0:T(8,128)(2,1)S(1)}, bf16[192,256]{1,0:T(8,128)(2,1)S(1)}, u32[]{:S(2)}, u32[]{:S(2)}) collective-permute-start(bf16[192,256]{1,0:T(8,128)(2,1)S(1)} %get-tuple-element.28), channel_id=1, source_target_pairs={{0,32},{16,48},{32,64},{48,80},{64,96},{80,112},{96,0},{112,16},{1... | collective-permute-start | bytes 294920 | tf_op jit(solution)/shard_map/ppermute | solution.py:25
  124.0 7.0 %collective-permute-start.17 = (bf16[192,256]{1,0:T(8,128)(2,1)S(1)}, bf16[192,256]{1,0:T(8,128)(2,1)S(1)}, u32[]{:S(2)}, u32[]{:S(2)}) collective-permute-start(bf16[192,256]{1,0:T(8,128)(2,1)S(1)} %get-tuple-element.29), channel_id=1, source_target_pairs={{0,112},{16,0},{32,16},{48,32},{64,48},{80,64},{96,80},{112,96},{1... | collective-permute-start | bytes 294920 | tf_op jit(solution)/shard_map/ppermute | solution.py:25
  131.1 4.7 %collective-permute-start.20 = (bf16[192,256]{1,0:T(8,128)(2,1)S(1)}, bf16[192,256]{1,0:T(8,128)(2,1)S(1)}, u32[]{:S(2)}, u32[]{:S(2)}) collective-permute-start(bf16[192,256]{1,0:T(8,128)(2,1)S(1)} %fusion.38), channel_id=1, source_target_pairs={{0,16},{16,0},{32,48},{48,32},{64,80},{80,64},{96,112},{112,96},{1... | collective-permute-start | bytes 294920 | tf_op jit(solution)/shard_map/ppermute | solution.py:8

commit v9 on v8

--- a/solution.py
+++ b/solution.py
@@ -172,11 +172,13 @@
     )
     rscale = total_rows ** (-0.5)
     grad_own = ((recon_own - mlp_outputs.astype(jnp.float32)) * rscale).astype(jnp.bfloat16)
-    out_grad = jnp.concatenate(rows_of_all(grad_own), 0)
+    grad_pair = rows_of_all(grad_own)
+    out_grad = jnp.concatenate(grad_pair, 0)
 
     near = layer_count // 2
     lower = layer_terms(out_grad, dec_weight[:near], used[:near])
-    lower, grad_after = lax.optimization_barrier((lower, out_grad))
+    lower, grad_pair = lax.optimization_barrier((lower, grad_pair))
+    grad_after = jnp.concatenate(grad_pair, 0)
     upper = layer_terms(grad_after, dec_weight[near:], used[near:])
     own_terms = jnp.where(plane == 1, upper, lower)
     dec_grad = lax.dot_general(

time: 138 us -> 138 us (level)
  matrix products: 12.1 us -> 14.2 us
    ppermute x2, waiting for transfers between devices: 3.26 us -> 1.55 us  [to_earlier_plane(): return lax.ppermute(x, 'layer', [(i + ring, i) for i in range(ring)])]
  transfers between devices with their start and end apart: 21 -> 21, of which waited for: 15 -> 15; matrix products, arithmetic and copies ran while one was open for 6% -> 7% of each run, Pallas kernels for 0% -> 0%
where the time goes in v9:
time: 138 us; the launch traced here: 137 us
  blocking collectives  42.3 us (31%)
  waiting for transfers between devices  41 us (30%)
  starting transfers between devices  35.1 us (25%)
  matrix products  14.2 us (10%)
  local copies, waits for them, and re-layouts  2.29 us (2%)
    all_to_all x3, blocking collectives, exchanged(): lax.all_to_all(parts, axis, split_axis=0, concat_axis=0, tiled=True, axis...  42.3 us
    ppermute x12, starting transfers between devices, along_ring(): return lax.ppermute(x, 'layer', pairs)  23.5 us
    ppermute x12, waiting for transfers between devices, along_ring(): return lax.ppermute(x, 'layer', pairs)  22.8 us
    ppermute x5, waiting for transfers between devices, from_partner(): lax.ppermute(x, axis, [(i, i ^ bit) for i in range(lax.axis_size(axis))])  12.7 us
    ppermute x2, starting transfers between devices, to_later_plane(): return lax.ppermute(x, 'layer', [(i, i + ring) for i in range(ring)])  6.35 us
    dot_general x1, matrix products, local(): lax.dot_general(latents, grad_after, (((1,), (0,)), ((), ())), preferred_...  5.39 us
    dot_general x2, matrix products, layer_terms(): lax.dot_general(weight, out_grad, (((2,), (1,)), ((), ())), preferred_ele...  4.88 us
    ppermute x2, waiting for transfers between devices, to_later_plane(): return lax.ppermute(x, 'layer', [(i, i + ring) for i in range(ring)])  3.98 us
  transfers between devices with their start and end apart: 21, of which 15 were waited for; matrix products, arithmetic and copies ran while one was open for 7% of the time, Pallas kernels for 0%

profile of v9, /device:TPU:2, one launch (start us, length us, event | category | flops | bytes accessed | tf_op | source)
XLA Modules:
  0.0 136.9 jit_solution(15591334691334782170)
XLA Ops:
  1.5 16.3 %all_to_all.15 = bf16[8,24,1024]{2,1,0:T(8,128)(2,1)S(1)} all-to-all(bf16[8,24,1024]{2,1,0:T(8,128)(2,1)S(1)} %broadcast_in_dim.72), channel_id=1, replica_groups={{0,2,4,6,8,10,12,14},{1,3,5,7,9,11,13,15},{16,18,20,22,24,26,28,30},{17..., dimensions={0} | all-to-all | bytes 786432 | tf_op jit(solution)/shard_map/all_to_all | solution.py:16
  18.1 1.4 %collective-permute-done = bf16[192,1024]{1,0:T(8,128)(2,1)S(1)} collective-permute-done((bf16[192,1024]{1,0:T(8,128)(2,1)S(1)}, bf16[192,1024]{1,0:T(8,128)(2,1)S(1)}, u32[]{:S(2)}, u32[]{:S(2)}) %collective-permute-start) | collective-permute-done | bytes 393248 | tf_op jit(solution)/shard_map/ppermute | solution.py:8
  19.8 2.0 %collective-permute-start.1 = (f32[192,256]{1,0:T(8,128)S(1)}, f32[192,256]{1,0:T(8,128)S(1)}, u32[]{:S(2)}, u32[]{:S(2)}) collective-permute-start(f32[192,256]{1,0:T(8,128)S(1)} %get-tuple-element.45), channel_id=1, source_target_pairs={{0,16},{16,0},{32,48},{48,32},{64,80},{80,64},{96,112},{112,96},{1... | collective-permute-start | bytes 589832 | tf_op jit(solution)/shard_map/ppermute | solution.py:8
  22.5 4.5 %collective-permute-done.1 = f32[192,256]{1,0:T(8,128)S(1)} collective-permute-done((f32[192,256]{1,0:T(8,128)S(1)}, f32[192,256]{1,0:T(8,128)S(1)}, u32[]{:S(2)}, u32[]{:S(2)}) %collective-permute-start.1) | collective-permute-done | bytes 196640 | tf_op jit(solution)/shard_map/ppermute | solution.py:8
  27.1 3.3 %collective-permute-start.3 = (bf16[192,256]{1,0:T(8,128)(2,1)S(1)}, bf16[192,256]{1,0:T(8,128)(2,1)S(1)}, u32[]{:S(2)}, u32[]{:S(2)}) collective-permute-start(bf16[192,256]{1,0:T(8,128)(2,1)S(1)} %get-tuple-element.27), channel_id=1, source_target_pairs={{0,32},{16,48},{32,64},{48,80},{64,96},{80,112},{96,0},{112,16},{1... | collective-permute-start | bytes 294920 | tf_op jit(solution)/shard_map/ppermute | solution.py:25
  30.4 2.9 %collective-permute-start.6 = (bf16[192,256]{1,0:T(8,128)(2,1)S(1)}, bf16[192,256]{1,0:T(8,128)(2,1)S(1)}, u32[]{:S(2)}, u32[]{:S(2)}) collective-permute-start(bf16[192,256]{1,0:T(8,128)(2,1)S(1)} %get-tuple-element.27), channel_id=1, source_target_pairs={{0,96},{16,112},{32,0},{48,16},{64,32},{80,48},{96,64},{112,80},{1... | collective-permute-start | bytes 294920 | tf_op jit(solution)/shard_map/ppermute | solution.py:25
  33.4 2.4 %collective-permute-start.5 = (bf16[192,256]{1,0:T(8,128)(2,1)S(1)}, bf16[192,256]{1,0:T(8,128)(2,1)S(1)}, u32[]{:S(2)}, u32[]{:S(2)}) collective-permute-start(bf16[192,256]{1,0:T(8,128)(2,1)S(1)} %get-tuple-element.27), channel_id=1, source_target_pairs={{0,112},{16,0},{32,16},{48,32},{64,48},{80,64},{96,80},{112,96},{1... | collective-permute-start | bytes 294920 | tf_op jit(solution)/shard_map/ppermute | solution.py:25
  36.4 3.1 %collective-permute-done.6 = bf16[192,256]{1,0:T(8,128)(2,1)S(1)} collective-permute-done((bf16[192,256]{1,0:T(8,128)(2,1)S(1)}, bf16[192,256]{1,0:T(8,128)(2,1)S(1)}, u32[]{:S(2)}, u32[]{:S(2)}) %collective-permute-start.6) | collective-permute-done | bytes 98336 | tf_op jit(solution)/shard_map/ppermute | solution.py:25
  39.5 2.1 %collective-permute-done.2 = bf16[192,256]{1,0:T(8,128)(2,1)S(1)} collective-permute-done((bf16[192,256]{1,0:T(8,128)(2,1)S(1)}, bf16[192,256]{1,0:T(8,128)(2,1)S(1)}, u32[]{:S(2)}, u32[]{:S(2)}) %collective-permute-start.2) | collective-permute-done | bytes 98336 | tf_op jit(solution)/shard_map/ppermute | solution.py:25
  41.6 2.6 %collective-permute-start.8 = (bf16[5,192,256]{2,1,0:T(8,128)(2,1)S(1)}, bf16[5,192,256]{2,1,0:T(8,128)(2,1)S(1)}, u32[]{:S(2)}, u32[]{:S(2)}) collective-permute-start(bf16[5,192,256]{2,1,0:T(8,128)(2,1)S(1)} %bitcast_dynamic-update-slice_fusion.1), channel_id=1, source_target_pairs={{0,128},{16,144},{32,160},{48,176},{64,192},{80,208},{96,224},{112... | collective-permute-start | bytes 1474568 | tf_op jit(solution)/shard_map/ppermute | solution.py:30
  44.3 2.2 %collective-permute-start.4 = (bf16[288,256]{1,0:T(8,128)(2,1)S(1)}, bf16[288,256]{1,0:T(8,128)(2,1)S(1)}, u32[]{:S(2)}, u32[]{:S(2)}) collective-permute-start(bf16[288,256]{1,0:T(8,128)(2,1)S(1)} %pad_maximum_fusion.2), channel_id=1, source_target_pairs={{0,32},{16,48},{32,64},{48,80},{64,96},{80,112},{96,0},{112,16},{1... | collective-permute-start | bytes 442376 | tf_op jit(solution)/shard_map/ppermute | solution.py:25
  46.6 2.0 %collective-permute-start.7 = (bf16[288,256]{1,0:T(8,128)(2,1)S(1)}, bf16[288,256]{1,0:T(8,128)(2,1)S(1)}, u32[]{:S(2)}, u32[]{:S(2)}) collective-permute-start(bf16[288,256]{1,0:T(8,128)(2,1)S(1)} %pad_maximum_fusion.3), channel_id=1, source_target_pairs={{0,96},{16,112},{32,0},{48,16},{64,32},{80,48},{96,64},{112,80},{1... | collective-permute-start | bytes 442376 | tf_op jit(solution)/shard_map/ppermute | solution.py:25
  48.8 4.5 %collective-permute-done.4 = bf16[288,256]{1,0:T(8,128)(2,1)S(1)} collective-permute-done((bf16[288,256]{1,0:T(8,128)(2,1)S(1)}, bf16[288,256]{1,0:T(8,128)(2,1)S(1)}, u32[]{:S(2)}, u32[]{:S(2)}) %collective-permute-start.4) | collective-permute-done | bytes 147488 | tf_op jit(solution)/shard_map/ppermute | solution.py:25
  53.4 3.7 %collective-permute-start.9 = (bf16[3,192,256]{2,1,0:T(8,128)(2,1)S(1)}, bf16[3,192,256]{2,1,0:T(8,128)(2,1)S(1)}, u32[]{:S(2)}, u32[]{:S(2)}) collective-permute-start(bf16[3,192,256]{2,1,0:T(8,128)(2,1)S(1)} %pad_maximum_fusion), channel_id=1, source_target_pairs={{0,128},{16,144},{32,160},{48,176},{64,192},{80,208},{96,224},{112... | collective-permute-start | bytes 884744 | tf_op jit(solution)/shard_map/ppermute | solution.py:30
  57.4 4.0 %collective-permute-done.9 = bf16[3,192,256]{2,1,0:T(8,128)(2,1)S(1)} collective-permute-done((bf16[3,192,256]{2,1,0:T(8,128)(2,1)S(1)}, bf16[3,192,256]{2,1,0:T(8,128)(2,1)S(1)}, u32[]{:S(2)}, u32[]{:S(2)}) %collective-permute-start.9) | collective-permute-done | bytes 294944 | tf_op jit(solution)/shard_map/ppermute | solution.py:30
  64.5 13.6 %all_to_all.16 = bf16[8,24,1024]{2,1,0:T(8,128)(2,1)S(1)} all-to-all(bf16[8,24,1024]{2,1,0:T(8,128)(2,1)S(1)} %bitcast.100), channel_id=1, replica_groups={{0,2,4,6,8,10,12,14},{1,3,5,7,9,11,13,15},{16,18,20,22,24,26,28,30},{17..., dimensions={0} | all-to-all | bytes 786432 | tf_op jit(solution)/shard_map/all_to_all | solution.py:16
  78.3 12.4 %all_to_all.17 = bf16[8,24,1024]{2,1,0:T(8,128)(2,1)S(1)} all-to-all(bf16[8,24,1024]{2,1,0:T(8,128)(2,1)S(1)} %broadcast_in_dim.80), channel_id=1, replica_groups={{0,2,4,6,8,10,12,14},{1,3,5,7,9,11,13,15},{16,18,20,22,24,26,28,30},{17..., dimensions={0} | all-to-all | bytes 786432 | tf_op jit(solution)/shard_map/all_to_all | solution.py:16
  90.7 1.8 %collective-permute-done.11 = bf16[192,1024]{1,0:T(8,128)(2,1)} collective-permute-done((bf16[192,1024]{1,0:T(8,128)(2,1)S(1)}, bf16[192,1024]{1,0:T(8,128)(2,1)}, u32[]{:S(2)}, u32[]{:S(2)}) %collective-permute-start.11) | collective-permute-done | bytes 393248 | tf_op jit(solution)/shard_map/ppermute | solution.py:8
  92.5 2.9 %fusion.8 = bf16[4,384,256]{2,1,0:T(8,128)(2,1)S(1)} fusion(bf16[8,256,1024]{2,1,0:T(8,128)(2,1)} %param.9, bf16[192,1024]{1,0:T(8,128)(2,1)} %collective-permute-done.11, bf16[192,1024]{1,0:T(8,128)(2,1)S(1)} %bitcast.113, pred[4]{0:T(512)(128)(4,1)S(1)} %get-tuple-element.44), kind=kOutput, calls=%fused_computation.8 | convolution fusion | flops 807665664 | bytes 3670020 | tf_op jit(solution)/shard_map/dot_general | solution.py:76
  95.5 1.3 collective-permute-start.12
  96.8 1.5 %collective-permute-start.13 = (bf16[5,192,256]{2,1,0:T(8,128)(2,1)S(1)}, bf16[5,192,256]{2,1,0:T(8,128)(2,1)S(1)}, u32[]{:S(2)}, u32[]{:S(2)}) collective-permute-start(bf16[5,192,256]{2,1,0:T(8,128)(2,1)S(1)} %get-tuple-element.36), channel_id=1, source_target_pairs={{128,0},{144,16},{160,32},{176,48},{192,64},{208,80},{224,96},{240... | collective-permute-start | bytes 1474568 | tf_op jit(solution)/shard_map/ppermute | solution.py:35
  98.3 2.0 %fusion.15 = bf16[4,384,256]{2,1,0:T(8,128)(2,1)S(1)} fusion(bf16[4,384,256]{2,1,0:T(8,128)(2,1)S(1)} %fusion.8, bf16[8,256,1024]{2,1,0:T(8,128)(2,1)S(1)} %copy-done.5, pred[4]{0:T(512)(128)(4,1)S(1)} %get-tuple-element.43, pred[]{:T(512)S(6)} %eq.42, bf16[192,1024]{1,0:T(8,128)(2,1)} %collective-permute-done.11, bf16[192,1024]{1,0:T(8,128)(2,1)S(1)} %bitcast.114), kind=kOutput, calls=%fused_computation.13 | convolution fusion | flops 808058880 | bytes 4456961 | tf_op jit(solution)/shard_map/dot_general | solution.py:76
  100.4 5.4 %convolution_convert_fusion = bf16[8,256,1024]{2,1,0:T(8,128)(2,1)} fusion(bf16[8,384,256]{2,1,0:T(8,128)(2,1)S(1)} %bitcast_select_fusion, bf16[192,1024]{1,0:T(8,128)(2,1)} %collective-permute-done.11, bf16[192,1024]{1,0:T(8,128)(2,1)S(1)} %bitcast.115), kind=kOutput, calls=%fused_computation | convolution fusion | flops 1614282752 | bytes 6553600 | tf_op jit(solution)/shard_map/dot_general | solution.py:184
  105.7 1.5 %collective-permute-done.12 = bf16[3,192,256]{2,1,0:T(8,128)(2,1)S(1)} collective-permute-done((bf16[3,192,256]{2,1,0:T(8,128)(2,1)S(1)}, bf16[3,192,256]{2,1,0:T(8,128)(2,1)S(1)}, u32[]{:S(2)}, u32[]{:S(2)}) %collective-permute-start.12) | collective-permute-done | bytes 294944 | tf_op jit(solution)/shard_map/ppermute | solution.py:35
  107.4 2.8 %collective-permute-start.16 = (bf16[288,256]{1,0:T(8,128)(2,1)S(1)}, bf16[288,256]{1,0:T(8,128)(2,1)S(1)}, u32[]{:S(2)}, u32[]{:S(2)}) collective-permute-start(bf16[288,256]{1,0:T(8,128)(2,1)S(1)} %pad_maximum_fusion.5), channel_id=1, source_target_pairs={{0,96},{16,112},{32,0},{48,16},{64,32},{80,48},{96,64},{112,80},{1... | collective-permute-start | bytes 442376 | tf_op jit(solution)/shard_map/ppermute | solution.py:25
  110.5 4.1 %collective-permute-done.16 = bf16[288,256]{1,0:T(8,128)(2,1)S(1)} collective-permute-done((bf16[288,256]{1,0:T(8,128)(2,1)S(1)}, bf16[288,256]{1,0:T(8,128)(2,1)S(1)}, u32[]{:S(2)}, u32[]{:S(2)}) %collective-permute-start.16) | collective-permute-done | bytes 147488 | tf_op jit(solution)/shard_map/ppermute | solution.py:25
  114.6 4.4 %collective-permute-done.14 = bf16[288,256]{1,0:T(8,128)(2,1)S(1)} collective-permute-done((bf16[288,256]{1,0:T(8,128)(2,1)S(1)}, bf16[288,256]{1,0:T(8,128)(2,1)S(1)}, u32[]{:S(2)}, u32[]{:S(2)}) %collective-permute-start.14) | collective-permute-done | bytes 147488 | tf_op jit(solution)/shard_map/ppermute | solution.py:25
  120.3 2.0 %collective-permute-start.19 = (bf16[192,256]{1,0:T(8,128)(2,1)S(1)}, bf16[192,256]{1,0:T(8,128)(2,1)S(1)}, u32[]{:S(2)}, u32[]{:S(2)}) collective-permute-start(bf16[192,256]{1,0:T(8,128)(2,1)S(1)} %get-tuple-element.29), channel_id=1, source_target_pairs={{0,96},{16,112},{32,0},{48,16},{64,32},{80,48},{96,64},{112,80},{1... | collective-permute-start | bytes 294920 | tf_op jit(solution)/shard_map/ppermute | solution.py:25
  123.2 3.4 %collective-permute-start.17 = (bf16[192,256]{1,0:T(8,128)(2,1)S(1)}, bf16[192,256]{1,0:T(8,128)(2,1)S(1)}, u32[]{:S(2)}, u32[]{:S(2)}) collective-permute-start(bf16[192,256]{1,0:T(8,128)(2,1)S(1)} %get-tuple-element.31), channel_id=1, source_target_pairs={{0,112},{16,0},{32,16},{48,32},{64,48},{80,64},{96,80},{112,96},{1... | collective-permute-start | bytes 294920 | tf_op jit(solution)/shard_map/ppermute | solution.py:25
  127.1 3.5 %collective-permute-done.18 = bf16[192,256]{1,0:T(8,128)(2,1)S(1)} collective-permute-done((bf16[192,256]{1,0:T(8,128)(2,1)S(1)}, bf16[192,256]{1,0:T(8,128)(2,1)S(1)}, u32[]{:S(2)}, u32[]{:S(2)}) %collective-permute-start.18) | collective-permute-done | bytes 98336 | tf_op jit(solution)/shard_map/ppermute | solution.py:25
  131.1 4.3 %collective-permute-done.20 = bf16[192,256]{1,0:T(8,128)(2,1)S(1)} collective-permute-done((bf16[192,256]{1,0:T(8,128)(2,1)S(1)}, bf16[192,256]{1,0:T(8,128)(2,1)S(1)}, u32[]{:S(2)}, u32[]{:S(2)}) %collective-permute-start.20) | collective-permute-done | bytes 98336 | tf_op jit(solution)/shard_map/ppermute | solution.py:8
  135.5 1.4 %fusion.20 = f32[1024,256]{1,0:T(8,128)} fusion(bf16[192,1024]{1,0:T(8,128)(2,1)S(1)} %copy-done.2, bf16[192,1024]{1,0:T(8,128)(2,1)S(1)} %bitcast.99, bf16[192,256]{1,0:T(8,128)(2,1)S(1)} %get-tuple-element.40, bf16[192,256]{1,0:T(8,128)(2,1)S(1)} %get-tuple-element.39), kind=kOutput, calls=%fused_computation.16 | convolution fusion | flops 203292672 | bytes 2031616 | tf_op jit(solution)/shard_map/dot_general | solution.py:196
  (90 shorter events, 10.3 us)
Async XLA Ops:
  0.6 17.2 %copy-start = (bf16[1024,256]{1,0:T(8,128)(2,1)S(1)}, bf16[1024,256]{1,0:T(8,128)(2,1)}, u32[]{:S(2)}) copy-start(bf16[1024,256]{1,0:T(8,128)(2,1)} %param.7) | copy-start | bytes 1572868
  17.8 1.7 %collective-permute-start = (bf16[192,1024]{1,0:T(8,128)(2,1)S(1)}, bf16[192,1024]{1,0:T(8,128)(2,1)S(1)}, u32[]{:S(2)}, u32[]{:S(2)}) collective-permute-start(bf16[192,1024]{1,0:T(8,128)(2,1)S(1)} %bitcast.97), channel_id=1, source_target_pairs={{0,1},{1,0},{2,3},{3,2},{4,5},{5,4},{6,7},{7,6},{8,9},{9,8},{10,11... | collective-permute-start | bytes 1179656 | tf_op jit(solution)/shard_map/ppermute | solution.py:8
  19.5 22.1 %copy-start.1 = (bf16[192,1024]{1,0:T(8,128)(2,1)}, bf16[192,1024]{1,0:T(8,128)(2,1)S(1)}, u32[]{:S(2)}) copy-start(bf16[192,1024]{1,0:T(8,128)(2,1)S(1)} %collective-permute-done) | copy-start | bytes 1179652
  19.8 7.2 %collective-permute-start.1 = (f32[192,256]{1,0:T(8,128)S(1)}, f32[192,256]{1,0:T(8,128)S(1)}, u32[]{:S(2)}, u32[]{:S(2)}) collective-permute-start(f32[192,256]{1,0:T(8,128)S(1)} %get-tuple-element.45), channel_id=1, source_target_pairs={{0,16},{16,0},{32,48},{48,32},{64,80},{80,64},{96,112},{112,96},{1... | collective-permute-start | bytes 589832 | tf_op jit(solution)/shard_map/ppermute | solution.py:8
  27.1 9.3 %collective-permute-start.3 = (bf16[192,256]{1,0:T(8,128)(2,1)S(1)}, bf16[192,256]{1,0:T(8,128)(2,1)S(1)}, u32[]{:S(2)}, u32[]{:S(2)}) collective-permute-start(bf16[192,256]{1,0:T(8,128)(2,1)S(1)} %get-tuple-element.27), channel_id=1, source_target_pairs={{0,32},{16,48},{32,64},{48,80},{64,96},{80,112},{96,0},{112,16},{1... | collective-permute-start | bytes 294920 | tf_op jit(solution)/shard_map/ppermute | solution.py:25
  30.4 9.1 %collective-permute-start.6 = (bf16[192,256]{1,0:T(8,128)(2,1)S(1)}, bf16[192,256]{1,0:T(8,128)(2,1)S(1)}, u32[]{:S(2)}, u32[]{:S(2)}) collective-permute-start(bf16[192,256]{1,0:T(8,128)(2,1)S(1)} %get-tuple-element.27), channel_id=1, source_target_pairs={{0,96},{16,112},{32,0},{48,16},{64,32},{80,48},{96,64},{112,80},{1... | collective-permute-start | bytes 294920 | tf_op jit(solution)/shard_map/ppermute | solution.py:25
  33.4 8.2 %collective-permute-start.5 = (bf16[192,256]{1,0:T(8,128)(2,1)S(1)}, bf16[192,256]{1,0:T(8,128)(2,1)S(1)}, u32[]{:S(2)}, u32[]{:S(2)}) collective-permute-start(bf16[192,256]{1,0:T(8,128)(2,1)S(1)} %get-tuple-element.27), channel_id=1, source_target_pairs={{0,112},{16,0},{32,16},{48,32},{64,48},{80,64},{96,80},{112,96},{1... | collective-permute-start | bytes 294920 | tf_op jit(solution)/shard_map/ppermute | solution.py:25
  35.8 5.8 %collective-permute-start.2 = (bf16[192,256]{1,0:T(8,128)(2,1)S(1)}, bf16[192,256]{1,0:T(8,128)(2,1)S(1)}, u32[]{:S(2)}, u32[]{:S(2)}) collective-permute-start(bf16[192,256]{1,0:T(8,128)(2,1)S(1)} %get-tuple-element.27), channel_id=1, source_target_pairs={{0,16},{16,32},{32,48},{48,64},{64,80},{80,96},{96,112},{112,0},{1... | collective-permute-start | bytes 294920 | tf_op jit(solution)/shard_map/ppermute | solution.py:25
  41.6 11.7 %collective-permute-start.8 = (bf16[5,192,256]{2,1,0:T(8,128)(2,1)S(1)}, bf16[5,192,256]{2,1,0:T(8,128)(2,1)S(1)}, u32[]{:S(2)}, u32[]{:S(2)}) collective-permute-start(bf16[5,192,256]{2,1,0:T(8,128)(2,1)S(1)} %bitcast_dynamic-update-slice_fusion.1), channel_id=1, source_target_pairs={{0,128},{16,144},{32,160},{48,176},{64,192},{80,208},{96,224},{112... | collective-permute-start | bytes 1474568 | tf_op jit(solution)/shard_map/ppermute | solution.py:30
  44.3 9.0 %collective-permute-start.4 = (bf16[288,256]{1,0:T(8,128)(2,1)S(1)}, bf16[288,256]{1,0:T(8,128)(2,1)S(1)}, u32[]{:S(2)}, u32[]{:S(2)}) collective-permute-start(bf16[288,256]{1,0:T(8,128)(2,1)S(1)} %pad_maximum_fusion.2), channel_id=1, source_target_pairs={{0,32},{16,48},{32,64},{48,80},{64,96},{80,112},{96,0},{112,16},{1... | collective-permute-start | bytes 442376 | tf_op jit(solution)/shard_map/ppermute | solution.py:25
  46.6 6.7 %collective-permute-start.7 = (bf16[288,256]{1,0:T(8,128)(2,1)S(1)}, bf16[288,256]{1,0:T(8,128)(2,1)S(1)}, u32[]{:S(2)}, u32[]{:S(2)}) collective-permute-start(bf16[288,256]{1,0:T(8,128)(2,1)S(1)} %pad_maximum_fusion.3), channel_id=1, source_target_pairs={{0,96},{16,112},{32,0},{48,16},{64,32},{80,48},{96,64},{112,80},{1... | collective-permute-start | bytes 442376 | tf_op jit(solution)/shard_map/ppermute | solution.py:25
  53.4 8.0 %collective-permute-start.9 = (bf16[3,192,256]{2,1,0:T(8,128)(2,1)S(1)}, bf16[3,192,256]{2,1,0:T(8,128)(2,1)S(1)}, u32[]{:S(2)}, u32[]{:S(2)}) collective-permute-start(bf16[3,192,256]{2,1,0:T(8,128)(2,1)S(1)} %pad_maximum_fusion), channel_id=1, source_target_pairs={{0,128},{16,144},{32,160},{48,176},{64,192},{80,208},{96,224},{112... | collective-permute-start | bytes 884744 | tf_op jit(solution)/shard_map/ppermute | solution.py:30
  57.3 4.3 %copy-start.4 = (bf16[8,256,1024]{2,1,0:T(8,128)(2,1)S(1)}, bf16[8,256,1024]{2,1,0:T(8,128)(2,1)}, u32[]{:S(2)}) copy-start(bf16[8,256,1024]{2,1,0:T(8,128)(2,1)} %param.9) | copy-start | bytes 12582916
  62.6 1.8 %collective-permute-start.10 = (bf16[192,1024]{1,0:T(8,128)(2,1)S(1)}, bf16[192,1024]{1,0:T(8,128)(2,1)S(1)}, u32[]{:S(2)}, u32[]{:S(2)}) collective-permute-start(bf16[192,1024]{1,0:T(8,128)(2,1)S(1)} %fusion.14), channel_id=1, source_target_pairs={{0,1},{1,0},{2,3},{3,2},{4,5},{5,4},{6,7},{7,6},{8,9},{9,8},{10,11... | collective-permute-start | bytes 1179656 | tf_op jit(solution)/shard_map/ppermute | solution.py:8
  63.7 14.5 %copy-start.3 = (bf16[24,1024]{1,0:T(8,128)(2,1)S(1)}, bf16[24,1024]{1,0:T(8,128)(2,1)}, u32[]{:S(2)}) copy-start(bf16[24,1024]{1,0:T(8,128)(2,1)} %param.6) | copy-start | bytes 147460
  90.6 1.9 %collective-permute-start.11 = (bf16[192,1024]{1,0:T(8,128)(2,1)S(1)}, bf16[192,1024]{1,0:T(8,128)(2,1)}, u32[]{:S(2)}, u32[]{:S(2)}) collective-permute-start(bf16[192,1024]{1,0:T(8,128)(2,1)S(1)} %bitcast.112), channel_id=1, source_target_pairs={{0,1},{1,0},{2,3},{3,2},{4,5},{5,4},{6,7},{7,6},{8,9},{9,8},{10,11... | collective-permute-start | bytes 1179656 | tf_op jit(solution)/shard_map/ppermute | solution.py:8
  92.5 5.8 %copy-start.5 = (bf16[8,256,1024]{2,1,0:T(8,128)(2,1)S(1)}, bf16[8,256,1024]{2,1,0:T(8,128)(2,1)}, u32[]{:S(2)}) copy-start(bf16[8,256,1024]{2,1,0:T(8,128)(2,1)} %param.9) | copy-start | bytes 12582916
  95.5 11.7 %collective-permute-start.12 = (bf16[3,192,256]{2,1,0:T(8,128)(2,1)S(1)}, bf16[3,192,256]{2,1,0:T(8,128)(2,1)S(1)}, u32[]{:S(2)}, u32[]{:S(2)}) collective-permute-start(bf16[3,192,256]{2,1,0:T(8,128)(2,1)S(1)} %pad_maximum_fusion.1), channel_id=1, source_target_pairs={{128,0},{144,16},{160,32},{176,48},{192,64},{208,80},{224,96},{240... | collective-permute-start | bytes 884744 | tf_op jit(solution)/shard_map/ppermute | solution.py:35
  96.8 22.2 %collective-permute-start.13 = (bf16[5,192,256]{2,1,0:T(8,128)(2,1)S(1)}, bf16[5,192,256]{2,1,0:T(8,128)(2,1)S(1)}, u32[]{:S(2)}, u32[]{:S(2)}) collective-permute-start(bf16[5,192,256]{2,1,0:T(8,128)(2,1)S(1)} %get-tuple-element.36), channel_id=1, source_target_pairs={{128,0},{144,16},{160,32},{176,48},{192,64},{208,80},{224,96},{240... | collective-permute-start | bytes 1474568 | tf_op jit(solution)/shard_map/ppermute | solution.py:35
  107.4 7.2 %collective-permute-start.16 = (bf16[288,256]{1,0:T(8,128)(2,1)S(1)}, bf16[288,256]{1,0:T(8,128)(2,1)S(1)}, u32[]{:S(2)}, u32[]{:S(2)}) collective-permute-start(bf16[288,256]{1,0:T(8,128)(2,1)S(1)} %pad_maximum_fusion.5), channel_id=1, source_target_pairs={{0,96},{16,112},{32,0},{48,16},{64,32},{80,48},{96,64},{112,80},{1... | collective-permute-start | bytes 442376 | tf_op jit(solution)/shard_map/ppermute | solution.py:25
  110.2 25.3 %copy-start.2 = (bf16[192,1024]{1,0:T(8,128)(2,1)S(1)}, bf16[192,1024]{1,0:T(8,128)(2,1)}, u32[]{:S(2)}) copy-start(bf16[192,1024]{1,0:T(8,128)(2,1)} %copy-done.1) | copy-start | bytes 1179652
  110.2 8.8 %collective-permute-start.14 = (bf16[288,256]{1,0:T(8,128)(2,1)S(1)}, bf16[288,256]{1,0:T(8,128)(2,1)S(1)}, u32[]{:S(2)}, u32[]{:S(2)}) collective-permute-start(bf16[288,256]{1,0:T(8,128)(2,1)S(1)} %pad_maximum_fusion.4), channel_id=1, source_target_pairs={{0,32},{16,48},{32,64},{48,80},{64,96},{80,112},{96,0},{112,16},{1... | collective-permute-start | bytes 442376 | tf_op jit(solution)/shard_map/ppermute | solution.py:25
  119.2 7.9 %collective-permute-start.15 = (bf16[192,256]{1,0:T(8,128)(2,1)S(1)}, bf16[192,256]{1,0:T(8,128)(2,1)S(1)}, u32[]{:S(2)}, u32[]{:S(2)}) collective-permute-start(bf16[192,256]{1,0:T(8,128)(2,1)S(1)} %get-tuple-element.28), channel_id=1, source_target_pairs={{0,16},{16,32},{32,48},{48,64},{64,80},{80,96},{96,112},{112,0},{1... | collective-permute-start | bytes 294920 | tf_op jit(solution)/shard_map/ppermute | solution.py:25
  120.3 6.8 %collective-permute-start.19 = (bf16[192,256]{1,0:T(8,128)(2,1)S(1)}, bf16[192,256]{1,0:T(8,128)(2,1)S(1)}, u32[]{:S(2)}, u32[]{:S(2)}) collective-permute-start(bf16[192,256]{1,0:T(8,128)(2,1)S(1)} %get-tuple-element.29), channel_id=1, source_target_pairs={{0,96},{16,112},{32,0},{48,16},{64,32},{80,48},{96,64},{112,80},{1... | collective-permute-start | bytes 294920 | tf_op jit(solution)/shard_map/ppermute | solution.py:25
  122.2 8.4 %collective-permute-start.18 = (bf16[192,256]{1,0:T(8,128)(2,1)S(1)}, bf16[192,256]{1,0:T(8,128)(2,1)S(1)}, u32[]{:S(2)}, u32[]{:S(2)}) collective-permute-start(bf16[192,256]{1,0:T(8,128)(2,1)S(1)} %get-tuple-element.30), channel_id=1, source_target_pairs={{0,32},{16,48},{32,64},{48,80},{64,96},{80,112},{96,0},{112,16},{1... | collective-permute-start | bytes 294920 | tf_op jit(solution)/shard_map/ppermute | solution.py:25
  123.2 7.4 %collective-permute-start.17 = (bf16[192,256]{1,0:T(8,128)(2,1)S(1)}, bf16[192,256]{1,0:T(8,128)(2,1)S(1)}, u32[]{:S(2)}, u32[]{:S(2)}) collective-permute-start(bf16[192,256]{1,0:T(8,128)(2,1)S(1)} %get-tuple-element.31), channel_id=1, source_target_pairs={{0,112},{16,0},{32,16},{48,32},{64,48},{80,64},{96,80},{112,96},{1... | collective-permute-start | bytes 294920 | tf_op jit(solution)/shard_map/ppermute | solution.py:25
  130.7 4.7 %collective-permute-start.20 = (bf16[192,256]{1,0:T(8,128)(2,1)S(1)}, bf16[192,256]{1,0:T(8,128)(2,1)S(1)}, u32[]{:S(2)}, u32[]{:S(2)}) collective-permute-start(bf16[192,256]{1,0:T(8,128)(2,1)S(1)} %fusion.37), channel_id=1, source_target_pairs={{0,16},{16,0},{32,48},{48,32},{64,80},{80,64},{96,112},{112,96},{1... | collective-permute-start | bytes 294920 | tf_op jit(solution)/shard_map/ppermute | solution.py:8
